TPU v7x, 32 devices: a whole 2x2x4 slice. The times are simulated.
32 devices in a mesh: dp: 8 (over y, x, core), tensor: 4 (over z).
Axes of the slice: x: 2, y: 2, z: 4, core: 2. Of those that a mesh axis runs over, the one named last changes fastest.
Arguments:
- x_in: bfloat16 [16384, 640], P(('dp', 'tensor')), may hold values from -6 to 6
- cotangent: bfloat16 [16384, 640], P(('dp', 'tensor')), may hold values from -6 to 6
- lengths: int32 [8, 8], P('dp'), may hold values from 0 to 1024, as said below
- bucket_ids: int32 [8], P('dp'), may hold values from 0 to 2, as said below
- bucket_weights: float32 [3], replicated, may hold values from 0.5 to 2
- ln1_gain: float32 [640], replicated, may hold values from 0.5 to 1.5
- ln1_bias: float32 [640], replicated, may hold values from -1.5 to 1.5
- w_qkv: bfloat16 [3, 640, 640], P(None, None, 'tensor'), may hold values from -0.25 to 0.25
- qv_bias: float32 [2, 640], P(None, 'tensor'), may hold values from -1.5 to 1.5
- w_out: bfloat16 [640, 640], P('tensor'), may hold values from -2.5 to 2.5
- b_out: float32 [640], replicated, may hold values from -1.5 to 1.5
- ln2_gain: float32 [640], replicated, may hold values from 0.5 to 1.5
- ln2_bias: float32 [640], replicated, may hold values from -1.5 to 1.5
- w_up: bfloat16 [640, 5120], P(None, 'tensor'), may hold values from -0.25 to 0.25
- b_up: float32 [5120], P('tensor'), may hold values from -1.5 to 1.5
- w_down: bfloat16 [5120, 640], P('tensor'), may hold values from -0.078125 to 0.078125
- b_down: float32 [640], replicated, may hold values from -1.5 to 1.5
Outputs:
- layer_out: bfloat16 [16384, 640], P(('dp', 'tensor'))
- x_grad: float32 [16384, 640], P(('dp', 'tensor'))
- ln1_gain_grad: float32 [640], replicated
- ln1_bias_grad: float32 [640], replicated
- w_qkv_grad: float32 [3, 640, 640], P(None, None, 'tensor')
- qv_bias_grad: float32 [2, 640], P(None, 'tensor')
- w_out_grad: float32 [640, 640], P('tensor')
- b_out_grad: float32 [640], replicated
- ln2_gain_grad: float32 [640], replicated
- ln2_bias_grad: float32 [640], replicated
- w_up_grad: float32 [640, 5120], P(None, 'tensor')
- b_up_grad: float32 [5120], P('tensor')
- w_down_grad: float32 [5120, 640], P('tensor')
- b_down_grad: float32 [640], replicated
Inputs may be any that keep to these rules, and one draw needn't show every extreme that they name: `bucket_ids`: every bucket 0, 1 and 2 is held by some index of dp. `lengths`: with span s = 256, 512, 1024 for bucket 0, 1, 2 of index i, entries j < 2048 / s of row i lie between s / 4 and s, entry 0 equals s; later entries are 0.
All inputs are finite; a program needn't handle non-finite values.
Results may differ from a plain program's by a relative error of at most 0.02.
Values may be sent and summed in bfloat16 or wider, within the bound.
A program may use at most 192 MiB of HBM per device.

v0:
```python
import jax
import jax.numpy as jnp
from jax import lax
from jax.sharding import PartitionSpec as P

HD = 32
BUCKET = 256


EPSILON = 1e-05


def norm_parts(values, gain, shift):
    centre = values - jnp.mean(values, axis=-1, keepdims=True)
    scale_inv = lax.rsqrt(jnp.mean(centre * centre, axis=-1, keepdims=True) + EPSILON)
    unit = centre * scale_inv
    return (unit * gain + shift, unit, scale_inv)


def norm_back(grad, unit, scale_inv, gain):
    scaled = grad * gain
    centred = (
        scaled
        - jnp.mean(scaled, axis=-1, keepdims=True)
        - unit * jnp.mean(scaled * unit, axis=-1, keepdims=True)
    )
    return (scale_inv * centred, jnp.sum(grad * unit, axis=0), jnp.sum(grad, axis=0))


def gelu_exact(values):
    return jax.nn.gelu(values, approximate=False)


def local(
    x_in,
    cotangent,
    lengths,
    bucket_ids,
    bucket_weights,
    ln1_gain,
    ln1_bias,
    w_qkv,
    qv_bias,
    w_out,
    b_out,
    ln2_gain,
    ln2_bias,
    w_up,
    b_up,
    w_down,
    b_down,
):
    f32 = jnp.float32
    bf16 = jnp.bfloat16
    parts = lax.axis_size("tensor")
    share = x_in.shape[0]
    rows = share * parts
    window = 4 * BUCKET
    local_w = w_qkv.shape[2]
    heads_local = local_w // HD
    factor = HD ** (-0.5)
    n_windows = rows // window
    bucket_now = bucket_ids[0]
    span = jnp.where(
        bucket_now == 0, BUCKET, jnp.where(bucket_now == 1, 2 * BUCKET, 4 * BUCKET)
    ).astype(jnp.int32)
    row_pos = jnp.arange(rows, dtype=jnp.int32)
    item_ids = row_pos // span
    slot_hit = item_ids[:, None] == jnp.arange(lengths.shape[1], dtype=jnp.int32)[None, :]
    row_len = jnp.sum(jnp.where(slot_hit, lengths[0][None, :], 0), axis=1)
    key_live = row_pos % span < row_len
    mine = lax.dynamic_slice_in_dim(key_live, lax.axis_index("tensor") * share, share, 0)
    bucket_hit = bucket_now == jnp.arange(3, dtype=jnp.int32)
    weight_now = jnp.sum(jnp.where(bucket_hit, bucket_weights, 0.0))
    row_weight = jnp.where(mine, weight_now, 0.0)
    x_float = x_in.astype(f32)
    normed, unit_one, inv_one = norm_parts(x_float, ln1_gain, ln1_bias)
    normed = normed.astype(bf16)
    normed_all = lax.all_gather(normed, "tensor", axis=0, tiled=True)
    bias_three = jnp.stack([qv_bias[0], jnp.zeros_like(qv_bias[0]), qv_bias[1]])
    projected = (
        jnp.einsum("rd,cde->rce", normed_all, w_qkv, preferred_element_type=f32) + bias_three[None]
    ).astype(bf16)
    queries = projected[:, 0].reshape(rows, heads_local, HD)
    key_rows = projected[:, 1].reshape(rows, heads_local, HD)
    value_rows = projected[:, 2].reshape(rows, heads_local, HD)

    def window_scores(start):
        query_b = lax.dynamic_slice_in_dim(queries, start, window, 0)
        key_b = lax.dynamic_slice_in_dim(key_rows, start, window, 0)
        value_b = lax.dynamic_slice_in_dim(value_rows, start, window, 0)
        item_b = lax.dynamic_slice_in_dim(item_ids, start, window, 0)
        live_b = lax.dynamic_slice_in_dim(key_live, start, window, 0)
        scores = jnp.einsum("qhd,khd->hqk", query_b, key_b, preferred_element_type=f32) * factor
        allowed = (item_b[:, None] == item_b[None, :]) & live_b[None, :]
        return (jnp.where(allowed[None], scores, -1e30), query_b, key_b, value_b)

    def forward_window(index):
        masked, query_b, key_b, value_b = window_scores(index * window)
        top = jnp.max(masked, axis=-1, keepdims=True)
        expo = jnp.exp(masked - top)
        total = jnp.sum(expo, axis=-1, keepdims=True)
        probs = expo / total
        mixed_b = jnp.einsum(
            "hqk,khd->qhd", probs.astype(bf16), value_b, preferred_element_type=f32
        ).astype(bf16)
        return (mixed_b, (top + jnp.log(total))[..., 0])

    window_ids = jnp.arange(n_windows, dtype=jnp.int32)
    mixed, log_norm = lax.map(forward_window, window_ids)
    mixed = mixed.reshape(rows, local_w)
    branch = lax.psum_scatter(
        jnp.dot(mixed, w_out, preferred_element_type=f32).astype(jnp.bfloat16),
        "tensor",
        scatter_dimension=0,
        tiled=True,
    ).astype(jnp.float32)
    middle = x_float + (branch + b_out)
    normed2, unit_two, inv_two = norm_parts(middle, ln2_gain, ln2_bias)
    normed2 = normed2.astype(bf16)
    normed2_all = lax.all_gather(normed2, "tensor", axis=0, tiled=True)
    hidden = jnp.dot(normed2_all, w_up, preferred_element_type=f32) + b_up
    active = gelu_exact(hidden).astype(bf16)
    ffn_out = lax.psum_scatter(
        jnp.dot(active, w_down, preferred_element_type=f32).astype(jnp.bfloat16),
        "tensor",
        scatter_dimension=0,
        tiled=True,
    ).astype(jnp.float32)
    result = middle + (ffn_out + b_down)
    layer_out = result.astype(bf16)
    out_grad = cotangent.astype(f32) * row_weight[:, None]
    out_low = out_grad.astype(bf16)
    grad_b_down = jnp.sum(out_low.astype(f32), axis=0)
    grads_all = lax.all_gather(out_low, "tensor", axis=0, tiled=True)
    grad_down = jnp.einsum("rf,rd->fd", active, grads_all, preferred_element_type=f32)
    act_grad = jnp.einsum("rd,fd->rf", grads_all, w_down, preferred_element_type=f32)
    hidden_grad = jax.vjp(gelu_exact, hidden)[1](act_grad)[0].astype(bf16)
    grad_up = jnp.einsum("rd,rf->df", normed2_all, hidden_grad, preferred_element_type=f32)
    grad_up_bias = jnp.sum(hidden_grad.astype(f32), axis=0)
    normed2_grad = lax.psum_scatter(
        jnp.einsum("rf,df->rd", hidden_grad, w_up, preferred_element_type=f32).astype(jnp.bfloat16),
        "tensor",
        scatter_dimension=0,
        tiled=True,
    ).astype(jnp.float32)
    middle_part, grad_g_two, grad_s_two = norm_back(normed2_grad, unit_two, inv_two, ln2_gain)
    middle_grad = out_grad + middle_part
    branch_low = middle_grad.astype(bf16)
    grad_b_out = jnp.sum(branch_low.astype(f32), axis=0)
    branch_all = lax.all_gather(branch_low, "tensor", axis=0, tiled=True)
    grad_w_out = jnp.einsum("rk,rd->kd", mixed, branch_all, preferred_element_type=f32)
    mixed_grad = jnp.einsum("rd,kd->rk", branch_all, w_out, preferred_element_type=f32).astype(bf16)
    mixed_grad = mixed_grad.reshape(rows, heads_local, HD)

    def backward_window(packed):
        index, norm_b = packed
        start = index * window
        masked, query_b, key_b, value_b = window_scores(start)
        grad_b = lax.dynamic_slice_in_dim(mixed_grad, start, window, 0)
        probs = jnp.exp(masked - norm_b[..., None])
        value_grad = jnp.einsum(
            "hqk,qhd->khd", probs.astype(bf16), grad_b, preferred_element_type=f32
        )
        prob_grad = jnp.einsum("qhd,khd->hqk", grad_b, value_b, preferred_element_type=f32)
        score_grad = (
            probs * (prob_grad - jnp.sum(probs * prob_grad, axis=-1, keepdims=True))
        ).astype(bf16)
        query_grad = (
            jnp.einsum("hqk,khd->qhd", score_grad, key_b, preferred_element_type=f32) * factor
        )
        key_grad = (
            jnp.einsum("hqk,qhd->khd", score_grad, query_b, preferred_element_type=f32) * factor
        )
        return jnp.stack([query_grad, key_grad, value_grad], axis=1).astype(bf16)

    proj_grad = lax.map(backward_window, (window_ids, log_norm)).reshape(rows, 3, local_w)
    grad_qkv = jnp.einsum("rd,rce->cde", normed_all, proj_grad, preferred_element_type=f32)
    grad_qv_bias = jnp.sum(proj_grad[:, ::2].astype(f32), axis=0)
    normed_grad = lax.psum_scatter(
        jnp.einsum("rce,cde->rd", proj_grad, w_qkv, preferred_element_type=f32).astype(
            jnp.bfloat16
        ),
        "tensor",
        scatter_dimension=0,
        tiled=True,
    ).astype(jnp.float32)
    input_part, grad_g_one, grad_s_one = norm_back(normed_grad, unit_one, inv_one, ln1_gain)
    x_grad = middle_grad + input_part
    (
        grad_qkv,
        grad_qv_bias,
        grad_w_out,
        grad_up,
        grad_up_bias,
        grad_down,
        grad_g_one,
        grad_s_one,
        grad_b_out,
        grad_g_two,
        grad_s_two,
        grad_b_down,
    ) = lax.psum(
        (
            grad_qkv,
            grad_qv_bias,
            grad_w_out,
            grad_up,
            grad_up_bias,
            grad_down,
            grad_g_one,
            grad_s_one,
            grad_b_out,
            grad_g_two,
            grad_s_two,
            grad_b_down,
        ),
        "dp",
    )
    grad_g_one, grad_s_one, grad_b_out, grad_g_two, grad_s_two, grad_b_down = lax.psum(
        (grad_g_one, grad_s_one, grad_b_out, grad_g_two, grad_s_two, grad_b_down), "tensor"
    )
    return (
        layer_out,
        x_grad,
        grad_g_one,
        grad_s_one,
        grad_qkv,
        grad_qv_bias,
        grad_w_out,
        grad_b_out,
        grad_g_two,
        grad_s_two,
        grad_up,
        grad_up_bias,
        grad_down,
        grad_b_down,
    )


def solution(mesh):
    return jax.shard_map(
        local,
        mesh=mesh,
        in_specs=(
            P(("dp", "tensor"), None),
            P(("dp", "tensor"), None),
            P("dp", None),
            P("dp"),
            P(),
            P(),
            P(),
            P(None, None, "tensor"),
            P(None, "tensor"),
            P("tensor", None),
            P(),
            P(),
            P(),
            P(None, "tensor"),
            P("tensor"),
            P("tensor", None),
            P(),
        ),
        out_specs=(
            P(("dp", "tensor"), None),
            P(("dp", "tensor"), None),
            P(),
            P(),
            P(None, None, "tensor"),
            P(None, "tensor"),
            P("tensor", None),
            P(),
            P(),
            P(),
            P(None, "tensor"),
            P("tensor"),
            P("tensor", None),
            P(),
        ),
        check_vma=False,
    )
```

profile of v0, /device:TPU:0, one launch (start us, length us, event | category | flops | bytes accessed | tf_op | source)
XLA Modules:
  0.0 813.2 jit_solution(5926795648594748620)
XLA Ops:
  15.0 55.0 %all-gather.5.cloned.1.call-done = bf16[2048,640]{1,0:T(8,128)(2,1)} async-done(((bf16[512,640]{1,0:T(8,128)(2,1)}), bf16[2048,640]{1,0:T(8,128)(2,1)}) %all-gather.5.cloned.1.call-update) | async-done | bytes 2621456 | tf_op jit(solution)/shard_map/all_gather | solution.py:79
  75.1 39.3 %while.22 = (s32[]{:T(128)}, bf16[2,1024,5,32]{1,3,2,0:T(8,128)(2,1)}, f32[2,5,1024]{2,1,0:T(8,128)S(1)}, s32[2]{0:T(128)S(1)}, bf16[2048,5,32]{0,2,1:T(8,128)(2...) while((s32[]{:T(128)}, ...), condition=%wide.region_6.7_spmd, body=%wide.region_3.6_spmd.sunk | while | flops 736259072 | bytes 68636880 | solution.py:110
  119.9 51.0 %reduce-scatter.5.cloned.1.call-done = bf16[512,640]{1,0:T(8,128)(2,1)} async-done(((bf16[2048,640]{1,0:T(8,128)(2,1)}), bf16[512,640]{1,0:T(8,128)(2,1)}) %reduce-scatter.5.cloned.1.call-update) | async-done | bytes 655376 | tf_op jit(solution)/shard_map/reduce_scatter | solution.py:112
  180.5 50.2 %all-gather.7.cloned.1.call-done = bf16[2048,640]{1,0:T(8,128)(2,1)} async-done(((bf16[512,640]{1,0:T(8,128)(2,1)}), bf16[2048,640]{1,0:T(8,128)(2,1)}) %all-gather.7.cloned.1.call-update) | async-done | bytes 2621456 | tf_op jit(solution)/shard_map/all_gather | solution.py:121
  230.7 28.8 %multiply_convert_fusion.1 = (bf16[2048,1280]{1,0:T(8,128)(2,1)}, f32[2048,1280]{1,0:T(8,128)}, f32[2048,1280]{1,0:T(8,128)}) fusion(f32[1280]{0:T(1024)S(1)} %copy-done.32, bf16[2048,640]{1,0:T(8,128)(2,1)} %all-gather.7.cloned.1.call-done, bf16[640,1280]{1,0:T(8,128)(2,1)S(1)} %copy-done), kind=kOutput, calls=%fused_computation.56 | convolution fusion | flops 3528458240 | bytes 30479360 | tf_op jit(solution)/shard_map/dot_general | solution.py:122
  259.5 26.8 %all-gather.9.cloned.1.call-done = bf16[2048,640]{1,0:T(8,128)(2,1)} async-done(((bf16[512,640]{1,0:T(8,128)(2,1)}), bf16[2048,640]{1,0:T(8,128)(2,1)}) %all-gather.9.cloned.1.call-update) | async-done | bytes 2621456 | tf_op jit(solution)/shard_map/all_gather | solution.py:135
  286.3 14.1 %convert_reduce_fusion = (f32[1280]{0:T(1024)}, bf16[2048,1280]{1,0:T(8,128)(2,1)S(1)}) fusion(f32[2048,1280]{1,0:T(8,128)} %get-tuple-element.187, bf16[2048,640]{1,0:T(8,128)(2,1)} %all-gather.9.cloned.1.call-done, bf16[1280,640]{1,0:T(8,128)(2,1)} %param.36, f32[2048,1280]{1,0:T(8,128)} %get-tuple-element.198, f32[1280]{0:T(1024)S(1)} %copy-done.32), kind=kOutput, calls=%fused_computation.54 | convolution fusion | flops 3400006400 | bytes 30484480 | tf_op jit(solution)/shard_map/rd,fd->rf/dot_general | solution.py:137
  308.3 8.8 %convolution_convert_fusion.1 = bf16[2048,640]{1,0:T(8,128)(2,1)} fusion(bf16[2048,1280]{1,0:T(8,128)(2,1)} %get-tuple-element.186, bf16[1280,640]{1,0:T(8,128)(2,1)} %param.36), kind=kOutput, calls=%fused_computation.73 | convolution fusion | flops 3356753920 | bytes 9502720 | tf_op jit(solution)/shard_map/dot_general | solution.py:125
  317.2 42.1 %reduce-scatter.9.cloned.1.call-done = bf16[512,640]{1,0:T(8,128)(2,1)} async-done(((bf16[2048,640]{1,0:T(8,128)(2,1)}), bf16[512,640]{1,0:T(8,128)(2,1)}) %reduce-scatter.9.cloned.1.call-update) | async-done | bytes 655376 | tf_op jit(solution)/shard_map/reduce_scatter | solution.py:141
  361.8 52.1 %reduce-scatter.7.cloned.1.call-done = bf16[512,640]{1,0:T(8,128)(2,1)} async-done(((bf16[2048,640]{1,0:T(8,128)(2,1)}), bf16[512,640]{1,0:T(8,128)(2,1)}) %reduce-scatter.7.cloned.1.call-update) | async-done | bytes 655376 | tf_op jit(solution)/shard_map/reduce_scatter | solution.py:124
  418.2 54.6 %all-gather.11.cloned.1.call-done = bf16[2048,640]{1,0:T(8,128)(2,1)} async-done(((bf16[512,640]{1,0:T(8,128)(2,1)}), bf16[2048,640]{1,0:T(8,128)(2,1)}) %all-gather.11.cloned.1.call-update) | async-done | bytes 2621456 | tf_op jit(solution)/shard_map/all_gather | solution.py:151
  475.5 126.8 %while.23 = (s32[]{:T(128)}, bf16[2,1024,3,5,32]{1,4,3,2,0:T(8,128)(2,1)}, s32[2]{0:T(128)S(1)}, bf16[2048,5,32]{0,2,1:T(8,128)(2,1)S(1)}, s32[2048]{0:T(1024)S(...) while((s32[]{:T(128)}, ...), condition=%wide.region_17.18_spmd, body=%wide.region_15.17_spmd.sunk | while | flops 1762225152 | bytes 182637856 | solution.py:177
  487.1 9.6 %fusion.148 = f32[5,1024,1024]{1,2,0:T(8,128)} fusion(bf16[2048,5,32]{0,2,1:T(8,128)(2,1)} %get-tuple-element.400, s32[]{:T(128)S(6)} %select_n.124, bf16[2048,5,32]{0,2,1:T(8,128)(2,1)S(1)} %get-tuple-element.397), kind=kOutput, calls=%fused_computation.40.clone.1 | convolution fusion | flops 335544320 | bytes 21627904 | tf_op jit(solution)/shard_map/while/body/eval_jaxpr/qhd,khd->hqk/dot_general | solution.py:94
  496.7 9.7 %fusion.149 = bf16[1,1024,1,5,32]{1,4,3,2,0:T(8,128)(2,1)S(1)} fusion(f32[5,1024,1024]{1,2,0:T(8,128)} %fusion.148, f32[5,1024]{1,0:T(8,128)S(1)} %dynamic-slice_bitcast_fusion.2, pred[1024,1024]{0,1:T(8,128)(4,1)S(1)} %compare_and_fusion.5, bf16[2048,5,32]{0,2,1:T(8,128)(2,1)S(1)} %get-tuple-element.402, s32[]{:T(128)S(6)} %select_n.124), kind=kOutput, calls=%fused_computation.31.clone.1 | convolution fusion | flops 356679680 | bytes 22708228 | tf_op jit(solution)/shard_map/while/body/eval_jaxpr/hqk,qhd->khd/dot_general | solution.py:162
  506.5 14.5 %multiply_reduce_fusion.3 = (f32[5,1024]{1,0:T(8,128)S(1)}, f32[5,1024,1024]{1,2,0:T(8,128)}) fusion(f32[5,1024,1024]{1,2,0:T(8,128)} %fusion.148, f32[5,1024]{1,0:T(8,128)S(1)} %dynamic-slice_bitcast_fusion.2, pred[1024,1024]{0,1:T(8,128)(4,1)S(1)} %compare_and_fusion.5, bf16[2048,5,32]{0,2,1:T(8,128)(2,1)} %get-tuple-element.403, ...), kind=kOutput, calls=%fused_computation.20.clone.1 | convolution fusion | flops 361753600 | bytes 43701248 | tf_op jit(solution)/shard_map/while/body/eval_jaxpr/qhd,khd->hqk/dot_general | solution.py:165
  520.9 14.9 %multiply_convert_fusion.3 = bf16[5,1024,1024]{1,2,0:T(8,128)(2,1)S(1)} fusion(f32[5,1024,1024]{1,2,0:T(8,128)} %get-tuple-element.325, f32[5,1024,1024]{1,2,0:T(8,128)} %fusion.148, f32[5,1024]{1,0:T(8,128)S(1)} %get-tuple-element.326, f32[5,1024]{1,0:T(8,128)S(1)} %dynamic-slice_bitcast_fusion.2, pred[1024,1024]{0,1:T(8,128)(4,1)S(1)} %compare_and_fusion.5), kind=kLoop, calls=%fused_computation.19.clone.1 | loop fusion | flops 31457280 | bytes 53518336 | tf_op jit(solution)/shard_map/while/body/eval_jaxpr/convert_element_type | solution.py:168
  545.8 9.6 %fusion.148 = f32[5,1024,1024]{1,2,0:T(8,128)} fusion(bf16[2048,5,32]{0,2,1:T(8,128)(2,1)} %get-tuple-element.400, s32[]{:T(128)S(6)} %select_n.124, bf16[2048,5,32]{0,2,1:T(8,128)(2,1)S(1)} %get-tuple-element.397), kind=kOutput, calls=%fused_computation.40.clone.1 | convolution fusion | flops 335544320 | bytes 21627904 | tf_op jit(solution)/shard_map/while/body/eval_jaxpr/qhd,khd->hqk/dot_general | solution.py:94
  555.4 9.7 %fusion.149 = bf16[1,1024,1,5,32]{1,4,3,2,0:T(8,128)(2,1)S(1)} fusion(f32[5,1024,1024]{1,2,0:T(8,128)} %fusion.148, f32[5,1024]{1,0:T(8,128)S(1)} %dynamic-slice_bitcast_fusion.2, pred[1024,1024]{0,1:T(8,128)(4,1)S(1)} %compare_and_fusion.5, bf16[2048,5,32]{0,2,1:T(8,128)(2,1)S(1)} %get-tuple-element.402, s32[]{:T(128)S(6)} %select_n.124), kind=kOutput, calls=%fused_computation.31.clone.1 | convolution fusion | flops 356679680 | bytes 22708228 | tf_op jit(solution)/shard_map/while/body/eval_jaxpr/hqk,qhd->khd/dot_general | solution.py:162
  565.1 14.5 %multiply_reduce_fusion.3 = (f32[5,1024]{1,0:T(8,128)S(1)}, f32[5,1024,1024]{1,2,0:T(8,128)}) fusion(f32[5,1024,1024]{1,2,0:T(8,128)} %fusion.148, f32[5,1024]{1,0:T(8,128)S(1)} %dynamic-slice_bitcast_fusion.2, pred[1024,1024]{0,1:T(8,128)(4,1)S(1)} %compare_and_fusion.5, bf16[2048,5,32]{0,2,1:T(8,128)(2,1)} %get-tuple-element.403, ...), kind=kOutput, calls=%fused_computation.20.clone.1 | convolution fusion | flops 361753600 | bytes 43701248 | tf_op jit(solution)/shard_map/while/body/eval_jaxpr/qhd,khd->hqk/dot_general | solution.py:165
  579.6 14.9 %multiply_convert_fusion.3 = bf16[5,1024,1024]{1,2,0:T(8,128)(2,1)S(1)} fusion(f32[5,1024,1024]{1,2,0:T(8,128)} %get-tuple-element.325, f32[5,1024,1024]{1,2,0:T(8,128)} %fusion.148, f32[5,1024]{1,0:T(8,128)S(1)} %get-tuple-element.326, f32[5,1024]{1,0:T(8,128)S(1)} %dynamic-slice_bitcast_fusion.2, pred[1024,1024]{0,1:T(8,128)(4,1)S(1)} %compare_and_fusion.5), kind=kLoop, calls=%fused_computation.19.clone.1 | loop fusion | flops 31457280 | bytes 53518336 | tf_op jit(solution)/shard_map/while/body/eval_jaxpr/convert_element_type | solution.py:168
  637.2 27.5 %reduce-scatter.11.cloned.1.call-done = bf16[512,640]{1,0:T(8,128)(2,1)} async-done(((bf16[2048,640]{1,0:T(8,128)(2,1)}), bf16[512,640]{1,0:T(8,128)(2,1)}) %reduce-scatter.11.cloned.1.call-update) | async-done | bytes 655376 | tf_op jit(solution)/shard_map/reduce_scatter | solution.py:180
  666.5 25.8 %all-reduce = (f32[640]{0:T(1024)S(1)}, f32[640]{0:T(1024)S(1)}, f32[2,160]{1,0:T(2,128)}, f32[640]{0:T(1024)S(1)}, f32[640]{0:T(1024)S(1)}, /*index=5*/f32[640]{0:T(1024)S(1)}, f32[1280]{0:T(1024)}, f32[640]{0:T(1024)S(1)}) all-reduce(f32[640]{0:T(1024)S(1)} %get-tuple-element.119, ...), channel_id=1, replica_groups=mesh['dp'=8,'tensor'=4] {'dp'}, use_global_device_ids=true, to_apply=%region_22.23 | all-reduce | flops 5440 | bytes 43520 | tf_op jit(solution)/shard_map/psum | solution.py:203
  692.3 18.1 %all-reduce.2 = (f32[640]{0:T(1024)}, f32[640]{0:T(1024)}, f32[640]{0:T(1024)}, f32[640]{0:T(1024)}, f32[640]{0:T(1024)}, /*index=5*/f32[640]{0:T(1024)}) all-reduce(f32[640]{0:T(1024)S(1)} %get-tuple-element.163, f32[640]{0:T(1024)S(1)} %get-tuple-element.164, ...), channel_id=1, replica_groups=mesh['dp'=8,'tensor'=4] {'tensor'}, use_global_device_ids=true, to_apply=%region_23.24 | all-reduce | flops 3840 | bytes 30720 | tf_op jit(solution)/shard_map/psum | solution.py:220
  713.1 83.2 %all-reduce.5.cloned.1.call-done = (f32[3,640,160]{1,2,0:T(8,128)}, f32[160,640]{1,0:T(8,128)}, f32[640,1280]{1,0:T(8,128)}, f32[1280,640]{1,0:T(8,128)}) async-done(((f32[3,640,160]{1,2,0:T(8,128)}, f32[160,640]{1,0:T(8,128)}, f32[640,1280]{1,0:T(8,128)}, f32[1280,640]{1,0:T(8,128)}), (f32[3,640,160]{1,2,0:T(8,128)}, f32[160,640]{1,0:T(8,128)}, f32[640,1280]{1,0:T(8,128)}, ...) | async-done | bytes 8192016 | tf_op jit(solution)/shard_map/psum | solution.py:203
  (175 shorter events, 150.2 us)
Async XLA Ops:
  7.2 223.6 %copy-start = (bf16[640,1280]{1,0:T(8,128)(2,1)S(1)}, bf16[640,1280]{1,0:T(8,128)(2,1)}, u32[]{:S(2)}) copy-start(bf16[640,1280]{1,0:T(8,128)(2,1)} %param.34) | copy-start | bytes 4915204
  7.2 62.8 %all-gather.5.cloned.1.call-start = ((), (), s32[]{:S(2)}) async-start(), calls=%async_computation.4 | async-start | bytes 3276800 | tf_op jit(solution)/shard_map/all_gather | solution.py:79
  8.6 65.0 %copy-start.16 = (f32[512]{0:T(512)}, f32[512]{0:T(512)S(1)}, u32[]{:S(2)}) copy-start(f32[512]{0:T(512)S(1)} %broadcast_multiply_fusion.5) | copy-start | bytes 6148
  10.0 63.6 %copy-start.20 = (f32[512]{0:T(512)}, f32[512]{0:T(512)S(1)}, u32[]{:S(2)}) copy-start(f32[512]{0:T(512)S(1)} %add_rsqrt_fusion.1) | copy-start | bytes 6148
  12.3 158.5 %reduce-scatter.5.cloned.1.call-start = ((), (), s32[]{:S(2)}) async-start(), calls=%async_computation.5 | async-start | bytes 3276800 | tf_op jit(solution)/shard_map/reduce_scatter | solution.py:112
  75.1 42.2 %copy-start.14 = (bf16[160,640]{1,0:T(8,128)(2,1)S(1)}, bf16[160,640]{1,0:T(8,128)(2,1)}, u32[]{:S(2)}) copy-start(bf16[160,640]{1,0:T(8,128)(2,1)} %param.30) | copy-start | bytes 614404
  114.4 56.5 %copy-start.2 = (bf16[512,640]{1,0:T(8,128)(2,1)S(1)}, bf16[512,640]{1,0:T(8,128)(2,1)}, u32[]{:S(2)}) copy-start(bf16[512,640]{1,0:T(8,128)(2,1)} %param.21) | copy-start | bytes 1966084
  114.4 56.5 %copy-start.15 = (f32[640]{0:T(1024)S(1)}, f32[640]{0:T(1024)}, u32[]{:S(2)}) copy-start(f32[640]{0:T(1024)} %param.31) | copy-start | bytes 7684
  116.2 57.5 %copy-start.19 = (f32[640]{0:T(1024)S(1)}, f32[640]{0:T(1024)}, u32[]{:S(2)}) copy-start(f32[640]{0:T(1024)} %param.32) | copy-start | bytes 7684
  116.2 57.5 %copy-start.27 = (f32[640]{0:T(1024)S(1)}, f32[640]{0:T(1024)}, u32[]{:S(2)}) copy-start(f32[640]{0:T(1024)} %param.33) | copy-start | bytes 7684
  117.3 58.9 %copy-start.33 = (f32[3]{0:T(128)S(1)}, f32[3]{0:T(128)}, u32[]{:S(2)}) copy-start(f32[3]{0:T(128)} %param.25) | copy-start | bytes 40
  119.8 110.9 %copy-start.32 = (f32[1280]{0:T(1024)S(1)}, f32[1280]{0:T(1024)}, u32[]{:S(2)}) copy-start(f32[1280]{0:T(1024)} %param.35) | copy-start | bytes 15364
  119.8 110.9 %all-gather.7.cloned.1.call-start = ((), (), s32[]{:S(2)}) async-start(), calls=%async_computation.6 | async-start | bytes 3276800 | tf_op jit(solution)/shard_map/all_gather | solution.py:121
  176.1 110.3 %all-gather.9.cloned.1.call-start = ((), (), s32[]{:S(2)}) async-start(), calls=%async_computation.8 | async-start | bytes 3276800 | tf_op jit(solution)/shard_map/all_gather | solution.py:135
  180.2 179.1 %reduce-scatter.9.cloned.1.call-start = ((), (), s32[]{:S(2)}) async-start(), calls=%async_computation.9 | async-start | bytes 3276800 | tf_op jit(solution)/shard_map/reduce_scatter | solution.py:141
  308.2 105.6 %reduce-scatter.7.cloned.1.call-start = ((), (), s32[]{:S(2)}) async-start(), calls=%async_computation.7 | async-start | bytes 3276800 | tf_op jit(solution)/shard_map/reduce_scatter | solution.py:124
  308.3 51.0 %copy-start.5 = (bf16[512,640]{1,0:T(8,128)(2,1)S(1)}, bf16[512,640]{1,0:T(8,128)(2,1)}, u32[]{:S(2)}) copy-start(bf16[512,640]{1,0:T(8,128)(2,1)} %reduce-scatter.5.cloned.1.call-done) | copy-start | bytes 1966084
  308.3 105.6 %copy-start.11 = (bf16[512,640]{1,0:T(8,128)(2,1)S(1)}, bf16[512,640]{1,0:T(8,128)(2,1)}, u32[]{:S(2)}) copy-start(bf16[512,640]{1,0:T(8,128)(2,1)} %param.22) | copy-start | bytes 1966084
  308.3 105.6 %copy-start.28 = (f32[640]{0:T(1024)S(1)}, f32[640]{0:T(1024)}, u32[]{:S(2)}) copy-start(f32[640]{0:T(1024)} %param.37) | copy-start | bytes 7684
  317.2 155.6 %all-gather.11.cloned.1.call-start = ((), (), s32[]{:S(2)}) async-start(), calls=%async_computation.10 | async-start | bytes 3276800 | tf_op jit(solution)/shard_map/all_gather | solution.py:151
  418.1 246.5 %reduce-scatter.11.cloned.1.call-start = ((), (), s32[]{:S(2)}) async-start(), calls=%async_computation.11 | async-start | bytes 3276800 | tf_op jit(solution)/shard_map/reduce_scatter | solution.py:180
  613.6 182.7 %all-reduce.5.cloned.1.call-start = ((), (), s32[]{:S(2)}) async-start(), calls=%async_computation.12 | async-start | bytes 16384000 | tf_op jit(solution)/shard_map/psum | solution.py:203
  635.4 31.1 %copy-start.22 = (f32[640]{0:T(1024)S(1)}, f32[640]{0:T(1024)}, u32[]{:S(2)}) copy-start(f32[640]{0:T(1024)} %get-tuple-element.181) | copy-start | bytes 7684
  635.4 75.0 %copy-start.9 = (f32[512,640]{1,0:T(8,128)S(1)}, f32[512,640]{1,0:T(8,128)}, u32[]{:S(2)}) copy-start(f32[512,640]{1,0:T(8,128)} %get-tuple-element.185) | copy-start | bytes 3932164
  (22 other events, 324.7 us)
Sparse Core Ops, SparseCore 0:
  12.4 57.4 all-gather.4
  119.9 50.8 reduce-scatter.4
  176.2 54.4 all-gather.6
  232.7 53.5 all-gather.8
  308.4 50.8 reduce-scatter.8
  362.0 51.7 reduce-scatter.6
  418.3 54.4 all-gather.10
  613.7 50.8 reduce-scatter.10
  669.9 126.3 all-reduce.4
where the time goes:
time: 822 us; the launch traced here: 813 us
  waiting for transfers between devices  443 us (54%)
  matrix products  198 us (24%)
  other arithmetic  72 us (9%)
  blocking collectives  43.9 us (5%)
  local copies, waits for them, and re-layouts  28.6 us (3%)
  between operations  15.3 us (2%)
  loops' own time  12.4 us (2%)
    psum x1, waiting for transfers between devices, local(): lax.psum((grad_qkv, grad_qv_bias, grad_w_out, grad_up, grad_up_bias, grad...  83.2 us
    all_gather x1, waiting for transfers between devices, local(): normed_all = lax.all_gather(normed, 'tensor', axis=0, tiled=True)  55 us
    all_gather x1, waiting for transfers between devices, local(): branch_all = lax.all_gather(branch_low, 'tensor', axis=0, tiled=True)  54.6 us
    reduce_scatter x1, waiting for transfers between devices, local(): lax.psum_scatter(jnp.dot(active, w_down, preferred_element_type=f32).asty...  52.1 us
    reduce_scatter x1, waiting for transfers between devices, local(): lax.psum_scatter(jnp.dot(mixed, w_out, preferred_element_type=f32).astype...  51 us
    all_gather x1, waiting for transfers between devices, local(): normed2_all = lax.all_gather(normed2, 'tensor', axis=0, tiled=True)  50.2 us
    reduce_scatter x1, waiting for transfers between devices, local(): lax.psum_scatter(jnp.einsum('rf,df->rd', hidden_grad, w_up, preferred_ele...  42.1 us
    convert_element_type x2, other arithmetic, backward_window(): score_grad = (probs * (prob_grad - jnp.sum(probs * prob_grad, axis=-1, ke...  29.7 us
  transfers between devices with their start and end apart: 9, of which 9 were waited for; matrix products, arithmetic and copies ran while one was open for 9% of the time, Pallas kernels for 0%

commit v1 on v0

v1 whole, which is shorter than its diff:
```python
import functools
import math

import jax
import jax.numpy as jnp
from jax import lax
from jax.experimental import pallas as pl
from jax.experimental.pallas import tpu as pltpu
from jax.sharding import PartitionSpec as P

HD = 32
BUCKET = 256
EPSILON = 1e-05
GROUP = 8
BLK = 256
BIG = 1e30
F32 = jnp.float32
BF16 = jnp.bfloat16
MESH = pl.DeviceIdType.MESH
RSQRT2 = 1.0 / math.sqrt(2.0)
RSQRT2PI = 1.0 / math.sqrt(2.0 * math.pi)
SLOTS_C = 2
G_LAG1 = 8
G_LAG2 = 5


def nn(a, b):
    return lax.dot_general(a, b, (((1,), (0,)), ((), ())), preferred_element_type=F32)


def nt(a, b):
    return lax.dot_general(a, b, (((1,), (1,)), ((), ())), preferred_element_type=F32)


def unit_of(values):
    centre = values - jnp.mean(values, axis=-1, keepdims=True)
    scale_inv = lax.rsqrt(jnp.mean(centre * centre, axis=-1, keepdims=True) + EPSILON)
    return centre * scale_inv, scale_inv


def norm_back(grad, unit, scale_inv, gain):
    scaled = grad * gain
    return scale_inv * (
        scaled
        - jnp.mean(scaled, axis=-1, keepdims=True)
        - unit * jnp.mean(scaled * unit, axis=-1, keepdims=True)
    )


def lanes(shape):
    return lax.broadcasted_iota(jnp.int32, shape, 1)


def kernel(
    x_ref,
    cot_ref,
    len_ref,
    bid_ref,
    bw_ref,
    g1_ref,
    s1_ref,
    wqkv_ref,
    qvb_ref,
    wout_ref,
    bout_ref,
    g2_ref,
    s2_ref,
    wup_ref,
    bup_ref,
    wdn_ref,
    bdn_ref,
    lo_ref,
    xg_ref,
    of_ref,
    oa_ref,
    osm_ref,
    ph_ref,
    fg,
    aw,
    rc_f,
    r2_f,
    r1_f,
    rz_f,
    rc_a,
    r2_a,
    r1_a,
    rz_a,
    xn,
    xp,
    qb,
    kb,
    vb,
    mx,
    dob,
    dd,
    pst,
    mid,
    acc0,
    acc1,
    uu,
    ol,
    olt,
    xnt,
    ngs,
    ngr,
    bupa,
    qvba,
    early,
    late,
    e_rx,
    e_rz,
    l_rx,
    l_rz,
    loc_sem,
    ps_sem,
    za_s,
    za_r,
    zx_sem,
    zb_s,
    zb_r,
    ga_s,
    ga_r,
    zf_s,
    zf_r,
    gf_s,
    gf_r,
    cf_s,
    cf_r,
    f2_s,
    f2_r,
    f1_s,
    f1_r,
    fz_s,
    fz_r,
    af_s,
    af_r,
    ca_s,
    ca_r,
    a2_s,
    a2_r,
    a1_s,
    a1_r,
    az_s,
    az_r,
    aa_s,
    aa_r,
    sm_s,
    sm_r,
    ng_sem,
    credit,
):
    share, width = x_ref.shape
    hw = wqkv_ref.shape[2]
    heads = hw // HD
    qkvw = 3 * hw
    parts = 4
    nblk = wup_ref.shape[1] // BLK
    piece = width // GROUP
    keys = 2 * share
    factor = HD ** (-0.5)
    q_scale = factor * math.log2(math.e)

    d = lax.axis_index("dp")
    t = lax.axis_index("tensor")
    c = d % 2
    bx = (d // 2) % 2
    by = (d // 4) % 2
    dev_c = (d + 1 - 2 * c, t)
    dx = d + 2 - 4 * bx
    dy = d + 4 - 8 * by
    tp = t + 1 - 2 * (t % 2)

    def far(k):
        return (t + k) % parts

    def route(par):
        low = bx + par * (by - bx)
        high = by + par * (bx - by)
        first = (dx + par * (dy - dx), t)
        second = (dy + par * (dx - dy), t)
        return low, high, first, second

    def rcopy(src, dst, ssem, rsem, dev):
        return pltpu.make_async_remote_copy(
            src_ref=src, dst_ref=dst, send_sem=ssem, recv_sem=rsem, device_id=dev, device_id_type=MESH
        )

    def rows(start, size):
        return pl.ds(pl.multiple_of(start, 16), size)

    def up_load(j):
        return pltpu.make_async_copy(
            wup_ref.at[:, pl.ds(j * BLK, BLK)], fg.at[t * nblk + j, 0], loc_sem.at[j]
        )

    def dn_load(j):
        return pltpu.make_async_copy(
            wdn_ref.at[pl.ds(j * BLK, BLK), :],
            uu.at[j // 2, pl.ds((j % 2) * BLK, BLK), :],
            loc_sem.at[nblk + j],
        )

    for j in range(nblk):
        up_load(j).start()
        dn_load(j).start()
    cot_load = pltpu.make_async_copy(cot_ref, ol, loc_sem.at[2 * nblk])
    cot_load.start()

    aw[t, :, 0:hw] = wqkv_ref[0]
    aw[t, :, hw : 2 * hw] = wqkv_ref[1]
    aw[t, :, 2 * hw : 3 * hw] = wqkv_ref[2]
    aw[t, :, 3 * hw : 4 * hw] = wout_ref[...].T

    barrier = pltpu.get_barrier_semaphore()
    for dev in (dev_c, (dx, t), (dy, t), (d, far(1)), (d, far(2)), (d, far(3))):
        pl.semaphore_signal(barrier, inc=1, device_id=dev, device_id_type=MESH)
    pl.semaphore_wait(barrier, 6)

    low_a, high_a, first_a, second_a = route(t % 2)
    pos_own_a = (c * 4 + high_a * 2 + low_a) * piece

    def za(k):
        view = aw.at[t, rows(pos_own_a, piece), :]
        return rcopy(view, view, za_s.at[k - 1], za_r.at[t], (d, far(parts - k)))

    def za_wait(s, par):
        low, high, _, _ = route(par)
        view = aw.at[s, rows((c * 4 + high * 2 + low) * piece, piece), :]
        rcopy(view, view, za_s.at[0], za_r.at[s], (d, t)).wait_recv()

    def zb(k, which):
        src = bup_ref if which == 0 else qvb_ref
        dst = (bupa if which == 0 else qvba).at[t]
        return rcopy(src, dst, zb_s.at[2 * (k - 1) + which], zb_r.at[which, t], (d, far(parts - k)))

    def zb_wait(s, which):
        src = bup_ref if which == 0 else qvb_ref
        dst = (bupa if which == 0 else qvba).at[s]
        rcopy(src, dst, zb_s.at[0], zb_r.at[which, s], (d, t)).wait_recv()

    x_copy = rcopy(x_ref, xp, zx_sem.at[0], zx_sem.at[1], (d, tp))

    for k in range(1, parts):
        za(k).start()
        zb(k, 1).start()
    x_copy.start()
    for k in range(1, parts):
        zb(k, 0).start()
    bupa[t] = bup_ref[...]
    qvba[t] = qvb_ref[...]

    gain1 = g1_ref[...]
    shift1 = s1_ref[...]
    unit, _ = unit_of(x_ref[...].astype(F32))
    normed = (unit * gain1 + shift1).astype(BF16)
    xn[0:share, :] = normed
    xnt[:, 0:share] = normed.T

    bucket = bid_ref[0]
    span = jnp.where(bucket == 0, BUCKET, jnp.where(bucket == 1, 2 * BUCKET, 4 * BUCKET))
    weight = jnp.where(bucket == 0, bw_ref[0], jnp.where(bucket == 1, bw_ref[1], bw_ref[2]))

    def slot_info(base, shape):
        place = base + lax.broadcasted_iota(jnp.int32, shape, 0)
        item = jnp.zeros(shape, jnp.int32)
        for j in range(1, len_ref.shape[1]):
            item = item + jnp.where(place >= j * span, 1, 0)
        length = jnp.zeros(shape, jnp.int32)
        for j in range(len_ref.shape[1]):
            length = jnp.where(item == j, len_ref[0, j], length)
        return item, (place - item * span) < length

    wide = (share, 2 * 128)
    lane = lanes(wide)
    slots = len_ref.shape[1]
    in_aux = (lane >= hw) & (lane < hw + slots)
    one_aux = jnp.where(lane >= hw, 1.0, 0.0).astype(BF16)

    own_item, own_live = slot_info(t * share, wide)
    q_aux = jnp.where(in_aux & (own_item == lane - hw), 1.0, 0.0).astype(BF16)
    k_aux0 = jnp.where(in_aux & ~((own_item == lane - hw) & own_live), -BIG, 0.0).astype(BF16)
    pair_item, pair_live = slot_info(tp * share, wide)
    k_aux1 = jnp.where(in_aux & ~((pair_item == lane - hw) & pair_live), -BIG, 0.0).astype(BF16)
    for s in range(parts):
        qb[s] = q_aux
        kb[s, 0:share] = k_aux0
        kb[s, share:keys] = k_aux1
        vb[s, 0:share] = one_aux
        vb[s, share:keys] = one_aux
    _, live1 = slot_info(t * share, (share, 128))
    row_weight = jnp.where(live1, weight, 0.0)[:, 0:1]

    def zf(k, j):
        low, high, _, _ = route((t + j) % 2)
        view = fg.at[t * nblk + j, :, rows((c * 4 + high * 2 + low) * piece, piece), :]
        return rcopy(
            view, view, zf_s.at[(k - 1) * nblk + j], zf_r.at[t * nblk + j], (d, far(parts - k))
        )

    for j in range(nblk):
        up_load(j).wait()
        dn_load(j).wait()
        fg[t * nblk + j, 1] = uu[j // 2, (j % 2) * BLK : (j % 2 + 1) * BLK, :].T
    for k in range(1, parts):
        for j in range(nblk):
            zf(k, j).start()

    def ga(stage, s):
        low, high, first, second = route(s % 2)
        if stage == 0:
            view, dev = aw.at[s, rows((c * 4 + high * 2 + low) * piece, piece), :], first
        elif stage == 1:
            view, dev = aw.at[s, rows((c * 4 + high * 2) * piece, 2 * piece), :], second
        else:
            view, dev = aw.at[s, rows(c * 4 * piece, 4 * piece), :], dev_c
        return rcopy(view, view, ga_s.at[stage, s], ga_r.at[stage, s], dev)

    def project(s, base, own):
        bias_q = qvba[s, 0:1, :]
        bias_v = qvba[s, 1:2, :]
        out = nn(xn[base : base + share, :], aw[s, :, 0:qkvw])
        if own:
            qb[s, :, 0:hw] = ((out[:, 0:hw] + bias_q) * q_scale).astype(BF16)
        kb[s, base : base + share, 0:hw] = out[:, hw : 2 * hw].astype(BF16)
        vb[s, base : base + share, 0:hw] = (out[:, 2 * hw : 3 * hw] + bias_v).astype(BF16)

    for k in range(1, parts):
        s = far(k)
        za_wait(s, s % 2)
        ga(0, s).start()
    project(t, 0, True)
    for stage in (1, 2):
        for k in range(1, parts):
            s = far(k)
            ga(stage - 1, s).wait_recv()
            ga(stage, s).start()
    for k in range(1, parts):
        s = far(k)
        zb_wait(s, 1)
        ga(2, s).wait_recv()
        project(s, 0, True)

    x_copy.wait_recv()
    unit, _ = unit_of(xp[...].astype(F32))
    normed = (unit * gain1 + shift1).astype(BF16)
    xn[share:keys, :] = normed
    xnt[:, share:keys] = normed.T

    def pair_project(k, carry):
        project(far(k), share, False)
        return carry

    lax.fori_loop(0, parts, pair_project, 0)

    n_far = (parts - 1) * nblk

    def far_block(m):
        s = (t + 1 + m // nblk) % parts
        j = m % nblk
        return s, j, s * nblk + j

    def gf(stage, m):
        s, j, b = far_block(m)
        low, high, first, second = route((s + j) % 2)
        if stage == 0:
            view, dev = fg.at[b, :, rows((c * 4 + high * 2 + low) * piece, piece), :], first
        elif stage == 1:
            view, dev = fg.at[b, :, rows((c * 4 + high * 2) * piece, 2 * piece), :], second
        else:
            view, dev = fg.at[b, :, rows(c * 4 * piece, 4 * piece), :], dev_c
        return rcopy(view, view, gf_s.at[stage, b], gf_r.at[stage, b], dev)

    def zf_wait(m):
        s, j, b = far_block(m)
        low, high, _, _ = route((s + j) % 2)
        view = fg.at[b, :, rows((c * 4 + high * 2 + low) * piece, piece), :]
        rcopy(view, view, zf_s.at[0], zf_r.at[b], (d, t)).wait_recv()

    def within(n, size):
        return (n >= 0) & (n < size)

    def gather_tick(n):
        @pl.when(within(n, n_far))
        def _():
            zf_wait(n)
            gf(0, n).start()

        @pl.when(within(n - 1, n_far))
        def _():
            gf(0, n - 1).wait_recv()
            gf(1, n - 1).start()

        @pl.when(within(n - 2, n_far))
        def _():
            gf(1, n - 2).wait_recv()
            gf(2, n - 2).start()

    def p_out(s, h, slot):
        return (
            pltpu.make_async_copy(
                pst.at[2 * slot], ph_ref.at[s * heads + h, 0], ps_sem.at[2 * slot]
            ),
            pltpu.make_async_copy(
                pst.at[2 * slot + 1], ph_ref.at[s * heads + h, 1], ps_sem.at[2 * slot + 1]
            ),
        )

    def att_forward(k, carry):
        s = far(k)
        qg = qb[s]
        kg = kb[s]
        vg = vb[s]
        lane_q = lanes((share, 2 * 128))
        out = jnp.zeros((share, 2 * 128), F32)
        for h in range(heads):
            head = (lane_q >= HD * h) & (lane_q < HD * (h + 1))
            qm = jnp.where(head | (lane_q >= hw), qg, jnp.zeros_like(qg))
            scores = nt(qm, kg)
            top = jnp.max(scores, axis=1, keepdims=True)
            probs = jnp.exp2(scores - top).astype(BF16)
            idx = k * heads + h
            slot = idx % 2

            @pl.when(idx >= 2)
            def _():
                for cp in p_out(s, h, slot):
                    cp.wait()

            pst[2 * slot] = probs[:, 0:share]
            pst[2 * slot + 1] = probs[:, share:keys]
            for cp in p_out(s, h, slot):
                cp.start()
            mixed = nn(probs, vg)
            inv_h = 1.0 / mixed[:, hw : hw + 1]
            out = jnp.where(head, mixed * inv_h, out)
            coarse = inv_h.astype(BF16).astype(F32)
            out = jnp.where(lane_q == hw + 2 * h, coarse, out)
            out = jnp.where(lane_q == hw + 2 * h + 1, inv_h - coarse, out)
        mx[s] = out.astype(BF16)
        gather_tick(2 * k)
        gather_tick(2 * k + 1)
        return carry

    lax.fori_loop(0, parts, att_forward, 0)
    for slot in range(2):
        for cp in p_out(0, 0, slot):
            cp.wait()

    branch = jnp.zeros((share, width), F32)
    for s in range(parts):
        branch = branch + nt(mx[s, :, 0:hw], aw[s, :, qkvw : 4 * hw])
    middle = x_ref[...].astype(F32) + (branch + bout_ref[...])
    mid[...] = middle
    unit, _ = unit_of(middle)
    normed = (unit * g2_ref[...] + s2_ref[...]).astype(BF16)
    n2 = uu.at[0, 0:share, :]
    n2t = uu.at[1, :, 0:share]
    n2[...] = normed
    n2t[...] = normed.T
    cot_load.wait()
    low_grad = (ol[...].astype(F32) * row_weight).astype(BF16)
    early[...] = jnp.zeros_like(early)
    late[...] = jnp.zeros_like(late)
    early[3:4, :] = jnp.sum(low_grad.astype(F32), axis=0, keepdims=True)
    ol[...] = low_grad
    olt[...] = low_grad.T
    acc0[...] = jnp.zeros_like(acc0)
    acc1[...] = jnp.zeros_like(acc1)

    for k in range(1, parts):
        zb_wait(far(k), 0)

    n_all = parts * nblk

    def block(r):
        k = r // nblk
        j = r % nblk
        s = (t + k) % parts
        home = s * nblk + j
        own = jnp.where(k == 0, 1, 0)
        return k, j, s, home, home + own * (n_all + j - home)

    def rf(stage, r):
        k, j, s, _, g = block(r)
        low, high, first, second = route((s + j) % 2)
        if stage == 0:
            return rcopy(
                fg.at[g, :, rows((1 - c) * 4 * piece, 4 * piece), :],
                rc_f.at[r % SLOTS_C],
                cf_s.at[r],
                cf_r.at[r],
                dev_c,
            )
        if stage == 1:
            return rcopy(
                fg.at[g, :, rows((c * 4 + (1 - high) * 2) * piece, 2 * piece), :],
                r2_f.at[r],
                f2_s.at[r],
                f2_r.at[r],
                second,
            )
        if stage == 2:
            return rcopy(
                fg.at[g, :, rows((c * 4 + high * 2 + 1 - low) * piece, piece), :],
                r1_f.at[r],
                f1_s.at[r],
                f1_r.at[r],
                first,
            )
        z = jnp.maximum(r - nblk, 0)
        return rcopy(
            fg.at[g, :, rows((c * 4 + high * 2 + low) * piece, piece), :],
            rz_f.at[z],
            fz_s.at[z],
            fz_r.at[z],
            (d, s),
        )

    def add_rows(ref, got):
        ref[...] = (ref[...].astype(F32) + got[...].astype(F32)).astype(BF16)

    def rf_second(r):
        k, j, s, _, g = block(r)
        rf(0, r).wait_recv()
        add_rows(fg.at[g, :, rows(c * 4 * piece, 4 * piece), :], rc_f.at[r % SLOTS_C])

        @pl.when(r < n_all - SLOTS_C)
        def _():
            pl.semaphore_signal(credit, inc=1, device_id=dev_c, device_id_type=MESH)

        rf(1, r).start()

    def rf_first(r):
        k, j, s, _, g = block(r)
        low, high, _, _ = route((s + j) % 2)
        rf(1, r).wait_recv()
        add_rows(fg.at[g, :, rows((c * 4 + high * 2) * piece, 2 * piece), :], r2_f.at[r])
        rf(2, r).start()

    def rf_far(r):
        k, j, s, _, g = block(r)
        low, high, _, _ = route((s + j) % 2)
        rf(2, r).wait_recv()
        add_rows(fg.at[g, :, rows((c * 4 + high * 2 + low) * piece, piece), :], r1_f.at[r])

        @pl.when(r >= nblk)
        def _():
            rf(3, r).start()

    def af(stage, j):
        low, high, first, second = route((t + j) % 2)
        b = t * nblk + j
        if stage == 0:
            view, dev = fg.at[b, :, rows((c * 4 + high * 2 + low) * piece, piece), :], first
        elif stage == 1:
            view, dev = fg.at[b, :, rows((c * 4 + high * 2) * piece, 2 * piece), :], second
        else:
            view, dev = fg.at[b, :, rows(c * 4 * piece, 4 * piece), :], dev_c
        return rcopy(view, view, af_s.at[stage, j], af_r.at[stage, j], dev)

    def f_final(j):
        low, high, _, _ = route((t + j) % 2)
        mine = rows((c * 4 + high * 2 + low) * piece, piece)
        total = fg[n_all + j, :, mine, :].astype(F32)
        for k in range(1, parts):
            z = (k - 1) * nblk + j
            rcopy(rz_f.at[z], rz_f.at[z], fz_s.at[z], fz_r.at[z], (d, t)).wait_recv()
            total = total + rz_f[z].astype(F32)
        fg[t * nblk + j, :, mine, :] = total.astype(BF16)
        af(0, j).start()

    def f_out(j):
        return pltpu.make_async_copy(fg.at[t * nblk + j], of_ref.at[j], loc_sem.at[j])

    def final_tick(n):
        @pl.when(within(n, nblk))
        def _():
            f_final(n)

        @pl.when(within(n - 1, nblk))
        def _():
            af(0, n - 1).wait_recv()
            af(1, n - 1).start()

        @pl.when(within(n - 2, nblk))
        def _():
            af(1, n - 2).wait_recv()
            af(2, n - 2).start()

        @pl.when(within(n - 3, nblk))
        def _():
            af(2, n - 3).wait_recv()
            f_out(n - 3).start()

    def reduce_tick(n):
        @pl.when(within(n, n_all))
        def _():
            rf_second(n)

        @pl.when(within(n - G_LAG1, n_all))
        def _():
            rf_first(n - G_LAG1)

        @pl.when(within(n - G_LAG1 - G_LAG2, n_all))
        def _():
            rf_far(n - G_LAG1 - G_LAG2)

    def drain_zf(m, carry):
        view = fg.at[0, :, 0:piece, :]
        rcopy(view, view, zf_s.at[m], zf_r.at[0], (d, t)).wait_send()
        return carry

    def ffn(r, carry):
        k, j, s, home, g = block(r)

        @pl.when(k > 0)
        def _():
            gf(2, jnp.maximum(r - nblk, 0)).wait_recv()

        wu = fg[home, 0]
        wd = fg[home, 1]
        hidden = nn(n2[...], wu) + bupa[s, :, pl.ds(pl.multiple_of(j * BLK, BLK), BLK)]
        cdf = 0.5 + 0.5 * lax.erf(hidden * RSQRT2)
        slope = cdf + hidden * (jnp.exp(-0.5 * hidden * hidden) * RSQRT2PI)
        active = (hidden * cdf).astype(BF16)
        act_grad = nn(ol[...], wd)
        hid_grad = (slope * act_grad).astype(BF16)
        acc0[...] += nt(active, wd)
        acc1[...] += nt(hid_grad, wu)
        early[pl.ds(4 + home, 1), 0:BLK] = jnp.sum(hid_grad.astype(F32), axis=0, keepdims=True)
        up_grad = nn(n2t[...], hid_grad).astype(BF16)
        dn_grad = nn(olt[...], active).astype(BF16)

        @pl.when(k > 0)
        def _():
            for stage in range(3):
                gf(stage, jnp.maximum(r - nblk, 0)).wait_send()

        fg[g, 0] = up_grad
        fg[g, 1] = dn_grad

        @pl.when(r == 2 * nblk)
        def _():
            lax.fori_loop(0, n_far, drain_zf, 0)

        @pl.when(r >= SLOTS_C)
        def _():
            pl.semaphore_wait(credit, 1)

        rf(0, r).start()
        gather_tick(2 * parts + r)
        reduce_tick(r - 1)
        return carry

    lax.fori_loop(0, n_all, ffn, 0)

    middle = mid[...]
    ngs[...] = (middle + (acc0[...] + bdn_ref[...])).astype(BF16)
    lo_copy = pltpu.make_async_copy(ngs, lo_ref, loc_sem.at[2 * nblk])
    lo_copy.start()
    unit, scale_inv = unit_of(middle)
    got = acc1[...]
    early[0:1, :] = jnp.sum(got * unit, axis=0, keepdims=True)
    early[1:2, :] = jnp.sum(got, axis=0, keepdims=True)
    middle_part = norm_back(got, unit, scale_inv, g2_ref[...])
    reload = pltpu.make_async_copy(cot_ref, ol, loc_sem.at[0])
    reload.start()
    reload.wait()
    out_grad = ol[...].astype(F32) * row_weight
    middle_grad = out_grad + middle_part
    mid[...] = middle_grad
    branch_low = middle_grad.astype(BF16)
    early[2:3, :] = jnp.sum(branch_low.astype(F32), axis=0, keepdims=True)
    branch_t = olt
    ol[...] = branch_low
    branch_t[...] = branch_low.T

    for k in range(1, parts):
        za(k).wait_send()
    for k in range(1, parts):
        for stage in range(3):
            ga(stage, far(k)).wait_send()

    def out_back(k, carry):
        s = far(k)
        mixed = mx[s]
        mixed_grad = nn(ol[...], aw[s, :, qkvw : 4 * hw]).astype(BF16).astype(F32)
        inv = mixed[:, 128:256].astype(F32)
        prod = mixed_grad * mixed[:, 0:hw].astype(F32)
        lane_h = lanes((share, hw))
        lane_q = lanes((share, 2 * 128))
        scaled = jnp.zeros((share, hw), F32)
        aux = jnp.zeros((share, 2 * 128), F32)
        for h in range(heads):
            head = (lane_h >= HD * h) & (lane_h < HD * (h + 1))
            at = hw - 128 + 2 * h
            inv_h = inv[:, at : at + 1] + inv[:, at + 1 : at + 2]
            scaled = jnp.where(head, mixed_grad * inv_h, scaled)
            delta = -jnp.sum(jnp.where(head, prod, 0.0), axis=1, keepdims=True) * inv_h
            coarse = delta.astype(BF16).astype(F32)
            aux = jnp.where(lane_q == hw + 2 * h, coarse, aux)
            aux = jnp.where(lane_q == hw + 2 * h + 1, delta - coarse, aux)
        dob[s] = aux.astype(BF16)
        dob[s, :, 0:hw] = scaled.astype(BF16)
        aw[s, :, qkvw : 4 * hw] = nn(branch_t[...], mixed[:, 0:hw]).astype(BF16)
        reduce_tick(n_all - 1 + k)
        return carry

    lax.fori_loop(0, parts, out_back, 0)

    def p_in(s, h, half):
        return pltpu.make_async_copy(ph_ref.at[s * heads + h, half], pst.at[h], ps_sem.at[h])

    def group_of(it):
        return (t + 1 + it % parts) % parts

    def fetch(it):
        for h in range(heads):
            p_in(group_of(it), h, 1 - it // parts).start()

    def att_group(it, half):
        s = group_of(it)
        base = half * share
        qg = qb[s]
        dg = dob[s]
        kg = kb[s, base : base + share]
        vg = vb[s, base : base + share]
        qt = qg[:, 0:hw].T
        dt = dg[:, 0:hw].T
        lane_q = lanes((share, 2 * 128))
        dq = jnp.zeros((share, 2 * 128), F32)
        dks = []
        dvs = []
        for h in range(heads):
            head = (lane_q >= HD * h) & (lane_q < HD * (h + 1))
            aux = (lane_q >= hw + 2 * h) & (lane_q < hw + 2 * h + 2)
            dm = jnp.where(head | aux, dg, jnp.zeros_like(dg))
            prob_grad = nt(dm, vg)
            p_in(s, h, half).wait()
            probs = pst[h]
            score_grad = (probs.astype(F32) * prob_grad).astype(BF16)
            dq = jnp.where(head, nn(score_grad, kg), dq)
            dks.append(nn(qt[HD * h : HD * (h + 1)], score_grad))
            dvs.append(nn(dt[HD * h : HD * (h + 1)], probs))
        dk = (jnp.concatenate(dks, axis=0) * math.log(2.0)).astype(BF16)
        dv = jnp.concatenate(dvs, axis=0).astype(BF16)
        return s, dq[:, 0:hw] * factor, dk.T, dv.T

    acc0[...] = jnp.zeros_like(acc0)
    acc1[...] = jnp.zeros_like(acc1)
    fetch(0)

    def pair_half(it, carry):
        s, dq, dk, dv = att_group(it, 1)
        fetch(it + 1)
        uu[s, 0:share, qkvw : 4 * hw] = dq.astype(BF16)
        uu[s, 0:share, 0:hw] = jnp.zeros((share, hw), BF16)
        uu[s, 0:share, hw : 2 * hw] = dk
        uu[s, 0:share, 2 * hw : 3 * hw] = dv
        acc0[...] += nt(uu[s, 0:share, 0:qkvw], aw[s, :, 0:qkvw])
        late[pl.ds(2 * s + 1, 1), 0:hw] = jnp.sum(dv.astype(F32), axis=0, keepdims=True)
        reduce_tick(n_all - 1 + parts + 2 * it)
        reduce_tick(n_all - 1 + parts + 2 * it + 1)
        return carry

    lax.fori_loop(0, parts, pair_half, 0)

    ng_copy = rcopy(ngs, ngr, ng_sem.at[0], ng_sem.at[1], (d, tp))
    pair_grad = acc0[...]
    lo_copy.wait()
    ngs[...] = pair_grad.astype(BF16)
    ng_copy.start()
    unit, _ = unit_of(xp[...].astype(F32))
    late[8:9, :] = jnp.sum(pair_grad * unit, axis=0, keepdims=True)
    late[9:10, :] = jnp.sum(pair_grad, axis=0, keepdims=True)

    def ra(stage, q):
        s = group_of(q)
        low, high, first, second = route(s % 2)
        if stage == 0:
            return rcopy(
                aw.at[s, rows((1 - c) * 4 * piece, 4 * piece), :],
                rc_a.at[q],
                ca_s.at[q],
                ca_r.at[q],
                dev_c,
            )
        if stage == 1:
            return rcopy(
                aw.at[s, rows((c * 4 + (1 - high) * 2) * piece, 2 * piece), :],
                r2_a.at[q],
                a2_s.at[q],
                a2_r.at[q],
                second,
            )
        if stage == 2:
            return rcopy(
                aw.at[s, rows((c * 4 + high * 2 + 1 - low) * piece, piece), :],
                r1_a.at[q],
                a1_s.at[q],
                a1_r.at[q],
                first,
            )
        return rcopy(
            aw.at[s, rows((c * 4 + high * 2 + low) * piece, piece), :],
            rz_a.at[q],
            az_s.at[q],
            az_r.at[q],
            (d, s),
        )

    def ra_step(stage, q):
        s = group_of(q)
        low, high, _, _ = route(s % 2)
        ra(stage, q).wait_recv()
        if stage == 0:
            add_rows(aw.at[s, rows(c * 4 * piece, 4 * piece), :], rc_a.at[q])
        elif stage == 1:
            add_rows(aw.at[s, rows((c * 4 + high * 2) * piece, 2 * piece), :], r2_a.at[q])
        else:
            add_rows(aw.at[s, rows((c * 4 + high * 2 + low) * piece, piece), :], r1_a.at[q])

    def own_half(it, carry):
        q = it - parts
        s, dq, dk, dv = att_group(it, 0)

        @pl.when(it + 1 < 2 * parts)
        def _():
            fetch(it + 1)

        dq = (uu[s, 0:share, qkvw : 4 * hw].astype(F32) + dq).astype(BF16)
        dd[:, 0:hw] = dq
        dd[:, hw : 2 * hw] = dk
        dd[:, 2 * hw : 3 * hw] = dv
        acc1[...] += nt(dd[:, 0:qkvw], aw[s, :, 0:qkvw])
        late[pl.ds(2 * s, 1), 0:hw] = jnp.sum(dq.astype(F32), axis=0, keepdims=True)
        late[pl.ds(2 * s + 1, 1), 0:hw] = late[pl.ds(2 * s + 1, 1), 0:hw] + jnp.sum(
            dv.astype(F32), axis=0, keepdims=True
        )
        aw[s, :, 0:qkvw] = (
            nn(xnt[:, 0:share], dd[:, 0:qkvw]) + nn(xnt[:, share:keys], uu[s, 0:share, 0:qkvw])
        ).astype(BF16)
        ra(0, q).start()
        reduce_tick(n_all - 1 + 3 * parts + q)

        @pl.when(q >= 1)
        def _():
            ra_step(0, q - 1)
            ra(1, q - 1).start()

        @pl.when(q >= 2)
        def _():
            ra_step(1, q - 2)
            ra(2, q - 2).start()

        @pl.when(q >= 3)
        def _():
            ra_step(2, q - 3)
            ra(3, q - 3).start()

        final_tick(2 * q)
        final_tick(2 * q + 1)
        return carry

    lax.fori_loop(parts, 2 * parts, own_half, 0)

    last = parts - 1
    ra_step(0, last)
    ra(1, last).start()
    ra_step(1, last - 1)
    ra(2, last - 1).start()
    ra_step(2, last - 2)
    ra(3, last - 2).start()

    own_grad = acc1[...]
    unit, scale_inv = unit_of(x_ref[...].astype(F32))
    late[8:9, :] = late[8:9, :] + jnp.sum(own_grad * unit, axis=0, keepdims=True)
    late[9:10, :] = late[9:10, :] + jnp.sum(own_grad, axis=0, keepdims=True)

    stages = (dev_c, (dx, t), (dy, t))

    def vec(which, stage):
        buf, rx = (early, e_rx) if which == 0 else (late, l_rx)
        return rcopy(buf, rx.at[stage], sm_s.at[which, stage], sm_r.at[which, stage], stages[stage])

    def vec_far(which, k):
        rz = e_rz if which == 0 else l_rz
        return rcopy(
            rz.at[t], rz.at[t], sm_s.at[which, 2 + k], sm_r.at[which, 3 + t], (d, far(k))
        )

    for stage in range(3):
        for which in range(2):
            vec(which, stage).start()
        if stage == 0:
            ra_step(1, last)
            ra(2, last).start()
            ra_step(2, last - 1)
            ra(3, last - 1).start()
        for which in range(2):
            buf, rx = (early, e_rx) if which == 0 else (late, l_rx)
            vec(which, stage).wait_recv()
            vec(which, stage).wait_send()
            buf[...] = buf[...] + rx[stage]
    for which in range(2):
        buf, rz = (early, e_rz) if which == 0 else (late, l_rz)
        rz[t] = buf[...]
        for k in range(1, parts):
            vec_far(which, k).start()

    ra_step(2, last)
    mine = rows(pos_own_a, piece)
    total = aw[t, mine, :].astype(F32)
    for q in range(parts - 1):
        rcopy(rz_a.at[q], rz_a.at[q], az_s.at[q], az_r.at[q], (d, t)).wait_recv()
        total = total + rz_a[q].astype(F32)
    done = uu.at[0]
    done[mine, :] = total.astype(BF16)

    def aa(stage):
        if stage == 0:
            view, dev = done.at[mine, :], first_a
        elif stage == 1:
            view, dev = done.at[rows((c * 4 + high_a * 2) * piece, 2 * piece), :], second_a
        else:
            view, dev = done.at[rows(c * 4 * piece, 4 * piece), :], dev_c
        return rcopy(view, view, aa_s.at[stage], aa_r.at[stage], dev)

    aa(0).start()
    for n in range(2 * parts, nblk + 3):
        final_tick(n)

    ng_copy.wait_recv()
    grad = own_grad + ngr[...].astype(F32)
    mid[...] = mid[...] + norm_back(grad, unit, scale_inv, gain1)
    xg_copy = pltpu.make_async_copy(mid, xg_ref, loc_sem.at[nblk])
    xg_copy.start()

    aa(0).wait_recv()
    aa(1).start()

    for which in range(2):
        rz = e_rz if which == 0 else l_rz
        for k in range(1, parts):
            s = far(k)
            rcopy(
                rz.at[s], rz.at[s], sm_s.at[which, 3], sm_r.at[which, 3 + s], (d, t)
            ).wait_recv()
    osm_ref[0:24, :] = ((e_rz[0] + e_rz[1]) + e_rz[2]) + e_rz[3]
    osm_ref[24:40, :] = ((l_rz[0] + l_rz[1]) + l_rz[2]) + l_rz[3]

    aa(1).wait_recv()
    aa(2).start()

    for k in range(1, parts):
        zb(k, 0).wait_send()
        zb(k, 1).wait_send()
        for which in range(2):
            vec_far(which, k).wait_send()
    x_copy.wait_send()
    ng_copy.wait_send()

    def drain_far(m, carry):
        rf(3, m + nblk).wait_send()
        return carry

    lax.fori_loop(0, n_far, drain_far, 0)

    def drain_all(r, carry):
        for stage in range(3):
            rf(stage, r).wait_send()
        return carry

    lax.fori_loop(0, n_all, drain_all, 0)

    def drain_own(j, carry):
        for stage in range(3):
            af(stage, j).wait_send()
        f_out(j).wait()
        return carry

    lax.fori_loop(0, nblk, drain_own, 0)

    for q in range(parts):
        for stage in range(3):
            ra(stage, q).wait_send()
        if q < parts - 1:
            ra(3, q).wait_send()
    aa(2).wait_recv()
    oa_copy = pltpu.make_async_copy(done, oa_ref, loc_sem.at[nblk + 1])
    oa_copy.start()
    oa_copy.wait()
    xg_copy.wait()
    for stage in range(3):
        aa(stage).wait_send()


def local(
    x_in,
    cotangent,
    lengths,
    bucket_ids,
    bucket_weights,
    ln1_gain,
    ln1_bias,
    w_qkv,
    qv_bias,
    w_out,
    b_out,
    ln2_gain,
    ln2_bias,
    w_up,
    b_up,
    w_down,
    b_down,
):
    share, width = x_in.shape
    hw = w_qkv.shape[2]
    heads = hw // HD
    parts = 4
    fw = w_up.shape[1]
    nblk = fw // BLK
    piece = width // GROUP
    keys = 2 * share
    n_all = parts * nblk
    n_far = n_all - nblk
    vm = pl.BlockSpec(memory_space=pltpu.VMEM)
    sm = pl.BlockSpec(memory_space=pltpu.SMEM)
    hbm = pl.BlockSpec(memory_space=pl.ANY)
    dma = pltpu.SemaphoreType.DMA
    scratch = [
        pltpu.VMEM((n_all + nblk, 2, width, BLK), BF16),
        pltpu.VMEM((parts, width, 4 * hw), BF16),
        pltpu.VMEM((SLOTS_C, 2, 4 * piece, BLK), BF16),
        pltpu.VMEM((n_all, 2, 2 * piece, BLK), BF16),
        pltpu.VMEM((n_all, 2, piece, BLK), BF16),
        pltpu.VMEM((n_far, 2, piece, BLK), BF16),
        pltpu.VMEM((parts, 4 * piece, 4 * hw), BF16),
        pltpu.VMEM((parts, 2 * piece, 4 * hw), BF16),
        pltpu.VMEM((parts, piece, 4 * hw), BF16),
        pltpu.VMEM((parts - 1, piece, 4 * hw), BF16),
        pltpu.VMEM((keys, width), BF16),
        pltpu.VMEM((share, width), BF16),
        pltpu.VMEM((parts, share, 256), BF16),
        pltpu.VMEM((parts, keys, 256), BF16),
        pltpu.VMEM((parts, keys, 256), BF16),
        pltpu.VMEM((parts, share, 256), BF16),
        pltpu.VMEM((parts, share, 256), BF16),
        pltpu.VMEM((share, 512), BF16),
        pltpu.VMEM((heads, share, share), BF16),
        pltpu.VMEM((share, width), F32),
        pltpu.VMEM((share, width), F32),
        pltpu.VMEM((share, width), F32),
        pltpu.VMEM((parts, width, width), BF16),
        pltpu.VMEM((share, width), BF16),
        pltpu.VMEM((width, share), BF16),
        pltpu.VMEM((width, keys), BF16),
        pltpu.VMEM((share, width), BF16),
        pltpu.VMEM((share, width), BF16),
        pltpu.VMEM((parts, 1, fw), F32),
        pltpu.VMEM((parts, 2, hw), F32),
        pltpu.VMEM((24, width), F32),
        pltpu.VMEM((16, width), F32),
        pltpu.VMEM((3, 24, width), F32),
        pltpu.VMEM((parts, 24, width), F32),
        pltpu.VMEM((3, 16, width), F32),
        pltpu.VMEM((parts, 16, width), F32),
        dma((2 * nblk + 1,)),
        dma((heads,)),
        dma((3,)),
        dma((parts,)),
        dma((2,)),
        dma((6,)),
        dma((2, parts)),
        dma((3, parts)),
        dma((3, parts)),
        dma((n_far,)),
        dma((n_all,)),
        dma((3, n_all)),
        dma((3, n_all)),
        dma((n_all,)),
        dma((n_all,)),
        dma((n_all,)),
        dma((n_all,)),
        dma((n_all,)),
        dma((n_all,)),
        dma((n_far,)),
        dma((n_far,)),
        dma((3, nblk)),
        dma((3, nblk)),
        dma((parts,)),
        dma((parts,)),
        dma((parts,)),
        dma((parts,)),
        dma((parts,)),
        dma((parts,)),
        dma((parts,)),
        dma((parts,)),
        dma((3,)),
        dma((3,)),
        dma((2, 7)),
        dma((2, 7)),
        dma((2,)),
        pltpu.SemaphoreType.REGULAR,
    ]
    layer_out, x_grad, of, oa, osm, _ = pl.pallas_call(
        kernel,
        out_shape=[
            jax.ShapeDtypeStruct((share, width), BF16),
            jax.ShapeDtypeStruct((share, width), F32),
            jax.ShapeDtypeStruct((nblk, 2, width, BLK), BF16),
            jax.ShapeDtypeStruct((width, 4 * hw), BF16),
            jax.ShapeDtypeStruct((40, width), F32),
            jax.ShapeDtypeStruct((parts * heads, 2, share, share), BF16),
        ],
        in_specs=[vm, hbm, sm, sm, sm, vm, vm, vm, vm, vm, vm, vm, vm, hbm, vm, hbm, vm],
        out_specs=[hbm, hbm, hbm, hbm, vm, hbm],
        scratch_shapes=scratch,
        compiler_params=pltpu.CompilerParams(
            collective_id=0, has_side_effects=True, vmem_limit_bytes=67043328
        ),
    )(
        x_in,
        cotangent,
        lengths,
        bucket_ids,
        bucket_weights,
        ln1_gain.reshape(1, -1),
        ln1_bias.reshape(1, -1),
        w_qkv,
        qv_bias,
        w_out,
        b_out.reshape(1, -1),
        ln2_gain.reshape(1, -1),
        ln2_bias.reshape(1, -1),
        w_up,
        b_up.reshape(1, -1),
        w_down,
        b_down.reshape(1, -1),
    )
    dp = lax.axis_size("dp")
    grads = (of, oa, osm)
    if dp > GROUP:
        groups = [[g + GROUP * i for i in range(dp // GROUP)] for g in range(GROUP)]
        grads = lax.psum(tuple(g.astype(F32) for g in grads), "dp", axis_index_groups=groups)
    of, oa, osm = grads
    t = lax.axis_index("tensor")
    of = of.astype(F32)
    oa = oa.astype(F32)
    grad_up = of[:, 0].transpose(1, 0, 2).reshape(width, fw)
    grad_down = of[:, 1].transpose(0, 2, 1).reshape(fw, width)
    grad_qkv = oa[:, : 3 * hw].reshape(width, 3, hw).transpose(1, 0, 2)
    grad_w_out = oa[:, 3 * hw :].T
    grad_up_bias = lax.dynamic_slice_in_dim(osm, 4 + t * nblk, nblk, 0)[:, :BLK].reshape(fw)
    grad_qv = lax.dynamic_slice_in_dim(osm, 24 + 2 * t, 2, 0)[:, :hw]
    return (
        layer_out,
        x_grad,
        osm[32],
        osm[33],
        grad_qkv,
        grad_qv,
        grad_w_out,
        osm[2],
        osm[0],
        osm[1],
        grad_up,
        grad_up_bias,
        grad_down,
        osm[3],
    )


def solution(mesh):
    return jax.shard_map(
        local,
        mesh=mesh,
        in_specs=(
            P(("dp", "tensor"), None),
            P(("dp", "tensor"), None),
            P("dp", None),
            P("dp"),
            P(),
            P(),
            P(),
            P(None, None, "tensor"),
            P(None, "tensor"),
            P("tensor", None),
            P(),
            P(),
            P(),
            P(None, "tensor"),
            P("tensor"),
            P("tensor", None),
            P(),
        ),
        out_specs=(
            P(("dp", "tensor"), None),
            P(("dp", "tensor"), None),
            P(),
            P(),
            P(None, None, "tensor"),
            P(None, "tensor"),
            P("tensor", None),
            P(),
            P(),
            P(),
            P(None, "tensor"),
            P("tensor"),
            P("tensor", None),
            P(),
        ),
        check_vma=False,
    )
```

time: 822 us -> 315 us (0.38)
  waiting for transfers between devices: 443 us -> 0 us
  Pallas kernels: 0 us -> 271 us
  matrix products: 198 us -> 0 us
  other arithmetic: 72 us -> 2.64 us
  blocking collectives: 43.9 us -> 0 us
  between operations: 15.3 us -> 1.34 us
  loops' own time: 12.4 us -> 0 us
  local copies, waits for them, and re-layouts: 28.6 us -> 37.7 us
    pallas_call x0 -> x1, Pallas kernels: none -> 271 us  [local(): pl.pallas_call(kernel, out_shape=[jax.ShapeDtypeStruct((share, width), BF...]
    dot_general x25 -> x0, matrix products: 194 us -> none  [the longest x4 29.1 us: window_scores(): jnp.einsum('qhd,khd->hqk', query_b, key_b, preferred_element_type=f32)]
    all_gather x4 -> x0, waiting for transfers between devices: 187 us -> none  [the longest x1 55 us: local(): normed_all = lax.all_gather(normed, 'tensor', axis=0, tiled=True)]
    reduce_scatter x4 -> x0, waiting for transfers between devices: 173 us -> none  [the longest x1 52.1 us: local(): lax.psum_scatter(jnp.dot(active, w_down, preferred_element_type=f32).asty...]
    psum x1 -> x0, waiting for transfers between devices: 83.2 us -> none  [local(): lax.psum((grad_qkv, grad_qv_bias, grad_w_out, grad_up, grad_up_bias, grad...]
    psum x2 -> x0, blocking collectives: 43.9 us -> none  [the longest x1 25.8 us: local(): lax.psum((grad_qkv, grad_qv_bias, grad_w_out, grad_up, grad_up_bias, grad...]
    convert_element_type x5 -> x2, other arithmetic: 34.6 us -> 2.64 us  [the longest x1 2.53 us: local(): of = of.astype(F32)]
    reduce_sum x13 -> x0, other arithmetic: 29.5 us -> none  [the longest x2 9.56 us: forward_window(): total = jnp.sum(expo, axis=-1, keepdims=True)]
  transfers between devices with their start and end apart: 9 -> 0, of which waited for: 9 -> 0; matrix products, arithmetic and copies ran while one was open for 9% -> 0% of each run, Pallas kernels for 0% -> 0%
where the time goes in v1:
time: 315 us; the launch traced here: 313 us
  Pallas kernels  271 us (86%)
  local copies, waits for them, and re-layouts  37.7 us (12%)
    pallas_call x1, Pallas kernels, local(): pl.pallas_call(kernel, out_shape=[jax.ShapeDtypeStruct((share, width), BF...  271 us
    unnamed x7, local copies, waits for them, and re-layouts  12.2 us

profile of v1, /device:TPU:0, one launch (start us, length us, event | category | flops | bytes accessed | tf_op | source)
XLA Modules:
  0.0 312.7 jit_solution(3885660067681908695)
XLA Ops:
  1.3 1.3 reshape.61.g1_ref
  2.6 1.3 reshape.62.s1_ref
  3.8 2.2 copy.34.wqkv_ref
  6.1 1.3 reshape.63.bout_ref
  7.3 1.3 reshape.64.g2_ref
  8.6 1.3 reshape.65.s2_ref
  9.9 1.3 reshape.66.bup_ref
  11.1 1.3 reshape.67.bdn_ref
  12.4 271.0 %shard_map.272 = (bf16[512,640]{1,0:T(8,128)(2,1)}, f32[512,640]{1,0:T(8,128)}, bf16[5,2,640,256]{3,2,1,0:T(8,128)(2,1)}, bf16[640,640]{1,0:T(8,128)(2,1)}, f32[...) custom-call(bf16[512,640]{1,0:T(8,128)(2,1)} %x_ref.1, bf16[512,640]{1,0:T(8,128)(2,1)} %cot_ref.1, s32[1,8]{1,0:T(1,128)} %len_ref.1, ...), custom_call_target="tpu_custom_call" | custom-call | tf_op jit(solution)/shard_map/pallas_call | solution.py:1106
  283.4 1.5 slice_reduce_fusion
  284.9 1.2 slice.48
  286.2 1.4 copy.35
  287.6 1.3 constant_dynamic-slice_fusion.1
  289.0 0.2 slice_bitcast_fusion.2
  289.3 1.0 copy.38
  290.2 2.5 convert_element_type.7
  292.8 2.1 slice_bitcast_fusion
  294.9 4.5 %copy.36 = f32[640,5,256]{0,2,1:T(8,128)} copy(f32[640,5,256]{2,0,1:T(8,128)} %get-tuple-element.59) | data formatting | bytes 6553600 | tf_op jit(solution)/shard_map/transpose | solution.py:1150
  299.4 4.6 %copy.39 = f32[640,1280]{1,0:T(8,128)} copy(f32[640,1280]{0,1:T(8,128)} %bitcast.15) | data formatting | bytes 6553600
  304.0 0.7 constant_dynamic-slice_fusion
  304.7 0.6 reshape.70
  305.3 2.9 copy.37
  308.2 2.0 copy.43
  310.2 2.5 copy.44
  (3 shorter events, 0.1 us)
Async XLA Ops:
  283.4 5.5 %copy-start = (bf16[640,640]{1,0:T(8,128)(2,1)S(1)}, bf16[640,640]{1,0:T(8,128)(2,1)}, u32[]{:S(2)}) copy-start(bf16[640,640]{1,0:T(8,128)(2,1)} %get-tuple-element.22) | copy-start | bytes 2457604

commit v2 on v1

--- a/solution.py
+++ b/solution.py
@@ -22,6 +22,7 @@
 SLOTS_C = 2
 G_LAG1 = 8
 G_LAG2 = 5
+LAG = 2
 
 
 def nn(a, b):
@@ -71,7 +72,8 @@
     bdn_ref,
     lo_ref,
     xg_ref,
-    of_ref,
+    ou_ref,
+    od_ref,
     oa_ref,
     osm_ref,
     ph_ref,
@@ -91,7 +93,8 @@
     kb,
     vb,
     mx,
-    dob,
+    dmx,
+    stat,
     dd,
     pst,
     mid,
@@ -100,7 +103,6 @@
     uu,
     ol,
     olt,
-    xnt,
     ngs,
     ngr,
     bupa,
@@ -150,7 +152,7 @@
     credit,
 ):
     share, width = x_ref.shape
-    hw = wqkv_ref.shape[2]
+    hw = wqkv_ref.shape[1]
     heads = hw // HD
     qkvw = 3 * hw
     parts = 4
@@ -200,16 +202,27 @@
             loc_sem.at[nblk + j],
         )
 
+    cot_load = pltpu.make_async_copy(cot_ref, ol, loc_sem.at[2 * nblk])
+
+    a_loads = [
+        pltpu.make_async_copy(
+            wqkv_ref.at[i], aw.at[t, pl.ds(i * hw, hw), :], loc_sem.at[2 * nblk + 1 + i]
+        )
+        for i in range(3)
+    ]
+    a_loads.append(
+        pltpu.make_async_copy(
+            wout_ref, aw.at[t, pl.ds(qkvw, hw), :], loc_sem.at[2 * nblk + 4]
+        )
+    )
+    for cp in a_loads:
+        cp.start()
     for j in range(nblk):
+        dn_load(j).start()
         up_load(j).start()
-        dn_load(j).start()
-    cot_load = pltpu.make_async_copy(cot_ref, ol, loc_sem.at[2 * nblk])
     cot_load.start()
-
-    aw[t, :, 0:hw] = wqkv_ref[0]
-    aw[t, :, hw : 2 * hw] = wqkv_ref[1]
-    aw[t, :, 2 * hw : 3 * hw] = wqkv_ref[2]
-    aw[t, :, 3 * hw : 4 * hw] = wout_ref[...].T
+    bupa[t] = bup_ref[...][None, :]
+    qvba[t] = qvb_ref[...]
 
     barrier = pltpu.get_barrier_semaphore()
     for dev in (dev_c, (dx, t), (dy, t), (d, far(1)), (d, far(2)), (d, far(3))):
@@ -229,32 +242,47 @@
         rcopy(view, view, za_s.at[0], za_r.at[s], (d, t)).wait_recv()
 
     def zb(k, which):
-        src = bup_ref if which == 0 else qvb_ref
         dst = (bupa if which == 0 else qvba).at[t]
-        return rcopy(src, dst, zb_s.at[2 * (k - 1) + which], zb_r.at[which, t], (d, far(parts - k)))
+        return rcopy(dst, dst, zb_s.at[2 * (k - 1) + which], zb_r.at[which, t], (d, far(parts - k)))
 
     def zb_wait(s, which):
-        src = bup_ref if which == 0 else qvb_ref
         dst = (bupa if which == 0 else qvba).at[s]
-        rcopy(src, dst, zb_s.at[0], zb_r.at[which, s], (d, t)).wait_recv()
+        rcopy(dst, dst, zb_s.at[0], zb_r.at[which, s], (d, t)).wait_recv()
 
     x_copy = rcopy(x_ref, xp, zx_sem.at[0], zx_sem.at[1], (d, tp))
 
+    for cp in a_loads:
+        cp.wait()
     for k in range(1, parts):
         za(k).start()
         zb(k, 1).start()
     x_copy.start()
     for k in range(1, parts):
         zb(k, 0).start()
-    bupa[t] = bup_ref[...]
-    qvba[t] = qvb_ref[...]
-
-    gain1 = g1_ref[...]
-    shift1 = s1_ref[...]
+
+    def ga(stage, s):
+        low, high, first, second = route(s % 2)
+        if stage == 0:
+            view, dev = aw.at[s, rows((c * 4 + high * 2 + low) * piece, piece), :], first
+        elif stage == 1:
+            view, dev = aw.at[s, rows((c * 4 + high * 2) * piece, 2 * piece), :], second
+        else:
+            view, dev = aw.at[s, rows(c * 4 * piece, 4 * piece), :], dev_c
+        return rcopy(view, view, ga_s.at[stage, s], ga_r.at[stage, s], dev)
+
+    def ga_step(stage, k):
+        s = far(k)
+        if stage == 0:
+            za_wait(s, s % 2)
+        else:
+            ga(stage - 1, s).wait_recv()
+        ga(stage, s).start()
+
+    gain1 = g1_ref[...][None, :]
+    shift1 = s1_ref[...][None, :]
     unit, _ = unit_of(x_ref[...].astype(F32))
-    normed = (unit * gain1 + shift1).astype(BF16)
-    xn[0:share, :] = normed
-    xnt[:, 0:share] = normed.T
+    xn[0:share, :] = (unit * gain1 + shift1).astype(BF16)
+    ga_step(0, 1)
 
     bucket = bid_ref[0]
     span = jnp.where(bucket == 0, BUCKET, jnp.where(bucket == 1, 2 * BUCKET, 4 * BUCKET))
@@ -290,6 +318,8 @@
     _, live1 = slot_info(t * share, (share, 128))
     row_weight = jnp.where(live1, weight, 0.0)[:, 0:1]
 
+    ga_step(0, 2)
+
     def zf(k, j):
         low, high, _, _ = route((t + j) % 2)
         view = fg.at[t * nblk + j, :, rows((c * 4 + high * 2 + low) * piece, piece), :]
@@ -305,52 +335,20 @@
         for j in range(nblk):
             zf(k, j).start()
 
-    def ga(stage, s):
-        low, high, first, second = route(s % 2)
-        if stage == 0:
-            view, dev = aw.at[s, rows((c * 4 + high * 2 + low) * piece, piece), :], first
-        elif stage == 1:
-            view, dev = aw.at[s, rows((c * 4 + high * 2) * piece, 2 * piece), :], second
-        else:
-            view, dev = aw.at[s, rows(c * 4 * piece, 4 * piece), :], dev_c
-        return rcopy(view, view, ga_s.at[stage, s], ga_r.at[stage, s], dev)
-
-    def project(s, base, own):
-        bias_q = qvba[s, 0:1, :]
-        bias_v = qvba[s, 1:2, :]
-        out = nn(xn[base : base + share, :], aw[s, :, 0:qkvw])
+    ga_step(1, 1)
+    ga_step(0, 3)
+
+    def project(s, half, own):
+        base = half * share
+        first = 0 if own else hw
+        out = nt(xn[base : base + share, :], aw[s, first:qkvw, :])
         if own:
-            qb[s, :, 0:hw] = ((out[:, 0:hw] + bias_q) * q_scale).astype(BF16)
-        kb[s, base : base + share, 0:hw] = out[:, hw : 2 * hw].astype(BF16)
-        vb[s, base : base + share, 0:hw] = (out[:, 2 * hw : 3 * hw] + bias_v).astype(BF16)
-
-    for k in range(1, parts):
-        s = far(k)
-        za_wait(s, s % 2)
-        ga(0, s).start()
-    project(t, 0, True)
-    for stage in (1, 2):
-        for k in range(1, parts):
-            s = far(k)
-            ga(stage - 1, s).wait_recv()
-            ga(stage, s).start()
-    for k in range(1, parts):
-        s = far(k)
-        zb_wait(s, 1)
-        ga(2, s).wait_recv()
-        project(s, 0, True)
-
-    x_copy.wait_recv()
-    unit, _ = unit_of(xp[...].astype(F32))
-    normed = (unit * gain1 + shift1).astype(BF16)
-    xn[share:keys, :] = normed
-    xnt[:, share:keys] = normed.T
-
-    def pair_project(k, carry):
-        project(far(k), share, False)
-        return carry
-
-    lax.fori_loop(0, parts, pair_project, 0)
+            qb[s, :, 0:hw] = ((out[:, 0:hw] + qvba[s, 0:1, :]) * q_scale).astype(BF16)
+        at = hw - first
+        kb[s, base : base + share, 0:hw] = out[:, at : at + hw].astype(BF16)
+        vb[s, base : base + share, 0:hw] = (
+            out[:, at + hw : at + 2 * hw] + qvba[s, 1:2, :]
+        ).astype(BF16)
 
     n_far = (parts - 1) * nblk
 
@@ -385,74 +383,136 @@
             zf_wait(n)
             gf(0, n).start()
 
-        @pl.when(within(n - 1, n_far))
-        def _():
-            gf(0, n - 1).wait_recv()
-            gf(1, n - 1).start()
-
-        @pl.when(within(n - 2, n_far))
-        def _():
-            gf(1, n - 2).wait_recv()
-            gf(2, n - 2).start()
-
-    def p_out(s, h, slot):
-        return (
-            pltpu.make_async_copy(
-                pst.at[2 * slot], ph_ref.at[s * heads + h, 0], ps_sem.at[2 * slot]
-            ),
-            pltpu.make_async_copy(
-                pst.at[2 * slot + 1], ph_ref.at[s * heads + h, 1], ps_sem.at[2 * slot + 1]
-            ),
-        )
-
-    def att_forward(k, carry):
-        s = far(k)
-        qg = qb[s]
-        kg = kb[s]
-        vg = vb[s]
-        lane_q = lanes((share, 2 * 128))
+        @pl.when(within(n - LAG, n_far))
+        def _():
+            gf(0, n - LAG).wait_recv()
+            gf(1, n - LAG).start()
+
+        @pl.when(within(n - 2 * LAG, n_far))
+        def _():
+            gf(1, n - 2 * LAG).wait_recv()
+            gf(2, n - 2 * LAG).start()
+
+    lane_w = lanes((share, 2 * 128))
+    lane_n = lanes((share, 128))
+
+    def head_lanes(h):
+        return (lane_w >= HD * h) & (lane_w < HD * (h + 1))
+
+    def spread(values, at):
         out = jnp.zeros((share, 2 * 128), F32)
         for h in range(heads):
-            head = (lane_q >= HD * h) & (lane_q < HD * (h + 1))
-            qm = jnp.where(head | (lane_q >= hw), qg, jnp.zeros_like(qg))
+            out = jnp.where(head_lanes(h), values[:, at + h : at + h + 1], out)
+        return out
+
+    def p_out(s, h, half, buf):
+        return pltpu.make_async_copy(
+            pst.at[buf, h], ph_ref.at[s * heads + h, half], ps_sem.at[buf, h]
+        )
+
+    def att_forward(k, half):
+        s = far(k)
+        base = half * share
+        buf = k % 2
+        if half == 1:
+            for h in range(heads):
+                p_out(s, h, half, buf).wait()
+        else:
+
+            @pl.when(k >= 2)
+            def _():
+                for h in range(heads):
+                    p_out(s, h, half, buf).wait()
+
+        qg = qb[s]
+        kg = kb[s, base : base + share]
+        vg = vb[s, base : base + share]
+        out = jnp.zeros((share, 2 * 128), F32)
+        tops = jnp.zeros((share, 128), F32)
+        sums = jnp.ones((share, 128), F32)
+        for h in range(heads):
+            head = head_lanes(h)
+            qm = jnp.where(head | (lane_w >= hw), qg, jnp.zeros_like(qg))
             scores = nt(qm, kg)
             top = jnp.max(scores, axis=1, keepdims=True)
             probs = jnp.exp2(scores - top).astype(BF16)
-            idx = k * heads + h
-            slot = idx % 2
-
-            @pl.when(idx >= 2)
-            def _():
-                for cp in p_out(s, h, slot):
-                    cp.wait()
-
-            pst[2 * slot] = probs[:, 0:share]
-            pst[2 * slot + 1] = probs[:, share:keys]
-            for cp in p_out(s, h, slot):
-                cp.start()
+            pst[buf, h] = probs
             mixed = nn(probs, vg)
-            inv_h = 1.0 / mixed[:, hw : hw + 1]
-            out = jnp.where(head, mixed * inv_h, out)
-            coarse = inv_h.astype(BF16).astype(F32)
-            out = jnp.where(lane_q == hw + 2 * h, coarse, out)
-            out = jnp.where(lane_q == hw + 2 * h + 1, inv_h - coarse, out)
-        mx[s] = out.astype(BF16)
-        gather_tick(2 * k)
-        gather_tick(2 * k + 1)
+            out = jnp.where(head, mixed, out)
+            tops = jnp.where(lane_n == h, top, tops)
+            sums = jnp.where(lane_n == h, mixed[:, hw : hw + 1], sums)
+        for h in range(heads):
+            p_out(s, h, half, buf).start()
+        log_sum = tops + jnp.log2(sums)
+        if half == 0:
+            mx[s] = (out * spread(1.0 / sums, 0)).astype(BF16)
+            stat[s] = jnp.where(lane_n < 8, tops, pltpu.roll(log_sum, 8, 1))
+        else:
+            before = stat[s]
+            log_before = pltpu.roll(before, 120, 1)
+            upper = jnp.maximum(log_sum, log_before)
+            lower = jnp.minimum(log_sum, log_before)
+            log_all = upper + jnp.log2(1.0 + jnp.exp2(lower - upper))
+            part0 = jnp.exp2(log_before - log_all)
+            part1 = jnp.exp2(log_sum - log_all) / sums
+            mx[s] = (mx[s].astype(F32) * spread(part0, 0) + out * spread(part1, 0)).astype(BF16)
+            stat[s] = jnp.where(
+                lane_n < 8,
+                jnp.exp2(before - log_all),
+                pltpu.roll(jnp.exp2(tops - log_all), 8, 1),
+            )
+
+    def own_keys(k, carry):
+        s = far(k)
+
+        @pl.when(k > 0)
+        def _():
+            zb_wait(s, 1)
+            ga(2, s).wait_recv()
+
+        project(s, 0, True)
+        att_forward(k, 0)
+
+        @pl.when(k == 0)
+        def _():
+            ga_step(2, 1)
+            ga_step(1, 2)
+
+        @pl.when(k == 1)
+        def _():
+            ga_step(2, 2)
+            ga_step(1, 3)
+
+        @pl.when(k == 2)
+        def _():
+            ga_step(2, 3)
+
         return carry
 
-    lax.fori_loop(0, parts, att_forward, 0)
-    for slot in range(2):
-        for cp in p_out(0, 0, slot):
-            cp.wait()
+    lax.fori_loop(0, parts, own_keys, 0)
+
+    x_copy.wait_recv()
+    unit, _ = unit_of(xp[...].astype(F32))
+    xn[share:keys, :] = (unit * gain1 + shift1).astype(BF16)
+
+    def pair_keys(k, carry):
+        project(far(k), 1, False)
+        att_forward(k, 1)
+        gather_tick(k)
+        return carry
+
+    lax.fori_loop(0, parts, pair_keys, 0)
+    for buf in range(2):
+        for h in range(heads):
+            p_out(0, h, 1, buf).wait()
 
     branch = jnp.zeros((share, width), F32)
     for s in range(parts):
-        branch = branch + nt(mx[s, :, 0:hw], aw[s, :, qkvw : 4 * hw])
-    middle = x_ref[...].astype(F32) + (branch + bout_ref[...])
+        branch = branch + nn(mx[s, :, 0:hw], aw[s, qkvw : 4 * hw, :])
+    middle = x_ref[...].astype(F32) + (branch + bout_ref[...][None, :])
     mid[...] = middle
     unit, _ = unit_of(middle)
-    normed = (unit * g2_ref[...] + s2_ref[...]).astype(BF16)
+    normed = (unit * g2_ref[...][None, :] + s2_ref[...][None, :]).astype(BF16)
     n2 = uu.at[0, 0:share, :]
     n2t = uu.at[1, :, 0:share]
     n2[...] = normed
@@ -569,28 +629,16 @@
         fg[t * nblk + j, :, mine, :] = total.astype(BF16)
         af(0, j).start()
 
-    def f_out(j):
-        return pltpu.make_async_copy(fg.at[t * nblk + j], of_ref.at[j], loc_sem.at[j])
-
-    def final_tick(n):
-        @pl.when(within(n, nblk))
-        def _():
-            f_final(n)
-
-        @pl.when(within(n - 1, nblk))
-        def _():
-            af(0, n - 1).wait_recv()
-            af(1, n - 1).start()
-
-        @pl.when(within(n - 2, nblk))
-        def _():
-            af(1, n - 2).wait_recv()
-            af(2, n - 2).start()
-
-        @pl.when(within(n - 3, nblk))
-        def _():
-            af(2, n - 3).wait_recv()
-            f_out(n - 3).start()
+    def f_out(j, which):
+        if which == 0:
+            return pltpu.make_async_copy(
+                fg.at[t * nblk + j, 0], ou_ref.at[:, pl.ds(j * BLK, BLK)], loc_sem.at[j]
+            )
+        return pltpu.make_async_copy(
+            ol.at[pl.ds((j % 2) * BLK, BLK), :],
+            od_ref.at[pl.ds(j * BLK, BLK), :],
+            loc_sem.at[nblk + 2 + j % 2],
+        )
 
     def reduce_tick(n):
         @pl.when(within(n, n_all))
@@ -648,21 +696,21 @@
             pl.semaphore_wait(credit, 1)
 
         rf(0, r).start()
-        gather_tick(2 * parts + r)
+        gather_tick(parts + r)
         reduce_tick(r - 1)
         return carry
 
     lax.fori_loop(0, n_all, ffn, 0)
 
     middle = mid[...]
-    ngs[...] = (middle + (acc0[...] + bdn_ref[...])).astype(BF16)
+    ngs[...] = (middle + (acc0[...] + bdn_ref[...][None, :])).astype(BF16)
     lo_copy = pltpu.make_async_copy(ngs, lo_ref, loc_sem.at[2 * nblk])
     lo_copy.start()
     unit, scale_inv = unit_of(middle)
     got = acc1[...]
     early[0:1, :] = jnp.sum(got * unit, axis=0, keepdims=True)
     early[1:2, :] = jnp.sum(got, axis=0, keepdims=True)
-    middle_part = norm_back(got, unit, scale_inv, g2_ref[...])
+    middle_part = norm_back(got, unit, scale_inv, g2_ref[...][None, :])
     reload = pltpu.make_async_copy(cot_ref, ol, loc_sem.at[0])
     reload.start()
     reload.wait()
@@ -671,9 +719,7 @@
     mid[...] = middle_grad
     branch_low = middle_grad.astype(BF16)
     early[2:3, :] = jnp.sum(branch_low.astype(F32), axis=0, keepdims=True)
-    branch_t = olt
     ol[...] = branch_low
-    branch_t[...] = branch_low.T
 
     for k in range(1, parts):
         za(k).wait_send()
@@ -683,84 +729,98 @@
 
     def out_back(k, carry):
         s = far(k)
-        mixed = mx[s]
-        mixed_grad = nn(ol[...], aw[s, :, qkvw : 4 * hw]).astype(BF16).astype(F32)
-        inv = mixed[:, 128:256].astype(F32)
-        prod = mixed_grad * mixed[:, 0:hw].astype(F32)
+        mixed = mx[s, :, 0:hw]
+        mixed_grad = nt(ol[...], aw[s, qkvw : 4 * hw, :]).astype(BF16)
+        dmx[s, :, 0:hw] = mixed_grad
+        prod = mixed_grad.astype(F32) * mixed.astype(F32)
         lane_h = lanes((share, hw))
-        lane_q = lanes((share, 2 * 128))
-        scaled = jnp.zeros((share, hw), F32)
-        aux = jnp.zeros((share, 2 * 128), F32)
+        known = stat[s]
         for h in range(heads):
             head = (lane_h >= HD * h) & (lane_h < HD * (h + 1))
-            at = hw - 128 + 2 * h
-            inv_h = inv[:, at : at + 1] + inv[:, at + 1 : at + 2]
-            scaled = jnp.where(head, mixed_grad * inv_h, scaled)
-            delta = -jnp.sum(jnp.where(head, prod, 0.0), axis=1, keepdims=True) * inv_h
-            coarse = delta.astype(BF16).astype(F32)
-            aux = jnp.where(lane_q == hw + 2 * h, coarse, aux)
-            aux = jnp.where(lane_q == hw + 2 * h + 1, delta - coarse, aux)
-        dob[s] = aux.astype(BF16)
-        dob[s, :, 0:hw] = scaled.astype(BF16)
-        aw[s, :, qkvw : 4 * hw] = nn(branch_t[...], mixed[:, 0:hw]).astype(BF16)
+            delta = jnp.sum(jnp.where(head, prod, 0.0), axis=1, keepdims=True)
+            known = jnp.where(lane_n == 16 + h, delta, known)
+        stat[s] = known
+        aw[s, qkvw : 4 * hw, :] = nn(mixed.T, ol[...]).astype(BF16)
         reduce_tick(n_all - 1 + k)
         return carry
 
     lax.fori_loop(0, parts, out_back, 0)
 
-    def p_in(s, h, half):
-        return pltpu.make_async_copy(ph_ref.at[s * heads + h, half], pst.at[h], ps_sem.at[h])
+    def p_in(s, h, half, buf):
+        return pltpu.make_async_copy(
+            ph_ref.at[s * heads + h, half], pst.at[buf, h], ps_sem.at[buf, h]
+        )
 
     def group_of(it):
         return (t + 1 + it % parts) % parts
 
     def fetch(it):
         for h in range(heads):
-            p_in(group_of(it), h, 1 - it // parts).start()
+            p_in(group_of(it), h, 1 - it // parts, it % 2).start()
 
     def att_group(it, half):
         s = group_of(it)
         base = half * share
+        buf = it % 2
+
+        @pl.when(it + 1 < 2 * parts)
+        def _():
+            fetch(it + 1)
+
+        for h in range(heads):
+            p_in(s, h, half, buf).wait()
+        known = stat[s]
+        wanted = known if half == 0 else pltpu.roll(known, 120, 1)
+        delta = -(pltpu.roll(known, 112, 1) * wanted)
+        coarse = delta.astype(BF16).astype(F32)
+        fine = delta - coarse
+        scaled = dmx[s].astype(F32) * spread(wanted, 0)
+        for h in range(heads):
+            scaled = jnp.where(lane_w == hw + 2 * h, coarse[:, h : h + 1], scaled)
+            scaled = jnp.where(lane_w == hw + 2 * h + 1, fine[:, h : h + 1], scaled)
+        dg = jnp.where(lane_w < hw + 2 * heads, scaled, 0.0).astype(BF16)
         qg = qb[s]
-        dg = dob[s]
         kg = kb[s, base : base + share]
         vg = vb[s, base : base + share]
         qt = qg[:, 0:hw].T
         dt = dg[:, 0:hw].T
-        lane_q = lanes((share, 2 * 128))
         dq = jnp.zeros((share, 2 * 128), F32)
         dks = []
         dvs = []
         for h in range(heads):
-            head = (lane_q >= HD * h) & (lane_q < HD * (h + 1))
-            aux = (lane_q >= hw + 2 * h) & (lane_q < hw + 2 * h + 2)
+            head = head_lanes(h)
+            aux = (lane_w >= hw + 2 * h) & (lane_w < hw + 2 * h + 2)
             dm = jnp.where(head | aux, dg, jnp.zeros_like(dg))
             prob_grad = nt(dm, vg)
-            p_in(s, h, half).wait()
-            probs = pst[h]
+            probs = pst[buf, h]
             score_grad = (probs.astype(F32) * prob_grad).astype(BF16)
             dq = jnp.where(head, nn(score_grad, kg), dq)
             dks.append(nn(qt[HD * h : HD * (h + 1)], score_grad))
             dvs.append(nn(dt[HD * h : HD * (h + 1)], probs))
-        dk = (jnp.concatenate(dks, axis=0) * math.log(2.0)).astype(BF16)
-        dv = jnp.concatenate(dvs, axis=0).astype(BF16)
-        return s, dq[:, 0:hw] * factor, dk.T, dv.T
+        dqt = (dq[:, 0:hw] * factor).T
+        dkt = (jnp.concatenate(dks, axis=0) * math.log(2.0)).astype(BF16)
+        dvt = jnp.concatenate(dvs, axis=0).astype(BF16)
+        return s, dqt, dkt, dvt
 
     acc0[...] = jnp.zeros_like(acc0)
     acc1[...] = jnp.zeros_like(acc1)
+    dmx_pad = jnp.zeros((share, 2 * 128 - hw), BF16)
+    for s in range(parts):
+        dmx[s, :, hw : 2 * 128] = dmx_pad
     fetch(0)
 
+    def row_sums(values):
+        return jnp.sum(values.astype(F32), axis=0, keepdims=True)
+
     def pair_half(it, carry):
-        s, dq, dk, dv = att_group(it, 1)
-        fetch(it + 1)
-        uu[s, 0:share, qkvw : 4 * hw] = dq.astype(BF16)
-        uu[s, 0:share, 0:hw] = jnp.zeros((share, hw), BF16)
-        uu[s, 0:share, hw : 2 * hw] = dk
-        uu[s, 0:share, 2 * hw : 3 * hw] = dv
-        acc0[...] += nt(uu[s, 0:share, 0:qkvw], aw[s, :, 0:qkvw])
-        late[pl.ds(2 * s + 1, 1), 0:hw] = jnp.sum(dv.astype(F32), axis=0, keepdims=True)
-        reduce_tick(n_all - 1 + parts + 2 * it)
-        reduce_tick(n_all - 1 + parts + 2 * it + 1)
+        s, dqt, dkt, dvt = att_group(it, 1)
+        uu[s, 0:hw, 0:share] = dqt.astype(BF16)
+        uu[s, hw : 2 * hw, 0:share] = dkt
+        uu[s, 2 * hw : qkvw, 0:share] = dvt
+        back = uu[s, hw:qkvw, 0:share].T
+        acc0[...] += nn(back, aw[s, hw:qkvw, :])
+        late[pl.ds(2 * s + 1, 1), 0:hw] = row_sums(back[:, hw : 2 * hw])
+        reduce_tick(n_all - 1 + parts + it)
         return carry
 
     lax.fori_loop(0, parts, pair_half, 0)
@@ -820,28 +880,52 @@
         else:
             add_rows(aw.at[s, rows((c * 4 + high * 2 + low) * piece, piece), :], r1_a.at[q])
 
+    stages = (dev_c, (dx, t), (dy, t))
+
+    def vec(which, stage):
+        buf, rx = (early, e_rx) if which == 0 else (late, l_rx)
+        return rcopy(buf, rx.at[stage], sm_s.at[which, stage], sm_r.at[which, stage], stages[stage])
+
+    def vec_far(which, k):
+        rz = e_rz if which == 0 else l_rz
+        return rcopy(
+            rz.at[t], rz.at[t], sm_s.at[which, 2 + k], sm_r.at[which, 3 + t], (d, far(k))
+        )
+
+    def vec_next(which, stage):
+        buf, rx = (early, e_rx) if which == 0 else (late, l_rx)
+        vec(which, stage).wait_recv()
+        vec(which, stage).wait_send()
+        buf[...] = buf[...] + rx[stage]
+        if stage < 2:
+            vec(which, stage + 1).start()
+        else:
+            rz = e_rz if which == 0 else l_rz
+            rz[t] = buf[...]
+            for k in range(1, parts):
+                vec_far(which, k).start()
+
+    vec(0, 0).start()
+
     def own_half(it, carry):
         q = it - parts
-        s, dq, dk, dv = att_group(it, 0)
-
-        @pl.when(it + 1 < 2 * parts)
-        def _():
-            fetch(it + 1)
-
-        dq = (uu[s, 0:share, qkvw : 4 * hw].astype(F32) + dq).astype(BF16)
-        dd[:, 0:hw] = dq
-        dd[:, hw : 2 * hw] = dk
-        dd[:, 2 * hw : 3 * hw] = dv
-        acc1[...] += nt(dd[:, 0:qkvw], aw[s, :, 0:qkvw])
-        late[pl.ds(2 * s, 1), 0:hw] = jnp.sum(dq.astype(F32), axis=0, keepdims=True)
-        late[pl.ds(2 * s + 1, 1), 0:hw] = late[pl.ds(2 * s + 1, 1), 0:hw] + jnp.sum(
-            dv.astype(F32), axis=0, keepdims=True
+        s, dqt, dkt, dvt = att_group(it, 0)
+        dqt = (uu[s, 0:hw, 0:share].astype(F32) + dqt).astype(BF16)
+        dd[0:hw, :] = dqt
+        dd[hw : 2 * hw, :] = dkt
+        dd[2 * hw : qkvw, :] = dvt
+        back = dd[...].T
+        acc1[...] += nn(back, aw[s, 0:qkvw, :])
+        late[pl.ds(2 * s, 1), 0:hw] = row_sums(back[:, 0:hw])
+        late[pl.ds(2 * s + 1, 1), 0:hw] = late[pl.ds(2 * s + 1, 1), 0:hw] + row_sums(
+            back[:, 2 * hw : qkvw]
         )
-        aw[s, :, 0:qkvw] = (
-            nn(xnt[:, 0:share], dd[:, 0:qkvw]) + nn(xnt[:, share:keys], uu[s, 0:share, 0:qkvw])
+        aw[s, 0:hw, :] = nn(dqt, xn[0:share, :]).astype(BF16)
+        aw[s, hw:qkvw, :] = (
+            nn(dd[hw:qkvw, :], xn[0:share, :]) + nn(uu[s, hw:qkvw, 0:share], xn[share:keys, :])
         ).astype(BF16)
         ra(0, q).start()
-        reduce_tick(n_all - 1 + 3 * parts + q)
+        reduce_tick(n_all - 1 + 2 * parts + q)
 
         @pl.when(q >= 1)
         def _():
@@ -858,8 +942,12 @@
             ra_step(2, q - 3)
             ra(3, q - 3).start()
 
-        final_tick(2 * q)
-        final_tick(2 * q + 1)
+        for stage in range(3):
+
+            @pl.when(q == stage)
+            def _():
+                vec_next(0, stage)
+
         return carry
 
     lax.fori_loop(parts, 2 * parts, own_half, 0)
@@ -871,42 +959,37 @@
     ra(2, last - 1).start()
     ra_step(2, last - 2)
     ra(3, last - 2).start()
+    for n in range(n_all - 1 + 3 * parts, n_all + G_LAG1 + G_LAG2):
+        reduce_tick(n)
 
     own_grad = acc1[...]
     unit, scale_inv = unit_of(x_ref[...].astype(F32))
     late[8:9, :] = late[8:9, :] + jnp.sum(own_grad * unit, axis=0, keepdims=True)
     late[9:10, :] = late[9:10, :] + jnp.sum(own_grad, axis=0, keepdims=True)
-
-    stages = (dev_c, (dx, t), (dy, t))
-
-    def vec(which, stage):
-        buf, rx = (early, e_rx) if which == 0 else (late, l_rx)
-        return rcopy(buf, rx.at[stage], sm_s.at[which, stage], sm_r.at[which, stage], stages[stage])
-
-    def vec_far(which, k):
-        rz = e_rz if which == 0 else l_rz
-        return rcopy(
-            rz.at[t], rz.at[t], sm_s.at[which, 2 + k], sm_r.at[which, 3 + t], (d, far(k))
-        )
-
-    for stage in range(3):
-        for which in range(2):
-            vec(which, stage).start()
-        if stage == 0:
-            ra_step(1, last)
-            ra(2, last).start()
-            ra_step(2, last - 1)
-            ra(3, last - 1).start()
-        for which in range(2):
-            buf, rx = (early, e_rx) if which == 0 else (late, l_rx)
-            vec(which, stage).wait_recv()
-            vec(which, stage).wait_send()
-            buf[...] = buf[...] + rx[stage]
-    for which in range(2):
-        buf, rz = (early, e_rz) if which == 0 else (late, l_rz)
-        rz[t] = buf[...]
-        for k in range(1, parts):
-            vec_far(which, k).start()
+    vec(1, 0).start()
+    f_final(0)
+    vec_next(1, 0)
+    f_final(1)
+    ra_step(1, last)
+    ra(2, last).start()
+    vec_next(1, 1)
+    f_final(2)
+    f_final(3)
+    ra_step(2, last - 1)
+    ra(3, last - 1).start()
+    vec_next(1, 2)
+    f_final(4)
+
+    def f_second(j):
+        af(0, j).wait_recv()
+        af(1, j).start()
+
+    def f_third(j):
+        af(1, j).wait_recv()
+        af(2, j).start()
+
+    for j in range(nblk):
+        f_second(j)
 
     ra_step(2, last)
     mine = rows(pos_own_a, piece)
@@ -927,8 +1010,6 @@
         return rcopy(view, view, aa_s.at[stage], aa_r.at[stage], dev)
 
     aa(0).start()
-    for n in range(2 * parts, nblk + 3):
-        final_tick(n)
 
     ng_copy.wait_recv()
     grad = own_grad + ngr[...].astype(F32)
@@ -936,8 +1017,18 @@
     xg_copy = pltpu.make_async_copy(mid, xg_ref, loc_sem.at[nblk])
     xg_copy.start()
 
+    for j in range(nblk):
+        f_third(j)
     aa(0).wait_recv()
     aa(1).start()
+
+    for j in range(nblk):
+        af(2, j).wait_recv()
+        f_out(j, 0).start()
+        if j >= 2:
+            f_out(j - 2, 1).wait()
+        ol[(j % 2) * BLK : (j % 2 + 1) * BLK, :] = fg[t * nblk + j, 1].T
+        f_out(j, 1).start()
 
     for which in range(2):
         rz = e_rz if which == 0 else l_rz
@@ -946,8 +1037,14 @@
             rcopy(
                 rz.at[s], rz.at[s], sm_s.at[which, 3], sm_r.at[which, 3 + s], (d, t)
             ).wait_recv()
-    osm_ref[0:24, :] = ((e_rz[0] + e_rz[1]) + e_rz[2]) + e_rz[3]
-    osm_ref[24:40, :] = ((l_rz[0] + l_rz[1]) + l_rz[2]) + l_rz[3]
+    early[...] = ((e_rz[0] + e_rz[1]) + e_rz[2]) + e_rz[3]
+    late[...] = ((l_rz[0] + l_rz[1]) + l_rz[2]) + l_rz[3]
+    osm_ref[0:4, :] = early[0:4, :]
+    osm_ref[4:6, :] = late[8:10, :]
+    osm_ref[8:9, :] = late[pl.ds(2 * t, 1), :]
+    osm_ref[9:10, :] = late[pl.ds(2 * t + 1, 1), :]
+    for j in range(nblk):
+        osm_ref[16 + j : 17 + j, :] = early[pl.ds(4 + t * nblk + j, 1), :]
 
     aa(1).wait_recv()
     aa(2).start()
@@ -976,10 +1073,13 @@
     def drain_own(j, carry):
         for stage in range(3):
             af(stage, j).wait_send()
-        f_out(j).wait()
         return carry
 
     lax.fori_loop(0, nblk, drain_own, 0)
+    for j in range(nblk):
+        f_out(j, 0).wait()
+    for j in range(nblk - 2, nblk):
+        f_out(j, 1).wait()
 
     for q in range(parts):
         for stage in range(3):
@@ -993,6 +1093,75 @@
     xg_copy.wait()
     for stage in range(3):
         aa(stage).wait_send()
+
+
+def finish(
+    lo,
+    xg,
+    up,
+    dn,
+    at,
+    sm,
+    lo_out,
+    xg_out,
+    up_out,
+    dn_out,
+    qkv_out,
+    out_out,
+    g2_out,
+    s2_out,
+    bo_out,
+    bd_out,
+    g1_out,
+    s1_out,
+    qv_out,
+    bup_out,
+    lo_b,
+    xg_b,
+    up_b,
+    dn_b,
+    at_b,
+    up_f,
+    dn_f,
+    at_f,
+    in_sem,
+    out_sem,
+):
+    hw = out_out.shape[0]
+    qkvw = qkv_out.shape[0]
+    ins = [
+        pltpu.make_async_copy(src, dst, in_sem.at[i])
+        for i, (src, dst) in enumerate(((up, up_b), (dn, dn_b), (at, at_b), (xg, xg_b), (lo, lo_b)))
+    ]
+    for cp in ins:
+        cp.start()
+    outs = []
+
+    def send(src, dst):
+        outs.append(pltpu.make_async_copy(src, dst, out_sem.at[len(outs)]))
+        outs[-1].start()
+
+    for i, ref in enumerate((g2_out, s2_out, bo_out, bd_out, g1_out, s1_out)):
+        ref[...] = sm[i]
+    qv_out[...] = sm[8:10, 0:hw]
+    for j in range(bup_out.shape[0] // BLK):
+        bup_out[j * BLK : (j + 1) * BLK] = sm[16 + j, 0:BLK]
+    ins[0].wait()
+    up_f[...] = up_b[...].astype(F32)
+    send(up_f, up_out)
+    ins[1].wait()
+    dn_f[...] = dn_b[...].astype(F32)
+    send(dn_f, dn_out)
+    ins[2].wait()
+    at_f[...] = at_b[...].astype(F32)
+    send(at_f.at[pl.ds(0, qkvw), :], qkv_out)
+    send(at_f.at[pl.ds(qkvw, hw), :], out_out)
+    ins[3].wait()
+    send(xg_b, xg_out)
+    ins[4].wait()
+    send(lo_b, lo_out)
+    for cp in outs:
+        cp.wait()
 
 
 def local(
@@ -1046,15 +1215,15 @@
         pltpu.VMEM((parts, keys, 256), BF16),
         pltpu.VMEM((parts, share, 256), BF16),
         pltpu.VMEM((parts, share, 256), BF16),
-        pltpu.VMEM((share, 512), BF16),
-        pltpu.VMEM((heads, share, share), BF16),
+        pltpu.VMEM((parts, share, 128), F32),
+        pltpu.VMEM((3 * hw, share), BF16),
+        pltpu.VMEM((2, heads, share, share), BF16),
         pltpu.VMEM((share, width), F32),
         pltpu.VMEM((share, width), F32),
         pltpu.VMEM((share, width), F32),
         pltpu.VMEM((parts, width, width), BF16),
         pltpu.VMEM((share, width), BF16),
         pltpu.VMEM((width, share), BF16),
-        pltpu.VMEM((width, keys), BF16),
         pltpu.VMEM((share, width), BF16),
         pltpu.VMEM((share, width), BF16),
         pltpu.VMEM((parts, 1, fw), F32),
@@ -1065,8 +1234,8 @@
         pltpu.VMEM((parts, 24, width), F32),
         pltpu.VMEM((3, 16, width), F32),
         pltpu.VMEM((parts, 16, width), F32),
-        dma((2 * nblk + 1,)),
-        dma((heads,)),
+        dma((2 * nblk + 5,)),
+        dma((2, heads)),
         dma((3,)),
         dma((parts,)),
         dma((2,)),
@@ -1103,18 +1272,19 @@
         dma((2,)),
         pltpu.SemaphoreType.REGULAR,
     ]
-    layer_out, x_grad, of, oa, osm, _ = pl.pallas_call(
+    layer_out, x_grad, up, down, att, small, _ = pl.pallas_call(
         kernel,
         out_shape=[
             jax.ShapeDtypeStruct((share, width), BF16),
             jax.ShapeDtypeStruct((share, width), F32),
-            jax.ShapeDtypeStruct((nblk, 2, width, BLK), BF16),
-            jax.ShapeDtypeStruct((width, 4 * hw), BF16),
-            jax.ShapeDtypeStruct((40, width), F32),
+            jax.ShapeDtypeStruct((width, fw), BF16),
+            jax.ShapeDtypeStruct((fw, width), BF16),
+            jax.ShapeDtypeStruct((width, width), BF16),
+            jax.ShapeDtypeStruct((24, width), F32),
             jax.ShapeDtypeStruct((parts * heads, 2, share, share), BF16),
         ],
-        in_specs=[vm, hbm, sm, sm, sm, vm, vm, vm, vm, vm, vm, vm, vm, hbm, vm, hbm, vm],
-        out_specs=[hbm, hbm, hbm, hbm, vm, hbm],
+        in_specs=[vm, hbm, sm, sm, sm, vm, vm, hbm, vm, hbm, vm, vm, vm, hbm, vm, hbm, vm],
+        out_specs=[hbm, hbm, hbm, hbm, hbm, vm, hbm],
         scratch_shapes=scratch,
         compiler_params=pltpu.CompilerParams(
             collective_id=0, has_side_effects=True, vmem_limit_bytes=67043328
@@ -1125,49 +1295,77 @@
         lengths,
         bucket_ids,
         bucket_weights,
-        ln1_gain.reshape(1, -1),
-        ln1_bias.reshape(1, -1),
-        w_qkv,
+        ln1_gain,
+        ln1_bias,
+        w_qkv.transpose(0, 2, 1),
         qv_bias,
         w_out,
-        b_out.reshape(1, -1),
-        ln2_gain.reshape(1, -1),
-        ln2_bias.reshape(1, -1),
+        b_out,
+        ln2_gain,
+        ln2_bias,
         w_up,
-        b_up.reshape(1, -1),
+        b_up,
         w_down,
-        b_down.reshape(1, -1),
+        b_down,
     )
     dp = lax.axis_size("dp")
-    grads = (of, oa, osm)
     if dp > GROUP:
         groups = [[g + GROUP * i for i in range(dp // GROUP)] for g in range(GROUP)]
-        grads = lax.psum(tuple(g.astype(F32) for g in grads), "dp", axis_index_groups=groups)
-    of, oa, osm = grads
-    t = lax.axis_index("tensor")
-    of = of.astype(F32)
-    oa = oa.astype(F32)
-    grad_up = of[:, 0].transpose(1, 0, 2).reshape(width, fw)
-    grad_down = of[:, 1].transpose(0, 2, 1).reshape(fw, width)
-    grad_qkv = oa[:, : 3 * hw].reshape(width, 3, hw).transpose(1, 0, 2)
-    grad_w_out = oa[:, 3 * hw :].T
-    grad_up_bias = lax.dynamic_slice_in_dim(osm, 4 + t * nblk, nblk, 0)[:, :BLK].reshape(fw)
-    grad_qv = lax.dynamic_slice_in_dim(osm, 24 + 2 * t, 2, 0)[:, :hw]
+        sums = lax.psum(
+            tuple(g.astype(F32) for g in (up, down, att, small)), "dp", axis_index_groups=groups
+        )
+        up, down, att = (g.astype(BF16) for g in sums[:3])
+        small = sums[3]
+    flat = jax.ShapeDtypeStruct((width,), F32)
+    outs = pl.pallas_call(
+        finish,
+        out_shape=[
+            jax.ShapeDtypeStruct((share, width), BF16),
+            jax.ShapeDtypeStruct((share, width), F32),
+            jax.ShapeDtypeStruct((width, fw), F32),
+            jax.ShapeDtypeStruct((fw, width), F32),
+            jax.ShapeDtypeStruct((3 * hw, width), F32),
+            jax.ShapeDtypeStruct((hw, width), F32),
+            flat,
+            flat,
+            flat,
+            flat,
+            flat,
+            flat,
+            jax.ShapeDtypeStruct((2, hw), F32),
+            jax.ShapeDtypeStruct((fw,), F32),
+        ],
+        in_specs=[hbm] * 5 + [vm],
+        out_specs=[hbm] * 6 + [vm] * 8,
+        scratch_shapes=[
+            pltpu.VMEM((share, width), BF16),
+            pltpu.VMEM((share, width), F32),
+            pltpu.VMEM((width, fw), BF16),
+            pltpu.VMEM((fw, width), BF16),
+            pltpu.VMEM((width, width), BF16),
+            pltpu.VMEM((width, fw), F32),
+            pltpu.VMEM((fw, width), F32),
+            pltpu.VMEM((width, width), F32),
+            dma((5,)),
+            dma((7,)),
+        ],
+    )(layer_out, x_grad, up, down, att, small)
+    layer_out, x_grad, g_up, g_down, g_qkv, g_out, g2, s2, bo, bd, g1, s1, g_qv, g_bup = outs
     return (
         layer_out,
         x_grad,
-        osm[32],
-        osm[33],
-        grad_qkv,
-        grad_qv,
-        grad_w_out,
-        osm[2],
-        osm[0],
-        osm[1],
-        grad_up,
-        grad_up_bias,
-        grad_down,
-        osm[3],
+        g1,
+        s1,
+        g_qkv.reshape(3, hw, width).transpose(0, 2, 1),
+        g_qv,
+        g_out,
+        bo,
+        g2,
+        s2,
+        g_up,
+        g_bup,
+        g_down,
+        bd,
     )
 
 

time: 315 us -> 234 us (0.74)
  Pallas kernels: 271 us -> 232 us
  local copies, waits for them, and re-layouts: 37.7 us -> 0 us
    pallas_call x1, Pallas kernels: 271 us -> 224 us  [local(): pl.pallas_call(kernel, out_shape=[jax.ShapeDtypeStruct((share, width), BF...]
    unnamed x7 -> x0, local copies, waits for them, and re-layouts: 12.2 us -> none
    transpose x4 -> x0, local copies, waits for them, and re-layouts: 9.82 us -> none  [the longest x2 5.04 us: local(): grad_down = of[:, 1].transpose(0, 2, 1).reshape(fw, width)]
    reshape x8 -> x0, local copies, waits for them, and re-layouts: 9.49 us -> none  [the longest x1 1.29 us: local(): b_up.reshape(1, -1)]
    pallas_call x0 -> x1, Pallas kernels: none -> 7.09 us  [local(): pl.pallas_call(finish, out_shape=[jax.ShapeDtypeStruct((share, width), BF...]
    slice x5 -> x0, local copies, waits for them, and re-layouts: 6.22 us -> none  [the longest x2 2.68 us: local(): grad_qkv = oa[:, :3 * hw].reshape(width, 3, hw).transpose(1, 0, 2)]
where the time goes in v2:
time: 234 us; the launch traced here: 233 us
  Pallas kernels  232 us (99%)
    pallas_call x1, Pallas kernels, local(): pl.pallas_call(kernel, out_shape=[jax.ShapeDtypeStruct((share, width), BF...  224 us
    pallas_call x1, Pallas kernels, local(): pl.pallas_call(finish, out_shape=[jax.ShapeDtypeStruct((share, width), BF...  7.09 us

profile of v2, /device:TPU:0, one launch (start us, length us, event | category | flops | bytes accessed | tf_op | source)
XLA Modules:
  0.0 233.0 jit_solution(6823479215334903803)
XLA Ops:
  1.3 224.5 %shard_map.272 = (bf16[512,640]{1,0:T(8,128)(2,1)}, f32[512,640]{1,0:T(8,128)}, bf16[640,1280]{1,0:T(8,128)(2,1)}, bf16[1280,640]{1,0:T(8,128)(2,1)}, bf16[640,6...) custom-call(bf16[512,640]{1,0:T(8,128)(2,1)} %x_ref.1, bf16[512,640]{1,0:T(8,128)(2,1)} %cot_ref.1, ...), custom_call_target="tpu_custom_call" | custom-call | tf_op jit(solution)/shard_map/pallas_call | solution.py:1275
  225.8 7.1 %shard_map.273 = (bf16[512,640]{1,0:T(8,128)(2,1)}, f32[512,640]{1,0:T(8,128)}, f32[640,1280]{1,0:T(8,128)}, f32[1280,640]{1,0:T(8,128)}, f32[480,640]{1,0:T(8,1...) custom-call(bf16[512,640]{1,0:T(8,128)(2,1)} %get-tuple-element.34.l, ...), custom_call_target="tpu_custom_call" | custom-call | tf_op jit(solution)/shard_map/pallas_call | solution.py:1320

commit v3 on v2

--- a/solution.py
+++ b/solution.py
@@ -20,9 +20,81 @@
 RSQRT2 = 1.0 / math.sqrt(2.0)
 RSQRT2PI = 1.0 / math.sqrt(2.0 * math.pi)
 SLOTS_C = 2
-G_LAG1 = 8
-G_LAG2 = 5
-LAG = 2
+X_PLACE = 4
+CUTS = ((0, 256), (256, 384))
+PLAN = {
+    "p0": (
+        ("a0", (0, 1)),
+        ("a1", (0, 1)),
+    ),
+    "p1": (
+        ("a2", (0, 1)),
+    ),
+    "p2": (
+        ("a0", (1, 3)),
+    ),
+    "pj": (
+        ("a1", (1, 3)),
+        ("a2", (1, 3)),
+    ),
+    "o": (
+        ("g0", (0, 0, 0, 1, 2)),
+    ),
+    "q": (
+        ("g0", (2, 8, 10, 15, 15)),
+        ("g1", (0, 2, 4, 6, 10)),
+        ("g2", (0, 0, 0, 1, 3)),
+    ),
+    "mid": (
+        ("g1", (10, 11)),
+        ("g2", (3, 5)),
+    ),
+    "r": (
+        ("g1", (11, 12, 15, 15, 15, 15, 15, 15, 15, 15, 15, 15, 15, 15, 15, 15, 15, 15, 15, 15, 15)),
+        ("g2", (5, 5, 6, 8, 10, 10, 13, 15, 15, 15, 15, 15, 15, 15, 15, 15, 15, 15, 15, 15, 15)),
+        ("rf", (0, 0, 0, 0, 0, 0, 0, 0, 0, 0, 0, 0, 0, 2, 2, 2, 2, 2, 2, 3, 3)),
+        ("r1", (0, 0, 0, 0, 0, 0, 0, 0, 0, 0, 1, 2, 2, 2, 3, 3, 4, 4, 4, 6, 10)),
+        ("r2", (0, 0, 0, 0, 0, 0, 0, 1, 2, 3, 4, 4, 6, 6, 7, 8, 10, 10, 11, 11, 14)),
+    ),
+    "ln": (
+        ("rf", (3, 5)),
+    ),
+    "k": (
+        ("rf", (5, 5, 6, 6, 6)),
+        ("r1", (10, 10, 11, 11, 11)),
+        ("r2", (14, 15, 15, 17, 18)),
+    ),
+    "h": (
+        ("rf", (6, 9, 11, 11, 13)),
+        ("r1", (11, 11, 15, 15, 18)),
+        ("r2", (18, 18, 19, 19, 20)),
+    ),
+    "w": (
+        ("rf", (13, 18, 18, 19, 20)),
+        ("r1", (18, 19, 20, 20, 20)),
+        ("b3", (0, 0, 0, 0, 1)),
+        ("b2", (0, 0, 0, 1, 3)),
+        ("b1", (0, 0, 1, 3, 4)),
+        ("f0", (0, 3, 3, 4, 4)),
+        ("f1", (0, 0, 1, 2, 2)),
+        ("f2", (0, 0, 0, 0, 2)),
+    ),
+}
+TAIL = (
+    ("v", 0, 0),
+    ("b2", 3, 4),
+    ("b3", 1, 3),
+    ("f0", 4, 5),
+    ("f1", 2, 5),
+    ("b3", 3, 4),
+    ("aa0", 0, 0),
+    ("v", 0, 0),
+    ("ng", 0, 0),
+    ("v", 0, 0),
+    ("f2", 2, 5),
+    ("aa1", 0, 0),
+    ("aa2", 0, 0),
+)
 
 
 def nn(a, b):
@@ -136,14 +208,8 @@
     fz_r,
     af_s,
     af_r,
-    ca_s,
-    ca_r,
-    a2_s,
-    a2_r,
-    a1_s,
-    a1_r,
-    az_s,
-    az_r,
+    ra_s,
+    ra_r,
     aa_s,
     aa_r,
     sm_s,
@@ -173,7 +239,8 @@
     tp = t + 1 - 2 * (t % 2)
 
     def far(k):
-        return (t + k) % parts
+        low_t, high_t, low_k, high_k = t % 2, t // 2, k % 2, k // 2
+        return low_t + low_k - 2 * low_t * low_k + 2 * (high_t + high_k - 2 * high_t * high_k)
 
     def route(par):
         low = bx + par * (by - bx)
@@ -229,21 +296,28 @@
         pl.semaphore_signal(barrier, inc=1, device_id=dev, device_id_type=MESH)
     pl.semaphore_wait(barrier, 6)
 
-    low_a, high_a, first_a, second_a = route(t % 2)
-    pos_own_a = (c * 4 + high_a * 2 + low_a) * piece
-
-    def za(k):
-        view = aw.at[t, rows(pos_own_a, piece), :]
-        return rcopy(view, view, za_s.at[k - 1], za_r.at[t], (d, far(parts - k)))
-
-    def za_wait(s, par):
-        low, high, _, _ = route(par)
-        view = aw.at[s, rows((c * 4 + high * 2 + low) * piece, piece), :]
-        rcopy(view, view, za_s.at[0], za_r.at[s], (d, t)).wait_recv()
+    def a_rows(stage, s, a):
+        low, high, _, _ = route((s + a) % 2)
+        if stage == 0:
+            return rows((c * 4 + high * 2 + low) * piece, piece)
+        if stage == 1:
+            return rows((c * 4 + high * 2) * piece, 2 * piece)
+        return rows(c * 4 * piece, 4 * piece)
+
+    def a_lanes(a):
+        return pl.ds(CUTS[a][0], CUTS[a][1])
+
+    def za(k, a):
+        view = aw.at[t, a_rows(0, t, a), a_lanes(a)]
+        return rcopy(view, view, za_s.at[a, k - 1], za_r.at[a, t], (d, far(k)))
+
+    def za_wait(s, a):
+        view = aw.at[s, a_rows(0, s, a), a_lanes(a)]
+        rcopy(view, view, za_s.at[a, 0], za_r.at[a, s], (d, t)).wait_recv()
 
     def zb(k, which):
         dst = (bupa if which == 0 else qvba).at[t]
-        return rcopy(dst, dst, zb_s.at[2 * (k - 1) + which], zb_r.at[which, t], (d, far(parts - k)))
+        return rcopy(dst, dst, zb_s.at[2 * (k - 1) + which], zb_r.at[which, t], (d, far(k)))
 
     def zb_wait(s, which):
         dst = (bupa if which == 0 else qvba).at[s]
@@ -254,107 +328,32 @@
     for cp in a_loads:
         cp.wait()
     for k in range(1, parts):
-        za(k).start()
+        for a in range(2):
+            za(k, a).start()
         zb(k, 1).start()
-    x_copy.start()
     for k in range(1, parts):
         zb(k, 0).start()
 
-    def ga(stage, s):
-        low, high, first, second = route(s % 2)
-        if stage == 0:
-            view, dev = aw.at[s, rows((c * 4 + high * 2 + low) * piece, piece), :], first
-        elif stage == 1:
-            view, dev = aw.at[s, rows((c * 4 + high * 2) * piece, 2 * piece), :], second
-        else:
-            view, dev = aw.at[s, rows(c * 4 * piece, 4 * piece), :], dev_c
-        return rcopy(view, view, ga_s.at[stage, s], ga_r.at[stage, s], dev)
-
-    def ga_step(stage, k):
-        s = far(k)
-        if stage == 0:
-            za_wait(s, s % 2)
-        else:
-            ga(stage - 1, s).wait_recv()
-        ga(stage, s).start()
-
-    gain1 = g1_ref[...][None, :]
-    shift1 = s1_ref[...][None, :]
-    unit, _ = unit_of(x_ref[...].astype(F32))
-    xn[0:share, :] = (unit * gain1 + shift1).astype(BF16)
-    ga_step(0, 1)
-
-    bucket = bid_ref[0]
-    span = jnp.where(bucket == 0, BUCKET, jnp.where(bucket == 1, 2 * BUCKET, 4 * BUCKET))
-    weight = jnp.where(bucket == 0, bw_ref[0], jnp.where(bucket == 1, bw_ref[1], bw_ref[2]))
-
-    def slot_info(base, shape):
-        place = base + lax.broadcasted_iota(jnp.int32, shape, 0)
-        item = jnp.zeros(shape, jnp.int32)
-        for j in range(1, len_ref.shape[1]):
-            item = item + jnp.where(place >= j * span, 1, 0)
-        length = jnp.zeros(shape, jnp.int32)
-        for j in range(len_ref.shape[1]):
-            length = jnp.where(item == j, len_ref[0, j], length)
-        return item, (place - item * span) < length
-
-    wide = (share, 2 * 128)
-    lane = lanes(wide)
-    slots = len_ref.shape[1]
-    in_aux = (lane >= hw) & (lane < hw + slots)
-    one_aux = jnp.where(lane >= hw, 1.0, 0.0).astype(BF16)
-
-    own_item, own_live = slot_info(t * share, wide)
-    q_aux = jnp.where(in_aux & (own_item == lane - hw), 1.0, 0.0).astype(BF16)
-    k_aux0 = jnp.where(in_aux & ~((own_item == lane - hw) & own_live), -BIG, 0.0).astype(BF16)
-    pair_item, pair_live = slot_info(tp * share, wide)
-    k_aux1 = jnp.where(in_aux & ~((pair_item == lane - hw) & pair_live), -BIG, 0.0).astype(BF16)
-    for s in range(parts):
-        qb[s] = q_aux
-        kb[s, 0:share] = k_aux0
-        kb[s, share:keys] = k_aux1
-        vb[s, 0:share] = one_aux
-        vb[s, share:keys] = one_aux
-    _, live1 = slot_info(t * share, (share, 128))
-    row_weight = jnp.where(live1, weight, 0.0)[:, 0:1]
-
-    ga_step(0, 2)
-
-    def zf(k, j):
-        low, high, _, _ = route((t + j) % 2)
-        view = fg.at[t * nblk + j, :, rows((c * 4 + high * 2 + low) * piece, piece), :]
-        return rcopy(
-            view, view, zf_s.at[(k - 1) * nblk + j], zf_r.at[t * nblk + j], (d, far(parts - k))
-        )
-
-    for j in range(nblk):
-        up_load(j).wait()
-        dn_load(j).wait()
-        fg[t * nblk + j, 1] = uu[j // 2, (j % 2) * BLK : (j % 2 + 1) * BLK, :].T
-    for k in range(1, parts):
-        for j in range(nblk):
-            zf(k, j).start()
-
-    ga_step(1, 1)
-    ga_step(0, 3)
-
-    def project(s, half, own):
-        base = half * share
-        first = 0 if own else hw
-        out = nt(xn[base : base + share, :], aw[s, first:qkvw, :])
-        if own:
-            qb[s, :, 0:hw] = ((out[:, 0:hw] + qvba[s, 0:1, :]) * q_scale).astype(BF16)
-        at = hw - first
-        kb[s, base : base + share, 0:hw] = out[:, at : at + hw].astype(BF16)
-        vb[s, base : base + share, 0:hw] = (
-            out[:, at + hw : at + 2 * hw] + qvba[s, 1:2, :]
-        ).astype(BF16)
+    def ga(stage, s, a):
+        _, _, first, second = route((s + a) % 2)
+        view = aw.at[s, a_rows(stage, s, a), a_lanes(a)]
+        dev = (first, second, dev_c)[stage]
+        return rcopy(view, view, ga_s.at[stage, a, s], ga_r.at[stage, a, s], dev)
+
+    def step_a(stage, i):
+        s = far(i + 1)
+        for a in range(2):
+            if stage == 0:
+                za_wait(s, a)
+            else:
+                ga(stage - 1, s, a).wait_recv()
+            ga(stage, s, a).start()
 
     n_far = (parts - 1) * nblk
 
     def far_block(m):
-        s = (t + 1 + m // nblk) % parts
-        j = m % nblk
+        s = far(1 + m % (parts - 1))
+        j = m // (parts - 1)
         return s, j, s * nblk + j
 
     def gf(stage, m):
@@ -377,167 +376,22 @@
     def within(n, size):
         return (n >= 0) & (n < size)
 
-    def gather_tick(n):
-        @pl.when(within(n, n_far))
-        def _():
-            zf_wait(n)
-            gf(0, n).start()
-
-        @pl.when(within(n - LAG, n_far))
-        def _():
-            gf(0, n - LAG).wait_recv()
-            gf(1, n - LAG).start()
-
-        @pl.when(within(n - 2 * LAG, n_far))
-        def _():
-            gf(1, n - 2 * LAG).wait_recv()
-            gf(2, n - 2 * LAG).start()
-
-    lane_w = lanes((share, 2 * 128))
-    lane_n = lanes((share, 128))
-
-    def head_lanes(h):
-        return (lane_w >= HD * h) & (lane_w < HD * (h + 1))
-
-    def spread(values, at):
-        out = jnp.zeros((share, 2 * 128), F32)
-        for h in range(heads):
-            out = jnp.where(head_lanes(h), values[:, at + h : at + h + 1], out)
-        return out
-
-    def p_out(s, h, half, buf):
-        return pltpu.make_async_copy(
-            pst.at[buf, h], ph_ref.at[s * heads + h, half], ps_sem.at[buf, h]
-        )
-
-    def att_forward(k, half):
+    def step_g(stage, m):
+        if stage == 0:
+            zf_wait(m)
+        else:
+            gf(stage - 1, m).wait_recv()
+        gf(stage, m).start()
+
+    n_all = parts * nblk
+
+    def block(r):
+        own = jnp.where(r < nblk, 1, 0)
+        m = r - nblk
+        k = (1 - own) * (1 + m % (parts - 1))
+        j = own * r + (1 - own) * (m // (parts - 1))
         s = far(k)
-        base = half * share
-        buf = k % 2
-        if half == 1:
-            for h in range(heads):
-                p_out(s, h, half, buf).wait()
-        else:
-
-            @pl.when(k >= 2)
-            def _():
-                for h in range(heads):
-                    p_out(s, h, half, buf).wait()
-
-        qg = qb[s]
-        kg = kb[s, base : base + share]
-        vg = vb[s, base : base + share]
-        out = jnp.zeros((share, 2 * 128), F32)
-        tops = jnp.zeros((share, 128), F32)
-        sums = jnp.ones((share, 128), F32)
-        for h in range(heads):
-            head = head_lanes(h)
-            qm = jnp.where(head | (lane_w >= hw), qg, jnp.zeros_like(qg))
-            scores = nt(qm, kg)
-            top = jnp.max(scores, axis=1, keepdims=True)
-            probs = jnp.exp2(scores - top).astype(BF16)
-            pst[buf, h] = probs
-            mixed = nn(probs, vg)
-            out = jnp.where(head, mixed, out)
-            tops = jnp.where(lane_n == h, top, tops)
-            sums = jnp.where(lane_n == h, mixed[:, hw : hw + 1], sums)
-        for h in range(heads):
-            p_out(s, h, half, buf).start()
-        log_sum = tops + jnp.log2(sums)
-        if half == 0:
-            mx[s] = (out * spread(1.0 / sums, 0)).astype(BF16)
-            stat[s] = jnp.where(lane_n < 8, tops, pltpu.roll(log_sum, 8, 1))
-        else:
-            before = stat[s]
-            log_before = pltpu.roll(before, 120, 1)
-            upper = jnp.maximum(log_sum, log_before)
-            lower = jnp.minimum(log_sum, log_before)
-            log_all = upper + jnp.log2(1.0 + jnp.exp2(lower - upper))
-            part0 = jnp.exp2(log_before - log_all)
-            part1 = jnp.exp2(log_sum - log_all) / sums
-            mx[s] = (mx[s].astype(F32) * spread(part0, 0) + out * spread(part1, 0)).astype(BF16)
-            stat[s] = jnp.where(
-                lane_n < 8,
-                jnp.exp2(before - log_all),
-                pltpu.roll(jnp.exp2(tops - log_all), 8, 1),
-            )
-
-    def own_keys(k, carry):
-        s = far(k)
-
-        @pl.when(k > 0)
-        def _():
-            zb_wait(s, 1)
-            ga(2, s).wait_recv()
-
-        project(s, 0, True)
-        att_forward(k, 0)
-
-        @pl.when(k == 0)
-        def _():
-            ga_step(2, 1)
-            ga_step(1, 2)
-
-        @pl.when(k == 1)
-        def _():
-            ga_step(2, 2)
-            ga_step(1, 3)
-
-        @pl.when(k == 2)
-        def _():
-            ga_step(2, 3)
-
-        return carry
-
-    lax.fori_loop(0, parts, own_keys, 0)
-
-    x_copy.wait_recv()
-    unit, _ = unit_of(xp[...].astype(F32))
-    xn[share:keys, :] = (unit * gain1 + shift1).astype(BF16)
-
-    def pair_keys(k, carry):
-        project(far(k), 1, False)
-        att_forward(k, 1)
-        gather_tick(k)
-        return carry
-
-    lax.fori_loop(0, parts, pair_keys, 0)
-    for buf in range(2):
-        for h in range(heads):
-            p_out(0, h, 1, buf).wait()
-
-    branch = jnp.zeros((share, width), F32)
-    for s in range(parts):
-        branch = branch + nn(mx[s, :, 0:hw], aw[s, qkvw : 4 * hw, :])
-    middle = x_ref[...].astype(F32) + (branch + bout_ref[...][None, :])
-    mid[...] = middle
-    unit, _ = unit_of(middle)
-    normed = (unit * g2_ref[...][None, :] + s2_ref[...][None, :]).astype(BF16)
-    n2 = uu.at[0, 0:share, :]
-    n2t = uu.at[1, :, 0:share]
-    n2[...] = normed
-    n2t[...] = normed.T
-    cot_load.wait()
-    low_grad = (ol[...].astype(F32) * row_weight).astype(BF16)
-    early[...] = jnp.zeros_like(early)
-    late[...] = jnp.zeros_like(late)
-    early[3:4, :] = jnp.sum(low_grad.astype(F32), axis=0, keepdims=True)
-    ol[...] = low_grad
-    olt[...] = low_grad.T
-    acc0[...] = jnp.zeros_like(acc0)
-    acc1[...] = jnp.zeros_like(acc1)
-
-    for k in range(1, parts):
-        zb_wait(far(k), 0)
-
-    n_all = parts * nblk
-
-    def block(r):
-        k = r // nblk
-        j = r % nblk
-        s = (t + k) % parts
         home = s * nblk + j
-        own = jnp.where(k == 0, 1, 0)
         return k, j, s, home, home + own * (n_all + j - home)
 
     def rf(stage, r):
@@ -567,7 +421,7 @@
                 f1_r.at[r],
                 first,
             )
-        z = jnp.maximum(r - nblk, 0)
+        z = jnp.maximum((k - 1) * nblk + j, 0)
         return rcopy(
             fg.at[g, :, rows((c * 4 + high * 2 + low) * piece, piece), :],
             rz_f.at[z],
@@ -579,8 +433,8 @@
     def add_rows(ref, got):
         ref[...] = (ref[...].astype(F32) + got[...].astype(F32)).astype(BF16)
 
-    def rf_second(r):
-        k, j, s, _, g = block(r)
+    def rf_core(r):
+        _, _, _, _, g = block(r)
         rf(0, r).wait_recv()
         add_rows(fg.at[g, :, rows(c * 4 * piece, 4 * piece), :], rc_f.at[r % SLOTS_C])
 
@@ -588,7 +442,8 @@
         def _():
             pl.semaphore_signal(credit, inc=1, device_id=dev_c, device_id_type=MESH)
 
-        rf(1, r).start()
+    def turn(i):
+        return (i + nblk) % n_all
 
     def rf_first(r):
         k, j, s, _, g = block(r)
@@ -640,18 +495,303 @@
             loc_sem.at[nblk + 2 + j % 2],
         )
 
-    def reduce_tick(n):
-        @pl.when(within(n, n_all))
+    def f_second(j):
+        af(0, j).wait_recv()
+        af(1, j).start()
+
+    def f_third(j):
+        af(1, j).wait_recv()
+        af(2, j).start()
+
+    def ra_view(stage, s, a):
+        low, high, first, second = route((s + a) % 2)
+        if stage == 0:
+            return rows((1 - c) * 4 * piece, 4 * piece), rc_a, dev_c
+        if stage == 1:
+            return rows((c * 4 + (1 - high) * 2) * piece, 2 * piece), r2_a, second
+        if stage == 2:
+            return rows((c * 4 + high * 2 + 1 - low) * piece, piece), r1_a, first
+        return rows((c * 4 + high * 2 + low) * piece, piece), rz_a, (d, s)
+
+    def ra(stage, q, a):
+        s = group_of(q)
+        where, buf, dev = ra_view(stage, s, a)
+        if stage == 3:
+            q = jnp.minimum(q, parts - 2)
+        return rcopy(
+            aw.at[s, where, a_lanes(a)],
+            buf.at[q, :, a_lanes(a)],
+            ra_s.at[stage, a, q],
+            ra_r.at[stage, a, q],
+            dev,
+        )
+
+    def ra_add(stage, q, a):
+        s = group_of(q)
+        buf = (rc_a, r2_a, r1_a)[stage]
+        ra(stage, q, a).wait_recv()
+        add_rows(aw.at[s, a_rows(2 - stage, s, a), a_lanes(a)], buf.at[q, :, a_lanes(a)])
+
+    def group_of(it):
+        return far((it + 1) % parts)
+
+    def step_b(stage, q):
+        for a in range(2):
+            ra_add(stage - 1, q, a)
+        for a in range(2):
+            if stage < 3:
+                ra(stage, q, a).start()
+            else:
+
+                @pl.when(q < parts - 1)
+                def _():
+                    ra(3, q, a).start()
+
+    steps = {
+        "a0": lambda i: step_a(0, i),
+        "a1": lambda i: step_a(1, i),
+        "a2": lambda i: step_a(2, i),
+        "g0": lambda i: step_g(0, i),
+        "g1": lambda i: step_g(1, i),
+        "g2": lambda i: step_g(2, i),
+        "r2": lambda i: rf(1, turn(i)).start(),
+        "r1": lambda i: rf_first(turn(i)),
+        "rf": lambda i: rf_far(turn(i)),
+        "b1": lambda i: step_b(1, i),
+        "b2": lambda i: step_b(2, i),
+        "b3": lambda i: step_b(3, i),
+        "f0": lambda i: f_final(i),
+        "f1": lambda i: f_second(i),
+        "f2": lambda i: f_third(i),
+    }
+
+    def repeat(name, low, high):
+        def one(i, carry):
+            steps[name](i)
+            return carry
+
+        lax.fori_loop(low, high, one, 0)
+
+    def advance(place, idx=0):
+        for name, counts in PLAN[place]:
+            if len(counts) == 2:
+                repeat(name, counts[0], counts[1])
+                continue
+            low = counts[0]
+            high = counts[0]
+            for i in range(1, len(counts)):
+                more = counts[i] - counts[i - 1]
+                if more:
+                    low = low + jnp.where(idx >= i, more, 0)
+                    high = high + jnp.where(idx >= i - 1, more, 0)
+            repeat(name, low, high)
+
+    gain1 = g1_ref[...][None, :]
+    shift1 = s1_ref[...][None, :]
+    unit, _ = unit_of(x_ref[...].astype(F32))
+    xn[0:share, :] = (unit * gain1 + shift1).astype(BF16)
+    advance("p0")
+
+    def zf(k, j):
+        low, high, _, _ = route((t + j) % 2)
+        view = fg.at[t * nblk + j, :, rows((c * 4 + high * 2 + low) * piece, piece), :]
+        return rcopy(
+            view, view, zf_s.at[(k - 1) * nblk + j], zf_r.at[t * nblk + j], (d, far(k))
+        )
+
+    for j in range(nblk):
+        up_load(j).wait()
+        dn_load(j).wait()
+        fg[t * nblk + j, 1] = uu[j // 2, (j % 2) * BLK : (j % 2 + 1) * BLK, :].T
+    for m in range((parts - 1) * nblk):
+        if m == X_PLACE:
+            x_copy.start()
+        zf(1 + m % (parts - 1), m // (parts - 1)).start()
+
+    advance("p1")
+
+    bucket = bid_ref[0]
+    span = jnp.where(bucket == 0, BUCKET, jnp.where(bucket == 1, 2 * BUCKET, 4 * BUCKET))
+    weight = jnp.where(bucket == 0, bw_ref[0], jnp.where(bucket == 1, bw_ref[1], bw_ref[2]))
+
+    def slot_info(base, shape):
+        place = base + lax.broadcasted_iota(jnp.int32, shape, 0)
+        item = jnp.zeros(shape, jnp.int32)
+        for j in range(1, len_ref.shape[1]):
+            item = item + jnp.where(place >= j * span, 1, 0)
+        length = jnp.zeros(shape, jnp.int32)
+        for j in range(len_ref.shape[1]):
+            length = jnp.where(item == j, len_ref[0, j], length)
+        return item, (place - item * span) < length
+
+    wide = (share, 2 * 128)
+    lane = lanes(wide)
+    slots = len_ref.shape[1]
+    in_aux = (lane >= hw) & (lane < hw + slots)
+    one_aux = jnp.where(lane >= hw, 1.0, 0.0).astype(BF16)
+
+    own_item, own_live = slot_info(t * share, wide)
+    q_aux = jnp.where(in_aux & (own_item == lane - hw), 1.0, 0.0).astype(BF16)
+    k_aux0 = jnp.where(in_aux & ~((own_item == lane - hw) & own_live), -BIG, 0.0).astype(BF16)
+    pair_item, pair_live = slot_info(tp * share, wide)
+    k_aux1 = jnp.where(in_aux & ~((pair_item == lane - hw) & pair_live), -BIG, 0.0).astype(BF16)
+    for s in range(parts):
+        qb[s] = q_aux
+        kb[s, 0:share] = k_aux0
+        kb[s, share:keys] = k_aux1
+        vb[s, 0:share] = one_aux
+        vb[s, share:keys] = one_aux
+    _, live1 = slot_info(t * share, (share, 128))
+    row_weight = jnp.where(live1, weight, 0.0)[:, 0:1]
+
+    advance("p2")
+
+    def project(s, half, own):
+        base = half * share
+        first = 0 if own else hw
+        out = nt(xn[base : base + share, :], aw[s, first:qkvw, :])
+        if own:
+            qb[s, :, 0:hw] = ((out[:, 0:hw] + qvba[s, 0:1, :]) * q_scale).astype(BF16)
+        at = hw - first
+        kb[s, base : base + share, 0:hw] = out[:, at : at + hw].astype(BF16)
+        vb[s, base : base + share, 0:hw] = (
+            out[:, at + hw : at + 2 * hw] + qvba[s, 1:2, :]
+        ).astype(BF16)
+
+    lane_w = lanes((share, 2 * 128))
+    lane_n = lanes((share, 128))
+
+    def head_lanes(h):
+        return (lane_w >= HD * h) & (lane_w < HD * (h + 1))
+
+    def spread(values, at):
+        out = jnp.zeros((share, 2 * 128), F32)
+        for h in range(heads):
+            out = jnp.where(head_lanes(h), values[:, at + h : at + h + 1], out)
+        return out
+
+    def p_out(s, h, half, buf):
+        return pltpu.make_async_copy(
+            pst.at[buf, h], ph_ref.at[s * heads + h, half], ps_sem.at[buf, h]
+        )
+
+    at0 = hw - 128
+    at1 = at0 + 32
+    at2 = at0 + 64
+
+    def att_forward(k, half):
+        s = far(k)
+        base = half * share
+        buf = k % 2
+        if half == 1:
+            for h in range(heads):
+                p_out(s, h, half, buf).wait()
+        else:
+
+            @pl.when(k >= 2)
+            def _():
+                for h in range(heads):
+                    p_out(s, h, half, buf).wait()
+
+        qg = qb[s]
+        kg = kb[s, base : base + share]
+        vg = vb[s, base : base + share]
+        out = jnp.zeros((share, 2 * 128), F32)
+        tops = jnp.zeros((share, 128), F32)
+        for h in range(heads):
+            head = head_lanes(h)
+            qm = jnp.where(head | (lane_w >= hw), qg, jnp.zeros_like(qg))
+            scores = nt(qm, kg)
+            top = jnp.max(scores, axis=1, keepdims=True)
+            probs = jnp.exp2(scores - top).astype(BF16)
+            pst[buf, h] = probs
+            mixed = nn(probs, vg)
+            out = jnp.where(head | (lane_w == hw + h), mixed, out)
+            tops = jnp.where(lane_n == at0 + h, top, tops)
+        for h in range(heads):
+            p_out(s, h, half, buf).start()
+        sums = jnp.where((lane_n >= at0) & (lane_n < at0 + heads), out[:, 128:256], 1.0)
+        log_sum = tops + jnp.log2(sums)
+        if half == 0:
+            mx[s] = (out * spread(1.0 / sums, at0)).astype(BF16)
+            stat[s] = jnp.where(lane_n < at1, tops, pltpu.roll(log_sum, 32, 1))
+        else:
+            before = stat[s]
+            log_before = pltpu.roll(before, 96, 1)
+            upper = jnp.maximum(log_sum, log_before)
+            lower = jnp.minimum(log_sum, log_before)
+            log_all = upper + jnp.log2(1.0 + jnp.exp2(lower - upper))
+            part0 = jnp.exp2(log_before - log_all)
+            part1 = jnp.exp2(log_sum - log_all) / sums
+            mx[s] = (
+                mx[s].astype(F32) * spread(part0, at0) + out * spread(part1, at0)
+            ).astype(BF16)
+            stat[s] = jnp.where(
+                lane_n < at1,
+                jnp.exp2(before - log_all),
+                pltpu.roll(jnp.exp2(tops - log_all), 32, 1),
+            )
+
+    def own_keys(k, carry):
+        s = far(k)
+
+        @pl.when(k > 0)
         def _():
-            rf_second(n)
-
-        @pl.when(within(n - G_LAG1, n_all))
+            zb_wait(s, 1)
+            for a in range(2):
+                ga(2, s, a).wait_recv()
+
+        project(s, 0, True)
+
+        @pl.when(k == 0)
         def _():
-            rf_first(n - G_LAG1)
-
-        @pl.when(within(n - G_LAG1 - G_LAG2, n_all))
-        def _():
-            rf_far(n - G_LAG1 - G_LAG2)
+            advance("pj")
+
+        att_forward(k, 0)
+        advance("o", k)
+        return carry
+
+    lax.fori_loop(0, parts, own_keys, 0)
+
+    x_copy.wait_recv()
+    unit, _ = unit_of(xp[...].astype(F32))
+    xn[share:keys, :] = (unit * gain1 + shift1).astype(BF16)
+
+    def pair_keys(k, carry):
+        project(far(k), 1, False)
+        att_forward(k, 1)
+        advance("q", k)
+        return carry
+
+    lax.fori_loop(0, parts, pair_keys, 0)
+    for buf in range(2):
+        for h in range(heads):
+            p_out(0, h, 1, buf).wait()
+
+    branch = jnp.zeros((share, width), F32)
+    for s in range(parts):
+        branch = branch + nn(mx[s, :, 0:hw], aw[s, qkvw : 4 * hw, :])
+    middle = x_ref[...].astype(F32) + (branch + bout_ref[...][None, :])
+    mid[...] = middle
+    unit, _ = unit_of(middle)
+    normed = (unit * g2_ref[...][None, :] + s2_ref[...][None, :]).astype(BF16)
+    n2 = uu.at[0, 0:share, :]
+    n2t = uu.at[1, :, 0:share]
+    n2[...] = normed
+    n2t[...] = normed.T
+    cot_load.wait()
+    low_grad = (ol[...].astype(F32) * row_weight).astype(BF16)
+    early[...] = jnp.zeros_like(early)
+    late[...] = jnp.zeros_like(late)
+    early[3:4, :] = jnp.sum(low_grad.astype(F32), axis=0, keepdims=True)
+    ol[...] = low_grad
+    olt[...] = low_grad.T
+    acc0[...] = jnp.zeros_like(acc0)
+    acc1[...] = jnp.zeros_like(acc1)
+
+    for k in range(1, parts):
+        zb_wait(far(k), 0)
+    advance("mid")
 
     def drain_zf(m, carry):
         view = fg.at[0, :, 0:piece, :]
@@ -696,11 +836,16 @@
             pl.semaphore_wait(credit, 1)
 
         rf(0, r).start()
-        gather_tick(parts + r)
-        reduce_tick(r - 1)
+
+        @pl.when(r > 0)
+        def _():
+            rf_core(r - 1)
+
+        advance("r", r)
         return carry
 
     lax.fori_loop(0, n_all, ffn, 0)
+    rf_core(n_all - 1)
 
     middle = mid[...]
     ngs[...] = (middle + (acc0[...] + bdn_ref[...][None, :])).astype(BF16)
@@ -722,10 +867,15 @@
     ol[...] = branch_low
 
     for k in range(1, parts):
-        za(k).wait_send()
-    for k in range(1, parts):
-        for stage in range(3):
-            ga(stage, far(k)).wait_send()
+        for a in range(2):
+            za(k, a).wait_send()
+            for stage in range(3):
+                ga(stage, far(k), a).wait_send()
+    advance("ln")
+
+    head_row = lax.broadcasted_iota(jnp.int32, (hw, 128), 0)
+    head_col = (lax.broadcasted_iota(jnp.int32, (hw, 128), 1) - at2) * HD
+    pick = jnp.where((head_row >= head_col) & (head_row < head_col + HD), 1.0, 0.0).astype(BF16)
 
     def out_back(k, carry):
         s = far(k)
@@ -733,15 +883,12 @@
         mixed_grad = nt(ol[...], aw[s, qkvw : 4 * hw, :]).astype(BF16)
         dmx[s, :, 0:hw] = mixed_grad
         prod = mixed_grad.astype(F32) * mixed.astype(F32)
-        lane_h = lanes((share, hw))
-        known = stat[s]
-        for h in range(heads):
-            head = (lane_h >= HD * h) & (lane_h < HD * (h + 1))
-            delta = jnp.sum(jnp.where(head, prod, 0.0), axis=1, keepdims=True)
-            known = jnp.where(lane_n == 16 + h, delta, known)
-        stat[s] = known
+        coarse = prod.astype(BF16)
+        fine = (prod - coarse.astype(F32)).astype(BF16)
+        delta = nn(coarse, pick) + nn(fine, pick)
+        stat[s] = jnp.where((lane_n >= at2) & (lane_n < at2 + heads), delta, stat[s])
         aw[s, qkvw : 4 * hw, :] = nn(mixed.T, ol[...]).astype(BF16)
-        reduce_tick(n_all - 1 + k)
+        advance("k", k)
         return carry
 
     lax.fori_loop(0, parts, out_back, 0)
@@ -751,9 +898,6 @@
             ph_ref.at[s * heads + h, half], pst.at[buf, h], ps_sem.at[buf, h]
         )
 
-    def group_of(it):
-        return (t + 1 + it % parts) % parts
-
     def fetch(it):
         for h in range(heads):
             p_in(group_of(it), h, 1 - it // parts, it % 2).start()
@@ -770,15 +914,17 @@
         for h in range(heads):
             p_in(s, h, half, buf).wait()
         known = stat[s]
-        wanted = known if half == 0 else pltpu.roll(known, 120, 1)
-        delta = -(pltpu.roll(known, 112, 1) * wanted)
+        wanted = known if half == 0 else pltpu.roll(known, 96, 1)
+        delta = -(pltpu.roll(known, 64, 1) * wanted)
         coarse = delta.astype(BF16).astype(F32)
-        fine = delta - coarse
-        scaled = dmx[s].astype(F32) * spread(wanted, 0)
-        for h in range(heads):
-            scaled = jnp.where(lane_w == hw + 2 * h, coarse[:, h : h + 1], scaled)
-            scaled = jnp.where(lane_w == hw + 2 * h + 1, fine[:, h : h + 1], scaled)
-        dg = jnp.where(lane_w < hw + 2 * heads, scaled, 0.0).astype(BF16)
+        aux = jnp.where((lane_n >= at0) & (lane_n < at0 + heads), coarse, 0.0)
+        aux = jnp.where(
+            (lane_n >= at0 + 8) & (lane_n < at0 + 8 + heads), pltpu.roll(delta - coarse, 8, 1), aux
+        )
+        scaled = dmx[s].astype(F32) * spread(wanted, at0)
+        dg = jnp.concatenate(
+            [scaled[:, 0:128], jnp.where(lane_n < at0, scaled[:, 128:256], aux)], axis=1
+        ).astype(BF16)
         qg = qb[s]
         kg = kb[s, base : base + share]
         vg = vb[s, base : base + share]
@@ -789,8 +935,8 @@
         dvs = []
         for h in range(heads):
             head = head_lanes(h)
-            aux = (lane_w >= hw + 2 * h) & (lane_w < hw + 2 * h + 2)
-            dm = jnp.where(head | aux, dg, jnp.zeros_like(dg))
+            aux_h = (lane_w == hw + h) | (lane_w == hw + 8 + h)
+            dm = jnp.where(head | aux_h, dg, jnp.zeros_like(dg))
             prob_grad = nt(dm, vg)
             probs = pst[buf, h]
             score_grad = (probs.astype(F32) * prob_grad).astype(BF16)
@@ -820,7 +966,7 @@
         back = uu[s, hw:qkvw, 0:share].T
         acc0[...] += nn(back, aw[s, hw:qkvw, :])
         late[pl.ds(2 * s + 1, 1), 0:hw] = row_sums(back[:, hw : 2 * hw])
-        reduce_tick(n_all - 1 + parts + it)
+        advance("h", it)
         return carry
 
     lax.fori_loop(0, parts, pair_half, 0)
@@ -833,52 +979,6 @@
     unit, _ = unit_of(xp[...].astype(F32))
     late[8:9, :] = jnp.sum(pair_grad * unit, axis=0, keepdims=True)
     late[9:10, :] = jnp.sum(pair_grad, axis=0, keepdims=True)
-
-    def ra(stage, q):
-        s = group_of(q)
-        low, high, first, second = route(s % 2)
-        if stage == 0:
-            return rcopy(
-                aw.at[s, rows((1 - c) * 4 * piece, 4 * piece), :],
-                rc_a.at[q],
-                ca_s.at[q],
-                ca_r.at[q],
-                dev_c,
-            )
-        if stage == 1:
-            return rcopy(
-                aw.at[s, rows((c * 4 + (1 - high) * 2) * piece, 2 * piece), :],
-                r2_a.at[q],
-                a2_s.at[q],
-                a2_r.at[q],
-                second,
-            )
-        if stage == 2:
-            return rcopy(
-                aw.at[s, rows((c * 4 + high * 2 + 1 - low) * piece, piece), :],
-                r1_a.at[q],
-                a1_s.at[q],
-                a1_r.at[q],
-                first,
-            )
-        return rcopy(
-            aw.at[s, rows((c * 4 + high * 2 + low) * piece, piece), :],
-            rz_a.at[q],
-            az_s.at[q],
-            az_r.at[q],
-            (d, s),
-        )
-
-    def ra_step(stage, q):
-        s = group_of(q)
-        low, high, _, _ = route(s % 2)
-        ra(stage, q).wait_recv()
-        if stage == 0:
-            add_rows(aw.at[s, rows(c * 4 * piece, 4 * piece), :], rc_a.at[q])
-        elif stage == 1:
-            add_rows(aw.at[s, rows((c * 4 + high * 2) * piece, 2 * piece), :], r2_a.at[q])
-        else:
-            add_rows(aw.at[s, rows((c * 4 + high * 2 + low) * piece, piece), :], r1_a.at[q])
 
     stages = (dev_c, (dx, t), (dy, t))
 
@@ -924,23 +1024,9 @@
         aw[s, hw:qkvw, :] = (
             nn(dd[hw:qkvw, :], xn[0:share, :]) + nn(uu[s, hw:qkvw, 0:share], xn[share:keys, :])
         ).astype(BF16)
-        ra(0, q).start()
-        reduce_tick(n_all - 1 + 2 * parts + q)
-
-        @pl.when(q >= 1)
-        def _():
-            ra_step(0, q - 1)
-            ra(1, q - 1).start()
-
-        @pl.when(q >= 2)
-        def _():
-            ra_step(1, q - 2)
-            ra(2, q - 2).start()
-
-        @pl.when(q >= 3)
-        def _():
-            ra_step(2, q - 3)
-            ra(3, q - 3).start()
+        for a in range(2):
+            ra(0, q, a).start()
+        advance("w", q)
 
         for stage in range(3):
 
@@ -951,76 +1037,60 @@
         return carry
 
     lax.fori_loop(parts, 2 * parts, own_half, 0)
-
-    last = parts - 1
-    ra_step(0, last)
-    ra(1, last).start()
-    ra_step(1, last - 1)
-    ra(2, last - 1).start()
-    ra_step(2, last - 2)
-    ra(3, last - 2).start()
-    for n in range(n_all - 1 + 3 * parts, n_all + G_LAG1 + G_LAG2):
-        reduce_tick(n)
 
     own_grad = acc1[...]
     unit, scale_inv = unit_of(x_ref[...].astype(F32))
     late[8:9, :] = late[8:9, :] + jnp.sum(own_grad * unit, axis=0, keepdims=True)
     late[9:10, :] = late[9:10, :] + jnp.sum(own_grad, axis=0, keepdims=True)
     vec(1, 0).start()
-    f_final(0)
-    vec_next(1, 0)
-    f_final(1)
-    ra_step(1, last)
-    ra(2, last).start()
-    vec_next(1, 1)
-    f_final(2)
-    f_final(3)
-    ra_step(2, last - 1)
-    ra(3, last - 1).start()
-    vec_next(1, 2)
-    f_final(4)
-
-    def f_second(j):
-        af(0, j).wait_recv()
-        af(1, j).start()
-
-    def f_third(j):
-        af(1, j).wait_recv()
-        af(2, j).start()
-
-    for j in range(nblk):
-        f_second(j)
-
-    ra_step(2, last)
-    mine = rows(pos_own_a, piece)
-    total = aw[t, mine, :].astype(F32)
-    for q in range(parts - 1):
-        rcopy(rz_a.at[q], rz_a.at[q], az_s.at[q], az_r.at[q], (d, t)).wait_recv()
-        total = total + rz_a[q].astype(F32)
     done = uu.at[0]
-    done[mine, :] = total.astype(BF16)
-
-    def aa(stage):
-        if stage == 0:
-            view, dev = done.at[mine, :], first_a
-        elif stage == 1:
-            view, dev = done.at[rows((c * 4 + high_a * 2) * piece, 2 * piece), :], second_a
+    xg_copy = pltpu.make_async_copy(mid, xg_ref, loc_sem.at[nblk])
+
+    def aa(stage, a):
+        _, _, first, second = route((t + a) % 2)
+        view = done.at[a_rows(stage, t, a), a_lanes(a)]
+        dev = (first, second, dev_c)[stage]
+        return rcopy(view, view, aa_s.at[stage, a], aa_r.at[stage, a], dev)
+
+    def att_final():
+        for a in range(2):
+            mine = a_rows(0, t, a)
+            low = CUTS[a][0]
+            high = low + CUTS[a][1]
+            total = aw[t, mine, low:high].astype(F32)
+            for q in range(parts - 1):
+                view = rz_a.at[q, :, a_lanes(a)]
+                rcopy(view, view, ra_s.at[3, a, q], ra_r.at[3, a, q], (d, t)).wait_recv()
+                total = total + rz_a[q, :, low:high].astype(F32)
+            done[mine, low:high] = total.astype(BF16)
+            aa(0, a).start()
+
+    def att_round(stage):
+        for a in range(2):
+            aa(stage - 1, a).wait_recv()
+            aa(stage, a).start()
+
+    def rows_final():
+        ng_copy.wait_recv()
+        grad = own_grad + ngr[...].astype(F32)
+        mid[...] = mid[...] + norm_back(grad, unit, scale_inv, gain1)
+        xg_copy.start()
+
+    vec_stage = 0
+    for name, low, high in TAIL:
+        if name == "v":
+            vec_next(1, vec_stage)
+            vec_stage += 1
+        elif name == "aa0":
+            att_final()
+        elif name == "aa1":
+            att_round(1)
+        elif name == "aa2":
+            att_round(2)
+        elif name == "ng":
+            rows_final()
         else:
-            view, dev = done.at[rows(c * 4 * piece, 4 * piece), :], dev_c
-        return rcopy(view, view, aa_s.at[stage], aa_r.at[stage], dev)
-
-    aa(0).start()
-
-    ng_copy.wait_recv()
-    grad = own_grad + ngr[...].astype(F32)
-    mid[...] = mid[...] + norm_back(grad, unit, scale_inv, gain1)
-    xg_copy = pltpu.make_async_copy(mid, xg_ref, loc_sem.at[nblk])
-    xg_copy.start()
-
-    for j in range(nblk):
-        f_third(j)
-    aa(0).wait_recv()
-    aa(1).start()
+            repeat(name, low, high)
 
     for j in range(nblk):
         af(2, j).wait_recv()
@@ -1046,9 +1116,6 @@
     for j in range(nblk):
         osm_ref[16 + j : 17 + j, :] = early[pl.ds(4 + t * nblk + j, 1), :]
 
-    aa(1).wait_recv()
-    aa(2).start()
-
     for k in range(1, parts):
         zb(k, 0).wait_send()
         zb(k, 1).wait_send()
@@ -1082,17 +1149,20 @@
         f_out(j, 1).wait()
 
     for q in range(parts):
-        for stage in range(3):
-            ra(stage, q).wait_send()
-        if q < parts - 1:
-            ra(3, q).wait_send()
-    aa(2).wait_recv()
+        for a in range(2):
+            for stage in range(3):
+                ra(stage, q, a).wait_send()
+            if q < parts - 1:
+                ra(3, q, a).wait_send()
+    for a in range(2):
+        aa(2, a).wait_recv()
     oa_copy = pltpu.make_async_copy(done, oa_ref, loc_sem.at[nblk + 1])
     oa_copy.start()
     oa_copy.wait()
     xg_copy.wait()
     for stage in range(3):
-        aa(stage).wait_send()
+        for a in range(2):
+            aa(stage, a).wait_send()
 
 
 def finish(
@@ -1236,13 +1306,13 @@
         pltpu.VMEM((parts, 16, width), F32),
         dma((2 * nblk + 5,)),
         dma((2, heads)),
-        dma((3,)),
-        dma((parts,)),
+        dma((2, 3)),
+        dma((2, parts)),
         dma((2,)),
         dma((6,)),
         dma((2, parts)),
-        dma((3, parts)),
-        dma((3, parts)),
+        dma((3, 2, parts)),
+        dma((3, 2, parts)),
         dma((n_far,)),
         dma((n_all,)),
         dma((3, n_all)),
@@ -1257,16 +1327,10 @@
         dma((n_far,)),
         dma((3, nblk)),
         dma((3, nblk)),
-        dma((parts,)),
-        dma((parts,)),
-        dma((parts,)),
-        dma((parts,)),
-        dma((parts,)),
-        dma((parts,)),
-        dma((parts,)),
-        dma((parts,)),
-        dma((3,)),
-        dma((3,)),
+        dma((4, 2, parts)),
+        dma((4, 2, parts)),
+        dma((3, 2)),
+        dma((3, 2)),
         dma((2, 7)),
         dma((2, 7)),
         dma((2,)),

time: 234 us -> 209 us (0.89)
  Pallas kernels: 232 us -> 207 us
    pallas_call x1, Pallas kernels: 224 us -> 200 us  [local(): pl.pallas_call(kernel, out_shape=[jax.ShapeDtypeStruct((share, width), BF...]
where the time goes in v3:
time: 209 us
  Pallas kernels  207 us (99%)
    pallas_call x1, Pallas kernels, local(): pl.pallas_call(kernel, out_shape=[jax.ShapeDtypeStruct((share, width), BF...  200 us
    pallas_call x1, Pallas kernels, local(): pl.pallas_call(finish, out_shape=[jax.ShapeDtypeStruct((share, width), BF...  7.09 us

profile of v3, /device:TPU:0, one launch (start us, length us, event | category | flops | bytes accessed | tf_op | source)
XLA Modules:
  0.0 208.9 jit_solution(11914558574790791338)
XLA Ops:
  1.3 200.3 %shard_map.272 = (bf16[512,640]{1,0:T(8,128)(2,1)}, f32[512,640]{1,0:T(8,128)}, bf16[640,1280]{1,0:T(8,128)(2,1)}, bf16[1280,640]{1,0:T(8,128)(2,1)}, bf16[640,6...) custom-call(bf16[512,640]{1,0:T(8,128)(2,1)} %x_ref.1, bf16[512,640]{1,0:T(8,128)(2,1)} %cot_ref.1, ...), custom_call_target="tpu_custom_call" | custom-call | tf_op jit(solution)/shard_map/pallas_call | solution.py:1339
  201.6 7.1 %shard_map.273 = (bf16[512,640]{1,0:T(8,128)(2,1)}, f32[512,640]{1,0:T(8,128)}, f32[640,1280]{1,0:T(8,128)}, f32[1280,640]{1,0:T(8,128)}, f32[480,640]{1,0:T(8,1...) custom-call(bf16[512,640]{1,0:T(8,128)(2,1)} %get-tuple-element.34.l, ...), custom_call_target="tpu_custom_call" | custom-call | tf_op jit(solution)/shard_map/pallas_call | solution.py:1384

commit v4 on v3

--- a/solution.py
+++ b/solution.py
@@ -20,79 +20,77 @@
 RSQRT2 = 1.0 / math.sqrt(2.0)
 RSQRT2PI = 1.0 / math.sqrt(2.0 * math.pi)
 SLOTS_C = 2
-X_PLACE = 4
+X_PLACE = 0
+WIDE_FROM = 15
+NG_PLACE = 2
 CUTS = ((0, 256), (256, 384))
+CHUNKS = 4
 PLAN = {
     "p0": (
         ("a0", (0, 1)),
         ("a1", (0, 1)),
     ),
     "p1": (
-        ("a2", (0, 1)),
+        ("a0", (1, 2)),
     ),
     "p2": (
-        ("a0", (1, 3)),
+        ("a0", (2, 3)),
+        ("a1", (1, 3)),
+        ("a2", (0, 3)),
     ),
     "pj": (
-        ("a1", (1, 3)),
-        ("a2", (1, 3)),
     ),
     "o": (
-        ("g0", (0, 0, 0, 1, 2)),
     ),
     "q": (
-        ("g0", (2, 8, 10, 15, 15)),
-        ("g1", (0, 2, 4, 6, 10)),
-        ("g2", (0, 0, 0, 1, 3)),
+        ("g0", (0, 4, 12, 12, 15)),
+        ("g1", (0, 0, 0, 5, 8)),
     ),
     "mid": (
-        ("g1", (10, 11)),
-        ("g2", (3, 5)),
+        ("g1", (8, 10)),
+        ("g2", (0, 3)),
     ),
     "r": (
-        ("g1", (11, 12, 15, 15, 15, 15, 15, 15, 15, 15, 15, 15, 15, 15, 15, 15, 15, 15, 15, 15, 15)),
-        ("g2", (5, 5, 6, 8, 10, 10, 13, 15, 15, 15, 15, 15, 15, 15, 15, 15, 15, 15, 15, 15, 15)),
-        ("rf", (0, 0, 0, 0, 0, 0, 0, 0, 0, 0, 0, 0, 0, 2, 2, 2, 2, 2, 2, 3, 3)),
-        ("r1", (0, 0, 0, 0, 0, 0, 0, 0, 0, 0, 1, 2, 2, 2, 3, 3, 4, 4, 4, 6, 10)),
-        ("r2", (0, 0, 0, 0, 0, 0, 0, 1, 2, 3, 4, 4, 6, 6, 7, 8, 10, 10, 11, 11, 14)),
+        ("g1", (10, 13, 15, 15, 15, 15, 15, 15, 15, 15, 15, 15, 15, 15, 15, 15, 15, 15, 15, 15, 15)),
+        ("g2", (3, 3, 5, 5, 6, 9, 10, 13, 15, 15, 15, 15, 15, 15, 15, 15, 15, 15, 15, 15, 15)),
+        ("rf", (0, 0, 0, 0, 0, 0, 0, 0, 0, 0, 0, 0, 0, 1, 1, 1, 1, 1, 2, 2, 3)),
+        ("r1", (0, 0, 0, 0, 0, 0, 0, 0, 0, 0, 1, 2, 2, 2, 2, 3, 3, 5, 5, 6, 6)),
+        ("r2", (0, 0, 0, 0, 0, 0, 0, 1, 2, 3, 4, 5, 6, 6, 8, 8, 9, 11, 12, 12, 12)),
     ),
     "ln": (
-        ("rf", (3, 5)),
+        ("rf", (3, 4)),
     ),
     "k": (
-        ("rf", (5, 5, 6, 6, 6)),
-        ("r1", (10, 10, 11, 11, 11)),
-        ("r2", (14, 15, 15, 17, 18)),
+        ("rf", (4, 4, 4, 5, 5)),
+        ("r1", (6, 10, 10, 10, 10)),
+        ("r2", (12, 13, 14, 17, 17)),
     ),
     "h": (
-        ("rf", (6, 9, 11, 11, 13)),
-        ("r1", (11, 11, 15, 15, 18)),
-        ("r2", (18, 18, 19, 19, 20)),
+        ("rf", (5, 5, 5, 9, 12)),
+        ("r1", (10, 11, 12, 17, 18)),
+        ("r2", (17, 18, 19, 19, 20)),
     ),
     "w": (
-        ("rf", (13, 18, 18, 19, 20)),
-        ("r1", (18, 19, 20, 20, 20)),
+        ("rf", (12, 18, 19, 20, 20)),
+        ("r1", (18, 20, 20, 20, 20)),
         ("b3", (0, 0, 0, 0, 1)),
-        ("b2", (0, 0, 0, 1, 3)),
-        ("b1", (0, 0, 1, 3, 4)),
-        ("f0", (0, 3, 3, 4, 4)),
-        ("f1", (0, 0, 1, 2, 2)),
-        ("f2", (0, 0, 0, 0, 2)),
+        ("b2", (0, 0, 1, 1, 3)),
+        ("b1", (0, 1, 1, 3, 4)),
+        ("f0", (0, 3, 4, 5, 5)),
+        ("f1", (0, 0, 2, 3, 5)),
     ),
 }
 TAIL = (
+    ("b3", 1, 3),
+    ("b2", 3, 4),
     ("v", 0, 0),
-    ("b2", 3, 4),
-    ("b3", 1, 3),
-    ("f0", 4, 5),
-    ("f1", 2, 5),
+    ("v", 0, 0),
     ("b3", 3, 4),
     ("aa0", 0, 0),
+    ("f2", 0, 5),
     ("v", 0, 0),
+    ("aa1", 0, 0),
     ("ng", 0, 0),
-    ("v", 0, 0),
-    ("f2", 2, 5),
-    ("aa1", 0, 0),
     ("aa2", 0, 0),
 )
 
@@ -236,11 +234,28 @@
     dev_c = (d + 1 - 2 * c, t)
     dx = d + 2 - 4 * bx
     dy = d + 4 - 8 * by
-    tp = t + 1 - 2 * (t % 2)
+    t0 = t % 2
+    t1 = t // 2
+    tp = t + 1 - 2 * t0
+
+    def quotient(n, step, limit):
+        if isinstance(n, int):
+            return n // step
+        return sum(jnp.where(n >= i, 1, 0) for i in range(step, limit, step))
+
+    def odd(n, limit):
+        return n - 2 * quotient(n, 2, limit)
+
+    def differ(a, b):
+        return a + b - 2 * a * b
+
+    def far_bits(k):
+        high = quotient(k, 2, parts)
+        low = differ(t0, k - 2 * high)
+        return low + 2 * differ(t1, high), low
 
     def far(k):
-        low_t, high_t, low_k, high_k = t % 2, t // 2, k % 2, k // 2
-        return low_t + low_k - 2 * low_t * low_k + 2 * (high_t + high_k - 2 * high_t * high_k)
+        return far_bits(k)[0]
 
     def route(par):
         low = bx + par * (by - bx)
@@ -253,6 +268,12 @@
         return pltpu.make_async_remote_copy(
             src_ref=src, dst_ref=dst, send_sem=ssem, recv_sem=rsem, device_id=dev, device_id_type=MESH
         )
+
+    def arrived(view, sem):
+        rcopy(view, view, sem, sem, (d, t)).wait_recv()
+
+    def left(view, sem):
+        rcopy(view, view, sem, sem, (d, t)).wait_send()
 
     def rows(start, size):
         return pl.ds(pl.multiple_of(start, 16), size)
@@ -296,8 +317,8 @@
         pl.semaphore_signal(barrier, inc=1, device_id=dev, device_id_type=MESH)
     pl.semaphore_wait(barrier, 6)
 
-    def a_rows(stage, s, a):
-        low, high, _, _ = route((s + a) % 2)
+    def a_rows(stage, parity, a):
+        low, high, _, _ = route(parity if a == 0 else 1 - parity)
         if stage == 0:
             return rows((c * 4 + high * 2 + low) * piece, piece)
         if stage == 1:
@@ -307,13 +328,12 @@
     def a_lanes(a):
         return pl.ds(CUTS[a][0], CUTS[a][1])
 
+    def a_any(stage, a):
+        return aw.at[0, 0 : (piece, 2 * piece, 4 * piece)[stage], a_lanes(a)]
+
     def za(k, a):
-        view = aw.at[t, a_rows(0, t, a), a_lanes(a)]
+        view = aw.at[t, a_rows(0, t0, a), a_lanes(a)]
         return rcopy(view, view, za_s.at[a, k - 1], za_r.at[a, t], (d, far(k)))
-
-    def za_wait(s, a):
-        view = aw.at[s, a_rows(0, s, a), a_lanes(a)]
-        rcopy(view, view, za_s.at[a, 0], za_r.at[a, s], (d, t)).wait_recv()
 
     def zb(k, which):
         dst = (bupa if which == 0 else qvba).at[t]
@@ -334,31 +354,34 @@
     for k in range(1, parts):
         zb(k, 0).start()
 
-    def ga(stage, s, a):
-        _, _, first, second = route((s + a) % 2)
-        view = aw.at[s, a_rows(stage, s, a), a_lanes(a)]
+    def ga(stage, s, parity, a):
+        _, _, first, second = route(parity if a == 0 else 1 - parity)
+        view = aw.at[s, a_rows(stage, parity, a), a_lanes(a)]
         dev = (first, second, dev_c)[stage]
         return rcopy(view, view, ga_s.at[stage, a, s], ga_r.at[stage, a, s], dev)
 
     def step_a(stage, i):
-        s = far(i + 1)
+        s, parity = far_bits(i + 1)
         for a in range(2):
             if stage == 0:
-                za_wait(s, a)
+                arrived(a_any(0, a), za_r.at[a, s])
             else:
-                ga(stage - 1, s, a).wait_recv()
-            ga(stage, s, a).start()
+                arrived(a_any(stage - 1, a), ga_r.at[stage - 1, a, s])
+            ga(stage, s, parity, a).start()
 
     n_far = (parts - 1) * nblk
 
     def far_block(m):
-        s = far(1 + m % (parts - 1))
-        j = m // (parts - 1)
-        return s, j, s * nblk + j
+        j = quotient(m, parts - 1, n_far)
+        s, parity = far_bits(1 + m - (parts - 1) * j)
+        return s, j, s * nblk + j, differ(parity, odd(j, nblk))
+
+    def own_parity(j):
+        return differ(t0, odd(j, nblk))
 
     def gf(stage, m):
-        s, j, b = far_block(m)
-        low, high, first, second = route((s + j) % 2)
+        _, _, b, par = far_block(m)
+        low, high, first, second = route(par)
         if stage == 0:
             view, dev = fg.at[b, :, rows((c * 4 + high * 2 + low) * piece, piece), :], first
         elif stage == 1:
@@ -367,20 +390,38 @@
             view, dev = fg.at[b, :, rows(c * 4 * piece, 4 * piece), :], dev_c
         return rcopy(view, view, gf_s.at[stage, b], gf_r.at[stage, b], dev)
 
-    def zf_wait(m):
-        s, j, b = far_block(m)
-        low, high, _, _ = route((s + j) % 2)
-        view = fg.at[b, :, rows((c * 4 + high * 2 + low) * piece, piece), :]
-        rcopy(view, view, zf_s.at[0], zf_r.at[b], (d, t)).wait_recv()
-
-    def within(n, size):
-        return (n >= 0) & (n < size)
+    def f_any(stage):
+        return fg.at[0, :, 0 : (piece, 2 * piece, 4 * piece)[stage], :]
 
     def step_g(stage, m):
+        b = far_block(m)[2]
+        if WIDE_FROM >= n_far:
+            if stage == 0:
+                arrived(f_any(0), zf_r.at[b])
+            else:
+                arrived(f_any(stage - 1), gf_r.at[stage - 1, b])
+            gf(stage, m).start()
+            return
         if stage == 0:
-            zf_wait(m)
+
+            @pl.when(m < WIDE_FROM)
+            def _():
+                arrived(f_any(0), zf_r.at[b])
+                gf(0, m).start()
+
+            return
+        if stage == 1:
+
+            @pl.when(m < WIDE_FROM)
+            def _():
+                arrived(f_any(0), gf_r.at[0, b])
+
+            @pl.when(m >= WIDE_FROM)
+            def _():
+                arrived(f_any(1), zf_r.at[b])
+
         else:
-            gf(stage - 1, m).wait_recv()
+            arrived(f_any(1), gf_r.at[1, b])
         gf(stage, m).start()
 
     n_all = parts * nblk
@@ -388,19 +429,20 @@
     def block(r):
         own = jnp.where(r < nblk, 1, 0)
         m = r - nblk
-        k = (1 - own) * (1 + m % (parts - 1))
-        j = own * r + (1 - own) * (m // (parts - 1))
-        s = far(k)
+        turn_j = quotient(m, parts - 1, n_far)
+        k = (1 - own) * (1 + m - (parts - 1) * turn_j)
+        j = own * r + (1 - own) * turn_j
+        s, parity = far_bits(k)
         home = s * nblk + j
-        return k, j, s, home, home + own * (n_all + j - home)
-
-    def rf(stage, r):
-        k, j, s, _, g = block(r)
-        low, high, first, second = route((s + j) % 2)
+        return k, j, s, home, home + own * (n_all + j - home), differ(parity, odd(j, nblk))
+
+    def rf(stage, r, slot=None):
+        k, j, s, _, g, par = block(r)
+        low, high, first, second = route(par)
         if stage == 0:
             return rcopy(
                 fg.at[g, :, rows((1 - c) * 4 * piece, 4 * piece), :],
-                rc_f.at[r % SLOTS_C],
+                rc_f.at[slot],
                 cf_s.at[r],
                 cf_r.at[r],
                 dev_c,
@@ -433,29 +475,29 @@
     def add_rows(ref, got):
         ref[...] = (ref[...].astype(F32) + got[...].astype(F32)).astype(BF16)
 
-    def rf_core(r):
-        _, _, _, _, g = block(r)
-        rf(0, r).wait_recv()
-        add_rows(fg.at[g, :, rows(c * 4 * piece, 4 * piece), :], rc_f.at[r % SLOTS_C])
+    def rf_core(r, slot):
+        g = block(r)[4]
+        arrived(rc_f.at[slot], cf_r.at[r])
+        add_rows(fg.at[g, :, rows(c * 4 * piece, 4 * piece), :], rc_f.at[slot])
 
         @pl.when(r < n_all - SLOTS_C)
         def _():
             pl.semaphore_signal(credit, inc=1, device_id=dev_c, device_id_type=MESH)
 
     def turn(i):
-        return (i + nblk) % n_all
+        return i + nblk - n_all * jnp.where(i >= n_all - nblk, 1, 0)
 
     def rf_first(r):
-        k, j, s, _, g = block(r)
-        low, high, _, _ = route((s + j) % 2)
-        rf(1, r).wait_recv()
+        _, _, _, _, g, par = block(r)
+        _, high, _, _ = route(par)
+        arrived(r2_f.at[r], f2_r.at[r])
         add_rows(fg.at[g, :, rows((c * 4 + high * 2) * piece, 2 * piece), :], r2_f.at[r])
         rf(2, r).start()
 
     def rf_far(r):
-        k, j, s, _, g = block(r)
-        low, high, _, _ = route((s + j) % 2)
-        rf(2, r).wait_recv()
+        _, _, _, _, g, par = block(r)
+        low, high, _, _ = route(par)
+        arrived(r1_f.at[r], f1_r.at[r])
         add_rows(fg.at[g, :, rows((c * 4 + high * 2 + low) * piece, piece), :], r1_f.at[r])
 
         @pl.when(r >= nblk)
@@ -463,7 +505,7 @@
             rf(3, r).start()
 
     def af(stage, j):
-        low, high, first, second = route((t + j) % 2)
+        low, high, first, second = route(own_parity(j))
         b = t * nblk + j
         if stage == 0:
             view, dev = fg.at[b, :, rows((c * 4 + high * 2 + low) * piece, piece), :], first
@@ -474,12 +516,12 @@
         return rcopy(view, view, af_s.at[stage, j], af_r.at[stage, j], dev)
 
     def f_final(j):
-        low, high, _, _ = route((t + j) % 2)
+        low, high, _, _ = route(own_parity(j))
         mine = rows((c * 4 + high * 2 + low) * piece, piece)
         total = fg[n_all + j, :, mine, :].astype(F32)
         for k in range(1, parts):
             z = (k - 1) * nblk + j
-            rcopy(rz_f.at[z], rz_f.at[z], fz_s.at[z], fz_r.at[z], (d, t)).wait_recv()
+            arrived(rz_f.at[z], fz_r.at[z])
             total = total + rz_f[z].astype(F32)
         fg[t * nblk + j, :, mine, :] = total.astype(BF16)
         af(0, j).start()
@@ -496,27 +538,31 @@
         )
 
     def f_second(j):
-        af(0, j).wait_recv()
+        arrived(f_any(0), af_r.at[0, j])
         af(1, j).start()
 
     def f_third(j):
-        af(1, j).wait_recv()
+        arrived(f_any(1), af_r.at[1, j])
         af(2, j).start()
 
-    def ra_view(stage, s, a):
-        low, high, first, second = route((s + a) % 2)
+    def group_bits(it):
+        n = it + 1
+        return far_bits(n - parts * quotient(n, parts, 2 * parts + 1))
+
+    def group_of(it):
+        return group_bits(it)[0]
+
+    def ra(stage, q, a):
+        s, parity = group_bits(q)
+        low, high, first, second = route(parity if a == 0 else 1 - parity)
         if stage == 0:
-            return rows((1 - c) * 4 * piece, 4 * piece), rc_a, dev_c
-        if stage == 1:
-            return rows((c * 4 + (1 - high) * 2) * piece, 2 * piece), r2_a, second
-        if stage == 2:
-            return rows((c * 4 + high * 2 + 1 - low) * piece, piece), r1_a, first
-        return rows((c * 4 + high * 2 + low) * piece, piece), rz_a, (d, s)
-
-    def ra(stage, q, a):
-        s = group_of(q)
-        where, buf, dev = ra_view(stage, s, a)
-        if stage == 3:
+            where, buf, dev = rows((1 - c) * 4 * piece, 4 * piece), rc_a, dev_c
+        elif stage == 1:
+            where, buf, dev = rows((c * 4 + (1 - high) * 2) * piece, 2 * piece), r2_a, second
+        elif stage == 2:
+            where, buf, dev = rows((c * 4 + high * 2 + 1 - low) * piece, piece), r1_a, first
+        else:
+            where, buf, dev = rows((c * 4 + high * 2 + low) * piece, piece), rz_a, (d, s)
             q = jnp.minimum(q, parts - 2)
         return rcopy(
             aw.at[s, where, a_lanes(a)],
@@ -526,19 +572,13 @@
             dev,
         )
 
-    def ra_add(stage, q, a):
-        s = group_of(q)
-        buf = (rc_a, r2_a, r1_a)[stage]
-        ra(stage, q, a).wait_recv()
-        add_rows(aw.at[s, a_rows(2 - stage, s, a), a_lanes(a)], buf.at[q, :, a_lanes(a)])
-
-    def group_of(it):
-        return far((it + 1) % parts)
-
     def step_b(stage, q):
+        s, parity = group_bits(q)
+        buf = (rc_a, r2_a, r1_a)[stage - 1]
         for a in range(2):
-            ra_add(stage - 1, q, a)
-        for a in range(2):
+            view = buf.at[q, :, a_lanes(a)]
+            arrived(view, ra_r.at[stage - 1, a, q])
+            add_rows(aw.at[s, a_rows(3 - stage, parity, a), a_lanes(a)], view)
             if stage < 3:
                 ra(stage, q, a).start()
             else:
@@ -572,19 +612,24 @@
 
         lax.fori_loop(low, high, one, 0)
 
-    def advance(place, idx=0):
-        for name, counts in PLAN[place]:
-            if len(counts) == 2:
-                repeat(name, counts[0], counts[1])
-                continue
-            low = counts[0]
-            high = counts[0]
-            for i in range(1, len(counts)):
-                more = counts[i] - counts[i - 1]
-                if more:
-                    low = low + jnp.where(idx >= i, more, 0)
-                    high = high + jnp.where(idx >= i - 1, more, 0)
+    def advance(place, idx=None, reached=None):
+        after = []
+        for n, (name, counts) in enumerate(PLAN[place]):
+            low = counts[0] if reached is None else reached[n]
+            high = low
+            if idx is None:
+                high = counts[-1]
+            else:
+                for i in range(len(counts) - 1):
+                    more = counts[i + 1] - counts[i]
+                    if more:
+                        high = high + jnp.where(idx == i, more, 0)
             repeat(name, low, high)
+            after.append(high)
+        return tuple(after)
+
+    def begin(place):
+        return tuple(jnp.int32(counts[0]) for _, counts in PLAN[place])
 
     gain1 = g1_ref[...][None, :]
     shift1 = s1_ref[...][None, :]
@@ -593,8 +638,11 @@
     advance("p0")
 
     def zf(k, j):
-        low, high, _, _ = route((t + j) % 2)
-        view = fg.at[t * nblk + j, :, rows((c * 4 + high * 2 + low) * piece, piece), :]
+        low, high, _, _ = route(own_parity(j))
+        where = rows((c * 4 + high * 2 + low) * piece, piece)
+        if j * (parts - 1) + k - 1 >= WIDE_FROM:
+            where = rows((c * 4 + high * 2) * piece, 2 * piece)
+        view = fg.at[t * nblk + j, :, where, :]
         return rcopy(
             view, view, zf_s.at[(k - 1) * nblk + j], zf_r.at[t * nblk + j], (d, far(k))
         )
@@ -682,7 +730,7 @@
     def att_forward(k, half):
         s = far(k)
         base = half * share
-        buf = k % 2
+        buf = odd(k, parts)
         if half == 1:
             for h in range(heads):
                 p_out(s, h, half, buf).wait()
@@ -739,7 +787,7 @@
         def _():
             zb_wait(s, 1)
             for a in range(2):
-                ga(2, s, a).wait_recv()
+                arrived(a_any(2, a), ga_r.at[2, a, s])
 
         project(s, 0, True)
 
@@ -748,10 +796,9 @@
             advance("pj")
 
         att_forward(k, 0)
-        advance("o", k)
-        return carry
-
-    lax.fori_loop(0, parts, own_keys, 0)
+        return advance("o", k, carry)
+
+    lax.fori_loop(0, parts, own_keys, begin("o"))
 
     x_copy.wait_recv()
     unit, _ = unit_of(xp[...].astype(F32))
@@ -760,10 +807,9 @@
     def pair_keys(k, carry):
         project(far(k), 1, False)
         att_forward(k, 1)
-        advance("q", k)
-        return carry
-
-    lax.fori_loop(0, parts, pair_keys, 0)
+        return advance("q", k, carry)
+
+    lax.fori_loop(0, parts, pair_keys, begin("q"))
     for buf in range(2):
         for h in range(heads):
             p_out(0, h, 1, buf).wait()
@@ -793,17 +839,12 @@
         zb_wait(far(k), 0)
     advance("mid")
 
-    def drain_zf(m, carry):
-        view = fg.at[0, :, 0:piece, :]
-        rcopy(view, view, zf_s.at[m], zf_r.at[0], (d, t)).wait_send()
-        return carry
-
     def ffn(r, carry):
-        k, j, s, home, g = block(r)
+        k, j, s, home, g, _ = block(r)
 
         @pl.when(k > 0)
         def _():
-            gf(2, jnp.maximum(r - nblk, 0)).wait_recv()
+            arrived(f_any(2), gf_r.at[2, home])
 
         wu = fg[home, 0]
         wd = fg[home, 1]
@@ -821,31 +862,36 @@
 
         @pl.when(k > 0)
         def _():
-            for stage in range(3):
-                gf(stage, jnp.maximum(r - nblk, 0)).wait_send()
+            for stage in (1, 2):
+                left(f_any(stage), gf_s.at[stage, home])
+
+        @pl.when((k > 0) & (r - nblk < WIDE_FROM))
+        def _():
+            left(f_any(0), gf_s.at[0, home])
 
         fg[g, 0] = up_grad
         fg[g, 1] = dn_grad
 
-        @pl.when(r == 2 * nblk)
+        @pl.when(r == 3 * nblk - 1)
         def _():
-            lax.fori_loop(0, n_far, drain_zf, 0)
+            for m in range(n_far):
+                zf(1 + m % (parts - 1), m // (parts - 1)).wait_send()
 
         @pl.when(r >= SLOTS_C)
         def _():
             pl.semaphore_wait(credit, 1)
 
-        rf(0, r).start()
+        slot = odd(r, n_all)
+        rf(0, r, slot).start()
 
         @pl.when(r > 0)
         def _():
-            rf_core(r - 1)
-
-        advance("r", r)
-        return carry
-
-    lax.fori_loop(0, n_all, ffn, 0)
-    rf_core(n_all - 1)
+            rf_core(r - 1, 1 - slot)
+
+        return advance("r", r, carry)
+
+    lax.fori_loop(0, n_all, ffn, begin("r"))
+    rf_core(n_all - 1, (n_all - 1) % SLOTS_C)
 
     middle = mid[...]
     ngs[...] = (middle + (acc0[...] + bdn_ref[...][None, :])).astype(BF16)
@@ -870,7 +916,7 @@
         for a in range(2):
             za(k, a).wait_send()
             for stage in range(3):
-                ga(stage, far(k), a).wait_send()
+                left(a_any(stage, a), ga_s.at[stage, a, far(k)])
     advance("ln")
 
     head_row = lax.broadcasted_iota(jnp.int32, (hw, 128), 0)
@@ -888,10 +934,9 @@
         delta = nn(coarse, pick) + nn(fine, pick)
         stat[s] = jnp.where((lane_n >= at2) & (lane_n < at2 + heads), delta, stat[s])
         aw[s, qkvw : 4 * hw, :] = nn(mixed.T, ol[...]).astype(BF16)
-        advance("k", k)
-        return carry
-
-    lax.fori_loop(0, parts, out_back, 0)
+        return advance("k", k, carry)
+
+    lax.fori_loop(0, parts, out_back, begin("k"))
 
     def p_in(s, h, half, buf):
         return pltpu.make_async_copy(
@@ -900,12 +945,12 @@
 
     def fetch(it):
         for h in range(heads):
-            p_in(group_of(it), h, 1 - it // parts, it % 2).start()
+            p_in(group_of(it), h, 1 - quotient(it, parts, 2 * parts), odd(it, 2 * parts)).start()
 
     def att_group(it, half):
         s = group_of(it)
         base = half * share
-        buf = it % 2
+        buf = odd(it, 2 * parts)
 
         @pl.when(it + 1 < 2 * parts)
         def _():
@@ -966,16 +1011,16 @@
         back = uu[s, hw:qkvw, 0:share].T
         acc0[...] += nn(back, aw[s, hw:qkvw, :])
         late[pl.ds(2 * s + 1, 1), 0:hw] = row_sums(back[:, hw : 2 * hw])
-        advance("h", it)
-        return carry
-
-    lax.fori_loop(0, parts, pair_half, 0)
+        return advance("h", it, carry)
+
+    lax.fori_loop(0, parts, pair_half, begin("h"))
 
     ng_copy = rcopy(ngs, ngr, ng_sem.at[0], ng_sem.at[1], (d, tp))
     pair_grad = acc0[...]
     lo_copy.wait()
     ngs[...] = pair_grad.astype(BF16)
-    ng_copy.start()
+    if NG_PLACE == 0:
+        ng_copy.start()
     unit, _ = unit_of(xp[...].astype(F32))
     late[8:9, :] = jnp.sum(pair_grad * unit, axis=0, keepdims=True)
     late[9:10, :] = jnp.sum(pair_grad, axis=0, keepdims=True)
@@ -1026,7 +1071,12 @@
         ).astype(BF16)
         for a in range(2):
             ra(0, q, a).start()
-        advance("w", q)
+        carry = advance("w", q, carry)
+        if NG_PLACE > 0:
+
+            @pl.when(q == NG_PLACE - 1)
+            def _():
+                ng_copy.start()
 
         for stage in range(3):
 
@@ -1036,7 +1086,7 @@
 
         return carry
 
-    lax.fori_loop(parts, 2 * parts, own_half, 0)
+    lax.fori_loop(parts, 2 * parts, own_half, begin("w"))
 
     own_grad = acc1[...]
     unit, scale_inv = unit_of(x_ref[...].astype(F32))
@@ -1047,14 +1097,14 @@
     xg_copy = pltpu.make_async_copy(mid, xg_ref, loc_sem.at[nblk])
 
     def aa(stage, a):
-        _, _, first, second = route((t + a) % 2)
-        view = done.at[a_rows(stage, t, a), a_lanes(a)]
+        _, _, first, second = route(t0 if a == 0 else 1 - t0)
+        view = done.at[a_rows(stage, t0, a), a_lanes(a)]
         dev = (first, second, dev_c)[stage]
         return rcopy(view, view, aa_s.at[stage, a], aa_r.at[stage, a], dev)
 
     def att_final():
         for a in range(2):
-            mine = a_rows(0, t, a)
+            mine = a_rows(0, t0, a)
             low = CUTS[a][0]
             high = low + CUTS[a][1]
             total = aw[t, mine, low:high].astype(F32)
@@ -1125,21 +1175,22 @@
     ng_copy.wait_send()
 
     def drain_far(m, carry):
-        rf(3, m + nblk).wait_send()
+        left(f_any(0), fz_s.at[m])
         return carry
 
     lax.fori_loop(0, n_far, drain_far, 0)
 
     def drain_all(r, carry):
-        for stage in range(3):
-            rf(stage, r).wait_send()
+        left(f_any(2), cf_s.at[r])
+        left(f_any(1), f2_s.at[r])
+        left(f_any(0), f1_s.at[r])
         return carry
 
     lax.fori_loop(0, n_all, drain_all, 0)
 
     def drain_own(j, carry):
         for stage in range(3):
-            af(stage, j).wait_send()
+            left(f_any(stage), af_s.at[stage, j])
         return carry
 
     lax.fori_loop(0, nblk, drain_own, 0)
@@ -1151,9 +1202,9 @@
     for q in range(parts):
         for a in range(2):
             for stage in range(3):
-                ra(stage, q, a).wait_send()
+                left(a_any(2 - stage, a), ra_s.at[stage, a, q])
             if q < parts - 1:
-                ra(3, q, a).wait_send()
+                left(a_any(0, a), ra_s.at[3, a, q])
     for a in range(2):
         aa(2, a).wait_recv()
     oa_copy = pltpu.make_async_copy(done, oa_ref, loc_sem.at[nblk + 1])
@@ -1199,37 +1250,39 @@
 ):
     hw = out_out.shape[0]
     qkvw = qkv_out.shape[0]
+    jobs = []
+    for n, (src, mid_b, wide, dst) in enumerate(
+        ((up, up_b, up_f, up_out), (dn, dn_b, dn_f, dn_out), (at, at_b, at_f, None))
+    ):
+        size = src.shape[0] // CHUNKS
+        for i in range(CHUNKS):
+            part = pl.ds(i * size, size)
+            if dst is not None:
+                to = dst.at[part, :]
+            elif (i + 1) * size <= qkvw:
+                to = qkv_out.at[part, :]
+            else:
+                to = out_out.at[pl.ds(i * size - qkvw, size), :]
+            jobs.append((src.at[part, :], mid_b.at[part, :], wide.at[part, :], to))
+    jobs.append((xg, xg_b, None, xg_out))
+    jobs.append((lo, lo_b, None, lo_out))
     ins = [
-        pltpu.make_async_copy(src, dst, in_sem.at[i])
-        for i, (src, dst) in enumerate(((up, up_b), (dn, dn_b), (at, at_b), (xg, xg_b), (lo, lo_b)))
+        pltpu.make_async_copy(job[0], job[1], in_sem.at[i]) for i, job in enumerate(jobs)
     ]
     for cp in ins:
         cp.start()
-    outs = []
-
-    def send(src, dst):
-        outs.append(pltpu.make_async_copy(src, dst, out_sem.at[len(outs)]))
-        outs[-1].start()
-
     for i, ref in enumerate((g2_out, s2_out, bo_out, bd_out, g1_out, s1_out)):
         ref[...] = sm[i]
     qv_out[...] = sm[8:10, 0:hw]
     for j in range(bup_out.shape[0] // BLK):
         bup_out[j * BLK : (j + 1) * BLK] = sm[16 + j, 0:BLK]
-    ins[0].wait()
-    up_f[...] = up_b[...].astype(F32)
-    send(up_f, up_out)
-    ins[1].wait()
-    dn_f[...] = dn_b[...].astype(F32)
-    send(dn_f, dn_out)
-    ins[2].wait()
-    at_f[...] = at_b[...].astype(F32)
-    send(at_f.at[pl.ds(0, qkvw), :], qkv_out)
-    send(at_f.at[pl.ds(qkvw, hw), :], out_out)
-    ins[3].wait()
-    send(xg_b, xg_out)
-    ins[4].wait()
-    send(lo_b, lo_out)
+    outs = []
+    for i, (_, got, wide, dst) in enumerate(jobs):
+        ins[i].wait()
+        if wide is not None:
+            wide[...] = got[...].astype(F32)
+        outs.append(pltpu.make_async_copy(got if wide is None else wide, dst, out_sem.at[i]))
+        outs[-1].start()
     for cp in outs:
         cp.wait()
 
@@ -1410,8 +1463,8 @@
             pltpu.VMEM((width, fw), F32),
             pltpu.VMEM((fw, width), F32),
             pltpu.VMEM((width, width), F32),
-            dma((5,)),
-            dma((7,)),
+            dma((3 * CHUNKS + 2,)),
+            dma((3 * CHUNKS + 2,)),
         ],
     )(layer_out, x_grad, up, down, att, small)
     layer_out, x_grad, g_up, g_down, g_qkv, g_out, g2, s2, bo, bd, g1, s1, g_qv, g_bup = outs

time: 209 us -> 207 us (level)
  no operation moved by 1% of the time
where the time goes in v4:
time: 207 us
  Pallas kernels  206 us (100%)
    pallas_call x1, Pallas kernels, local(): pl.pallas_call(kernel, out_shape=[jax.ShapeDtypeStruct((share, width), BF...  199 us
    pallas_call x1, Pallas kernels, local(): pl.pallas_call(finish, out_shape=[jax.ShapeDtypeStruct((share, width), BF...  7.1 us

profile of v4, /device:TPU:0, one launch (start us, length us, event | category | flops | bytes accessed | tf_op | source)
XLA Modules:
  0.0 207.2 jit_solution(11609867802318844315)
XLA Ops:
  1.3 198.7 %shard_map.272 = (bf16[512,640]{1,0:T(8,128)(2,1)}, f32[512,640]{1,0:T(8,128)}, bf16[640,1280]{1,0:T(8,128)(2,1)}, bf16[1280,640]{1,0:T(8,128)(2,1)}, bf16[640,6...) custom-call(bf16[512,640]{1,0:T(8,128)(2,1)} %x_ref.1, bf16[512,640]{1,0:T(8,128)(2,1)} %cot_ref.1, ...), custom_call_target="tpu_custom_call" | custom-call | tf_op jit(solution)/shard_map/pallas_call | solution.py:1392
  200.0 7.1 %shard_map.273 = (bf16[512,640]{1,0:T(8,128)(2,1)}, f32[512,640]{1,0:T(8,128)}, f32[640,1280]{1,0:T(8,128)}, f32[1280,640]{1,0:T(8,128)}, f32[480,640]{1,0:T(8,1...) custom-call(bf16[512,640]{1,0:T(8,128)(2,1)} %get-tuple-element.34.l, ...), custom_call_target="tpu_custom_call" | custom-call | tf_op jit(solution)/shard_map/pallas_call | solution.py:1437

commit v5 on v4

--- a/solution.py
+++ b/solution.py
@@ -22,7 +22,8 @@
 SLOTS_C = 2
 X_PLACE = 0
 WIDE_FROM = 15
-NG_PLACE = 2
+NG_PLACE = 1
+EARLY_FAR = 3
 CUTS = ((0, 256), (256, 384))
 CHUNKS = 4
 PLAN = {
@@ -31,65 +32,66 @@
         ("a1", (0, 1)),
     ),
     "p1": (
-        ("a0", (1, 2)),
+        ("a0", (1, 3)),
+        ("a2", (0, 1)),
     ),
     "p2": (
-        ("a0", (2, 3)),
         ("a1", (1, 3)),
-        ("a2", (0, 3)),
+        ("a2", (1, 3)),
     ),
     "pj": (
     ),
     "o": (
     ),
     "q": (
-        ("g0", (0, 4, 12, 12, 15)),
-        ("g1", (0, 0, 0, 5, 8)),
+        ("g0", (0, 0, 11, 14, 15)),
+        ("g1", (0, 0, 0, 0, 8)),
     ),
     "mid": (
         ("g1", (8, 10)),
-        ("g2", (0, 3)),
     ),
     "r": (
-        ("g1", (10, 13, 15, 15, 15, 15, 15, 15, 15, 15, 15, 15, 15, 15, 15, 15, 15, 15, 15, 15, 15)),
-        ("g2", (3, 3, 5, 5, 6, 9, 10, 13, 15, 15, 15, 15, 15, 15, 15, 15, 15, 15, 15, 15, 15)),
-        ("rf", (0, 0, 0, 0, 0, 0, 0, 0, 0, 0, 0, 0, 0, 1, 1, 1, 1, 1, 2, 2, 3)),
-        ("r1", (0, 0, 0, 0, 0, 0, 0, 0, 0, 0, 1, 2, 2, 2, 2, 3, 3, 5, 5, 6, 6)),
-        ("r2", (0, 0, 0, 0, 0, 0, 0, 1, 2, 3, 4, 5, 6, 6, 8, 8, 9, 11, 12, 12, 12)),
+        ("g1", (10, 11, 15, 15, 15, 15, 15, 15, 15, 15, 15, 15, 15, 15, 15, 15, 15, 15, 15, 15, 15)),
+        ("g2", (0, 0, 3, 3, 5, 8, 9, 9, 9, 11, 13, 15, 15, 15, 15, 15, 15, 15, 15, 15, 15)),
+        ("rf", (0, 0, 0, 0, 0, 0, 0, 0, 0, 0, 0, 0, 0, 0, 0, 2, 2, 4, 4, 5, 5)),
+        ("r1", (0, 0, 0, 0, 0, 0, 0, 0, 0, 0, 0, 0, 0, 2, 3, 3, 4, 4, 5, 5, 7)),
+        ("r2", (0, 0, 0, 0, 0, 0, 0, 1, 2, 3, 4, 4, 4, 6, 8, 8, 10, 11, 12, 13, 14)),
     ),
     "ln": (
-        ("rf", (3, 4)),
+        ("rf", (5, 7)),
+        ("r2", (14, 16)),
     ),
     "k": (
-        ("rf", (4, 4, 4, 5, 5)),
-        ("r1", (6, 10, 10, 10, 10)),
-        ("r2", (12, 13, 14, 17, 17)),
+        ("rf", (7, 7, 8, 8, 9)),
+        ("r1", (7, 9, 9, 9, 9)),
+        ("r2", (16, 16, 16, 20, 20)),
     ),
     "h": (
-        ("rf", (5, 5, 5, 9, 12)),
-        ("r1", (10, 11, 12, 17, 18)),
-        ("r2", (17, 18, 19, 19, 20)),
+        ("rf", (9, 9, 9, 11, 17)),
+        ("r1", (9, 14, 16, 17, 17)),
+        ("f0", (0, 0, 0, 0, 2)),
     ),
     "w": (
-        ("rf", (12, 18, 19, 20, 20)),
-        ("r1", (18, 20, 20, 20, 20)),
-        ("b3", (0, 0, 0, 0, 1)),
-        ("b2", (0, 0, 1, 1, 3)),
-        ("b1", (0, 1, 1, 3, 4)),
-        ("f0", (0, 3, 4, 5, 5)),
-        ("f1", (0, 0, 2, 3, 5)),
+        ("rf", (17, 17, 19, 19, 20)),
+        ("r1", (17, 20, 20, 20, 20)),
+        ("b3", (0, 0, 0, 0, 2)),
+        ("b2", (0, 0, 0, 2, 3)),
+        ("b1", (0, 0, 2, 3, 4)),
+        ("f0", (2, 2, 3, 3, 5)),
+        ("f1", (0, 1, 1, 3, 3)),
+        ("f2", (0, 0, 0, 0, 3)),
     ),
 }
 TAIL = (
-    ("b3", 1, 3),
     ("b2", 3, 4),
     ("v", 0, 0),
+    ("f1", 3, 5),
+    ("b3", 2, 4),
     ("v", 0, 0),
-    ("b3", 3, 4),
     ("aa0", 0, 0),
-    ("f2", 0, 5),
     ("v", 0, 0),
     ("aa1", 0, 0),
+    ("f2", 3, 5),
     ("ng", 0, 0),
     ("aa2", 0, 0),
 )
@@ -464,9 +466,17 @@
                 first,
             )
         z = jnp.maximum((k - 1) * nblk + j, 0)
+        if stage == 4:
+            return rcopy(
+                fg.at[g, :, rows((c * 4 + high * 2) * piece, 2 * piece), :],
+                rz_f.at[z],
+                fz_s.at[z],
+                fz_r.at[z],
+                (d, s),
+            )
         return rcopy(
             fg.at[g, :, rows((c * 4 + high * 2 + low) * piece, piece), :],
-            rz_f.at[z],
+            rz_f.at[z, :, 0:piece, :],
             fz_s.at[z],
             fz_r.at[z],
             (d, s),
@@ -488,19 +498,39 @@
         return i + nblk - n_all * jnp.where(i >= n_all - nblk, 1, 0)
 
     def rf_first(r):
-        _, _, _, _, g, par = block(r)
+        _, j, _, _, g, par = block(r)
         _, high, _, _ = route(par)
+        both = fg.at[g, :, rows((c * 4 + high * 2) * piece, 2 * piece), :]
         arrived(r2_f.at[r], f2_r.at[r])
-        add_rows(fg.at[g, :, rows((c * 4 + high * 2) * piece, 2 * piece), :], r2_f.at[r])
-        rf(2, r).start()
+        add_rows(both, r2_f.at[r])
+
+        @pl.when((j < EARLY_FAR) & (r >= nblk))
+        def _():
+            rf(4, r).start()
+
+        @pl.when((j < EARLY_FAR) & (r < nblk))
+        def _():
+            total = both[...].astype(F32)
+            for k in range(1, parts):
+                z = (k - 1) * nblk + j
+                arrived(rz_f.at[z], fz_r.at[z])
+                total = total + rz_f[z].astype(F32)
+            both[...] = total.astype(BF16)
+
+        @pl.when((j >= EARLY_FAR) | (r < nblk))
+        def _():
+            rf(2, r).start()
 
     def rf_far(r):
-        _, _, _, _, g, par = block(r)
+        _, j, _, _, g, par = block(r)
         low, high, _, _ = route(par)
-        arrived(r1_f.at[r], f1_r.at[r])
-        add_rows(fg.at[g, :, rows((c * 4 + high * 2 + low) * piece, piece), :], r1_f.at[r])
-
-        @pl.when(r >= nblk)
+
+        @pl.when((j >= EARLY_FAR) | (r < nblk))
+        def _():
+            arrived(r1_f.at[r], f1_r.at[r])
+            add_rows(fg.at[g, :, rows((c * 4 + high * 2 + low) * piece, piece), :], r1_f.at[r])
+
+        @pl.when((j >= EARLY_FAR) & (r >= nblk))
         def _():
             rf(3, r).start()
 
@@ -518,12 +548,20 @@
     def f_final(j):
         low, high, _, _ = route(own_parity(j))
         mine = rows((c * 4 + high * 2 + low) * piece, piece)
-        total = fg[n_all + j, :, mine, :].astype(F32)
-        for k in range(1, parts):
-            z = (k - 1) * nblk + j
-            arrived(rz_f.at[z], fz_r.at[z])
-            total = total + rz_f[z].astype(F32)
-        fg[t * nblk + j, :, mine, :] = total.astype(BF16)
+
+        @pl.when(j < EARLY_FAR)
+        def _():
+            fg[t * nblk + j, :, mine, :] = fg[n_all + j, :, mine, :]
+
+        @pl.when(j >= EARLY_FAR)
+        def _():
+            total = fg[n_all + j, :, mine, :].astype(F32)
+            for k in range(1, parts):
+                z = (k - 1) * nblk + j
+                arrived(rz_f.at[z, :, 0:piece, :], fz_r.at[z])
+                total = total + rz_f[z, :, 0:piece, :].astype(F32)
+            fg[t * nblk + j, :, mine, :] = total.astype(BF16)
+
         af(0, j).start()
 
     def f_out(j, which):
@@ -1174,16 +1212,16 @@
     x_copy.wait_send()
     ng_copy.wait_send()
 
-    def drain_far(m, carry):
-        left(f_any(0), fz_s.at[m])
-        return carry
-
-    lax.fori_loop(0, n_far, drain_far, 0)
+    for j in range(nblk):
+        for k in range(1, parts):
+            left(f_any(1 if j < EARLY_FAR else 0), fz_s.at[(k - 1) * nblk + j])
+    for r in range(n_all):
+        if r < nblk or (r - nblk) // (parts - 1) >= EARLY_FAR:
+            left(f_any(0), f1_s.at[r])
 
     def drain_all(r, carry):
         left(f_any(2), cf_s.at[r])
         left(f_any(1), f2_s.at[r])
-        left(f_any(0), f1_s.at[r])
         return carry
 
     lax.fori_loop(0, n_all, drain_all, 0)
@@ -1326,7 +1364,7 @@
         pltpu.VMEM((SLOTS_C, 2, 4 * piece, BLK), BF16),
         pltpu.VMEM((n_all, 2, 2 * piece, BLK), BF16),
         pltpu.VMEM((n_all, 2, piece, BLK), BF16),
-        pltpu.VMEM((n_far, 2, piece, BLK), BF16),
+        pltpu.VMEM((n_far, 2, 2 * piece, BLK), BF16),
         pltpu.VMEM((parts, 4 * piece, 4 * hw), BF16),
         pltpu.VMEM((parts, 2 * piece, 4 * hw), BF16),
         pltpu.VMEM((parts, piece, 4 * hw), BF16),

time: 207 us -> 203 us (0.981); the launches traced: 207 us -> 201 us
  Pallas kernels: 206 us -> 200 us
    pallas_call x1, Pallas kernels: 199 us -> 192 us  [local(): pl.pallas_call(kernel, out_shape=[jax.ShapeDtypeStruct((share, width), BF...]
where the time goes in v5:
time: 203 us; the launch traced here: 201 us
  Pallas kernels  200 us (99%)
    pallas_call x1, Pallas kernels, local(): pl.pallas_call(kernel, out_shape=[jax.ShapeDtypeStruct((share, width), BF...  192 us
    pallas_call x1, Pallas kernels, local(): pl.pallas_call(finish, out_shape=[jax.ShapeDtypeStruct((share, width), BF...  7.1 us

profile of v5, /device:TPU:0, one launch (start us, length us, event | category | flops | bytes accessed | tf_op | source)
XLA Modules:
  0.0 201.1 jit_solution(15338584876958782100)
XLA Ops:
  1.3 192.5 %shard_map.272 = (bf16[512,640]{1,0:T(8,128)(2,1)}, f32[512,640]{1,0:T(8,128)}, bf16[640,1280]{1,0:T(8,128)(2,1)}, bf16[1280,640]{1,0:T(8,128)(2,1)}, bf16[640,6...) custom-call(bf16[512,640]{1,0:T(8,128)(2,1)} %x_ref.1, bf16[512,640]{1,0:T(8,128)(2,1)} %cot_ref.1, ...), custom_call_target="tpu_custom_call" | custom-call | tf_op jit(solution)/shard_map/pallas_call | solution.py:1430
  193.8 7.1 %shard_map.273 = (bf16[512,640]{1,0:T(8,128)(2,1)}, f32[512,640]{1,0:T(8,128)}, f32[640,1280]{1,0:T(8,128)}, f32[1280,640]{1,0:T(8,128)}, f32[480,640]{1,0:T(8,1...) custom-call(bf16[512,640]{1,0:T(8,128)(2,1)} %get-tuple-element.34.l, ...), custom_call_target="tpu_custom_call" | custom-call | tf_op jit(solution)/shard_map/pallas_call | solution.py:1475

commit v6 on v5

--- a/solution.py
+++ b/solution.py
@@ -52,10 +52,10 @@
     ),
     "r": (
         ("g1", (10, 11, 15, 15, 15, 15, 15, 15, 15, 15, 15, 15, 15, 15, 15, 15, 15, 15, 15, 15, 15)),
-        ("g2", (0, 0, 3, 3, 5, 8, 9, 9, 9, 11, 13, 15, 15, 15, 15, 15, 15, 15, 15, 15, 15)),
-        ("rf", (0, 0, 0, 0, 0, 0, 0, 0, 0, 0, 0, 0, 0, 0, 0, 2, 2, 4, 4, 5, 5)),
-        ("r1", (0, 0, 0, 0, 0, 0, 0, 0, 0, 0, 0, 0, 0, 2, 3, 3, 4, 4, 5, 5, 7)),
-        ("r2", (0, 0, 0, 0, 0, 0, 0, 1, 2, 3, 4, 4, 4, 6, 8, 8, 10, 11, 12, 13, 14)),
+        ("g2", (0, 0, 3, 3, 5, 8, 8, 9, 9, 11, 13, 15, 15, 15, 15, 15, 15, 15, 15, 15, 15)),
+        ("rf", (0, 0, 0, 0, 0, 0, 0, 0, 0, 0, 0, 0, 0, 0, 0, 0, 0, 4, 4, 5, 5)),
+        ("r1", (0, 0, 0, 0, 0, 0, 0, 0, 0, 0, 0, 0, 0, 2, 2, 3, 4, 4, 5, 5, 7)),
+        ("r2", (0, 0, 0, 0, 0, 0, 0, 1, 2, 3, 4, 5, 6, 7, 8, 8, 10, 11, 12, 13, 14)),
     ),
     "ln": (
         ("rf", (5, 7)),
@@ -280,6 +280,10 @@
     def rows(start, size):
         return pl.ds(pl.multiple_of(start, 16), size)
 
+    barrier = pltpu.get_barrier_semaphore()
+    for dev in (dev_c, (dx, t), (dy, t), (d, far(1)), (d, far(2)), (d, far(3))):
+        pl.semaphore_signal(barrier, inc=1, device_id=dev, device_id_type=MESH)
+
     def up_load(j):
         return pltpu.make_async_copy(
             wup_ref.at[:, pl.ds(j * BLK, BLK)], fg.at[t * nblk + j, 0], loc_sem.at[j]
@@ -314,9 +318,6 @@
     bupa[t] = bup_ref[...][None, :]
     qvba[t] = qvb_ref[...]
 
-    barrier = pltpu.get_barrier_semaphore()
-    for dev in (dev_c, (dx, t), (dy, t), (d, far(1)), (d, far(2)), (d, far(3))):
-        pl.semaphore_signal(barrier, inc=1, device_id=dev, device_id_type=MESH)
     pl.semaphore_wait(barrier, 6)
 
     def a_rows(stage, parity, a):
@@ -1158,11 +1159,62 @@
             aa(stage - 1, a).wait_recv()
             aa(stage, a).start()
 
+    halves = [
+        pltpu.make_async_copy(
+            done.at[rows(n * 4 * piece, 4 * piece), :],
+            oa_ref.at[rows(n * 4 * piece, 4 * piece), :],
+            loc_sem.at[nblk + 1 + 3 * i],
+        )
+        for i, n in enumerate((c, 1 - c))
+    ]
+
     def rows_final():
         ng_copy.wait_recv()
         grad = own_grad + ngr[...].astype(F32)
         mid[...] = mid[...] + norm_back(grad, unit, scale_inv, gain1)
         xg_copy.start()
+
+    def wrap_up():
+        for j in range(nblk):
+            af(2, j).wait_recv()
+            f_out(j, 0).start()
+            if j >= 2:
+                f_out(j - 2, 1).wait()
+            ol[(j % 2) * BLK : (j % 2 + 1) * BLK, :] = fg[t * nblk + j, 1].T
+            f_out(j, 1).start()
+
+        for k in range(1, parts):
+            zb(k, 0).wait_send()
+            zb(k, 1).wait_send()
+        x_copy.wait_send()
+        ng_copy.wait_send()
+
+        for j in range(nblk):
+            for k in range(1, parts):
+                left(f_any(1 if j < EARLY_FAR else 0), fz_s.at[(k - 1) * nblk + j])
+        for r in range(n_all):
+            if r < nblk or (r - nblk) // (parts - 1) >= EARLY_FAR:
+                left(f_any(0), f1_s.at[r])
+
+        def drain_all(r, carry):
+            left(f_any(2), cf_s.at[r])
+            left(f_any(1), f2_s.at[r])
+            return carry
+
+        lax.fori_loop(0, n_all, drain_all, 0)
+
+        def drain_own(j, carry):
+            for stage in range(3):
+                left(f_any(stage), af_s.at[stage, j])
+            return carry
+
+        lax.fori_loop(0, nblk, drain_own, 0)
+        for q in range(parts):
+            for a in range(2):
+                for stage in range(3):
+                    left(a_any(2 - stage, a), ra_s.at[stage, a, q])
+                if q < parts - 1:
+                    left(a_any(0, a), ra_s.at[3, a, q])
 
     vec_stage = 0
     for name, low, high in TAIL:
@@ -1174,19 +1226,13 @@
         elif name == "aa1":
             att_round(1)
         elif name == "aa2":
+            wrap_up()
             att_round(2)
+            halves[0].start()
         elif name == "ng":
             rows_final()
         else:
             repeat(name, low, high)
-
-    for j in range(nblk):
-        af(2, j).wait_recv()
-        f_out(j, 0).start()
-        if j >= 2:
-            f_out(j - 2, 1).wait()
-        ol[(j % 2) * BLK : (j % 2 + 1) * BLK, :] = fg[t * nblk + j, 1].T
-        f_out(j, 1).start()
 
     for which in range(2):
         rz = e_rz if which == 0 else l_rz
@@ -1204,50 +1250,19 @@
     for j in range(nblk):
         osm_ref[16 + j : 17 + j, :] = early[pl.ds(4 + t * nblk + j, 1), :]
 
+    for a in range(2):
+        aa(2, a).wait_recv()
+    halves[1].start()
     for k in range(1, parts):
-        zb(k, 0).wait_send()
-        zb(k, 1).wait_send()
         for which in range(2):
             vec_far(which, k).wait_send()
-    x_copy.wait_send()
-    ng_copy.wait_send()
-
-    for j in range(nblk):
-        for k in range(1, parts):
-            left(f_any(1 if j < EARLY_FAR else 0), fz_s.at[(k - 1) * nblk + j])
-    for r in range(n_all):
-        if r < nblk or (r - nblk) // (parts - 1) >= EARLY_FAR:
-            left(f_any(0), f1_s.at[r])
-
-    def drain_all(r, carry):
-        left(f_any(2), cf_s.at[r])
-        left(f_any(1), f2_s.at[r])
-        return carry
-
-    lax.fori_loop(0, n_all, drain_all, 0)
-
-    def drain_own(j, carry):
-        for stage in range(3):
-            left(f_any(stage), af_s.at[stage, j])
-        return carry
-
-    lax.fori_loop(0, nblk, drain_own, 0)
     for j in range(nblk):
         f_out(j, 0).wait()
     for j in range(nblk - 2, nblk):
         f_out(j, 1).wait()
 
-    for q in range(parts):
-        for a in range(2):
-            for stage in range(3):
-                left(a_any(2 - stage, a), ra_s.at[stage, a, q])
-            if q < parts - 1:
-                left(a_any(0, a), ra_s.at[3, a, q])
-    for a in range(2):
-        aa(2, a).wait_recv()
-    oa_copy = pltpu.make_async_copy(done, oa_ref, loc_sem.at[nblk + 1])
-    oa_copy.start()
-    oa_copy.wait()
+    halves[0].wait()
+    halves[1].wait()
     xg_copy.wait()
     for stage in range(3):
         for a in range(2):

time: 203 us -> 202 us (level)
  no operation moved by 1% of the time
where the time goes in v6:
time: 202 us; the launch traced here: 200 us
  Pallas kernels  199 us (99%)
    pallas_call x1, Pallas kernels, local(): pl.pallas_call(kernel, out_shape=[jax.ShapeDtypeStruct((share, width), BF...  192 us
    pallas_call x1, Pallas kernels, local(): pl.pallas_call(finish, out_shape=[jax.ShapeDtypeStruct((share, width), BF...  7.1 us

profile of v6, /device:TPU:0, one launch (start us, length us, event | category | flops | bytes accessed | tf_op | source)
XLA Modules:
  0.0 200.2 jit_solution(4931031582035771965)
XLA Ops:
  1.3 191.6 %shard_map.272 = (bf16[512,640]{1,0:T(8,128)(2,1)}, f32[512,640]{1,0:T(8,128)}, bf16[640,1280]{1,0:T(8,128)(2,1)}, bf16[1280,640]{1,0:T(8,128)(2,1)}, bf16[640,6...) custom-call(bf16[512,640]{1,0:T(8,128)(2,1)} %x_ref.1, bf16[512,640]{1,0:T(8,128)(2,1)} %cot_ref.1, ...), custom_call_target="tpu_custom_call" | custom-call | tf_op jit(solution)/shard_map/pallas_call | solution.py:1445
  192.9 7.1 %shard_map.273 = (bf16[512,640]{1,0:T(8,128)(2,1)}, f32[512,640]{1,0:T(8,128)}, f32[640,1280]{1,0:T(8,128)}, f32[1280,640]{1,0:T(8,128)}, f32[480,640]{1,0:T(8,1...) custom-call(bf16[512,640]{1,0:T(8,128)(2,1)} %get-tuple-element.34.l, ...), custom_call_target="tpu_custom_call" | custom-call | tf_op jit(solution)/shard_map/pallas_call | solution.py:1490

commit v7 on v6

--- a/solution.py
+++ b/solution.py
@@ -52,10 +52,10 @@
     ),
     "r": (
         ("g1", (10, 11, 15, 15, 15, 15, 15, 15, 15, 15, 15, 15, 15, 15, 15, 15, 15, 15, 15, 15, 15)),
-        ("g2", (0, 0, 3, 3, 5, 8, 8, 9, 9, 11, 13, 15, 15, 15, 15, 15, 15, 15, 15, 15, 15)),
-        ("rf", (0, 0, 0, 0, 0, 0, 0, 0, 0, 0, 0, 0, 0, 0, 0, 0, 0, 4, 4, 5, 5)),
-        ("r1", (0, 0, 0, 0, 0, 0, 0, 0, 0, 0, 0, 0, 0, 2, 2, 3, 4, 4, 5, 5, 7)),
-        ("r2", (0, 0, 0, 0, 0, 0, 0, 1, 2, 3, 4, 5, 6, 7, 8, 8, 10, 11, 12, 13, 14)),
+        ("g2", (0, 0, 3, 3, 5, 8, 9, 9, 9, 11, 13, 15, 15, 15, 15, 15, 15, 15, 15, 15, 15)),
+        ("rf", (0, 0, 0, 0, 0, 0, 0, 0, 0, 0, 0, 0, 0, 0, 0, 2, 2, 4, 4, 5, 5)),
+        ("r1", (0, 0, 0, 0, 0, 0, 0, 0, 0, 0, 0, 0, 0, 2, 3, 3, 4, 4, 5, 5, 7)),
+        ("r2", (0, 0, 0, 0, 0, 0, 0, 1, 2, 3, 4, 4, 4, 6, 8, 8, 10, 11, 12, 13, 14)),
     ),
     "ln": (
         ("rf", (5, 7)),

time: 202 us -> 201 us (level)
  no operation moved by 1% of the time
where the time goes in v7:
time: 201 us; the launch traced here: 199 us
  Pallas kernels  198 us (99%)
    pallas_call x1, Pallas kernels, local(): pl.pallas_call(kernel, out_shape=[jax.ShapeDtypeStruct((share, width), BF...  191 us
    pallas_call x1, Pallas kernels, local(): pl.pallas_call(finish, out_shape=[jax.ShapeDtypeStruct((share, width), BF...  7.1 us

profile of v7, /device:TPU:0, one launch (start us, length us, event | category | flops | bytes accessed | tf_op | source)
XLA Modules:
  0.0 199.2 jit_solution(3974212549428273581)
XLA Ops:
  1.3 190.6 %shard_map.272 = (bf16[512,640]{1,0:T(8,128)(2,1)}, f32[512,640]{1,0:T(8,128)}, bf16[640,1280]{1,0:T(8,128)(2,1)}, bf16[1280,640]{1,0:T(8,128)(2,1)}, bf16[640,6...) custom-call(bf16[512,640]{1,0:T(8,128)(2,1)} %x_ref.1, bf16[512,640]{1,0:T(8,128)(2,1)} %cot_ref.1, ...), custom_call_target="tpu_custom_call" | custom-call | tf_op jit(solution)/shard_map/pallas_call | solution.py:1445
  191.9 7.1 %shard_map.273 = (bf16[512,640]{1,0:T(8,128)(2,1)}, f32[512,640]{1,0:T(8,128)}, f32[640,1280]{1,0:T(8,128)}, f32[1280,640]{1,0:T(8,128)}, f32[480,640]{1,0:T(8,1...) custom-call(bf16[512,640]{1,0:T(8,128)(2,1)} %get-tuple-element.34.l, ...), custom_call_target="tpu_custom_call" | custom-call | tf_op jit(solution)/shard_map/pallas_call | solution.py:1490
